TPU v7x, 32 devices: a whole 2x2x4 slice. The times are simulated.
32 devices in a mesh: gx: 4 (over y, x), gy: 8 (over z, core).
Axes of the slice: x: 2, y: 2, z: 4, core: 2. Of those that a mesh axis runs over, the one named last changes fastest.
Arguments:
- displacement: float32 [3, 8, 16, 3, 128], P(None, 'gx', 'gy'), may hold values from -0.15 to 0.15
- velocity: float32 [3, 8, 16, 3, 128], P(None, 'gx', 'gy'), may hold values from -18 to 18
- noise: float32 [4, 3, 8, 16, 3, 128], P(None, None, 'gx', 'gy'), may hold values from -1.7320508 to 1.7320508
- electron_temp: float32 [32, 4, 8], P(('gx', 'gy')), may hold values from 0.5 to 10
- pair_list: int32 [4, 8, 2, 324], P('gx', 'gy'), may hold values from 0 to 26, as said below
- pair_count: int32 [4, 8], P('gx', 'gy'), may hold values from 12 to 324, as said below
Outputs:
- new_displacement: float32 [3, 8, 16, 3, 128], P(None, 'gx', 'gy')
- new_velocity: float32 [3, 8, 16, 3, 128], P(None, 'gx', 'gy')
- electron_final: float32 [32, 4, 8], P(('gx', 'gy'))
Inputs may be any that keep to these rules, and one draw needn't show every extreme that they name: `pair_list`: in each brick the first pair_count entries name distinct (tile, code) pairs, the tile in 0 to 11 and the code in 0 to 26; every tile's code 13 is among them. Later entries are not read. `pair_count`: some brick has exactly 324 live entries and some brick exactly 12.
All inputs are finite; a program needn't handle non-finite values.
Results may differ from a plain program's by a relative error of at most 0.0003.
Values sent between devices are 32-bit elements; how exact they have to be, the bound alone decides.
No kernel may reach another device: no remote copies, remote signals or barrier semaphores. Data moves between devices by JAX's collectives and lax.ppermute only.
A program may use at most 64 MiB of HBM per device.

v0:
```python
from functools import partial

import jax
import jax.numpy as jnp
from jax import lax
from jax.sharding import PartitionSpec as P

CB = 4
TILE = 128
BXT = 2
BYT = 2
TZ = 3
TILES = 12
STEPS = 4
SUB = 6


lattice_edge = 3.1652
density_cut = 4.400224
embed_scale = 1.896373
pair_cut = 3.25
coef_zero = 47.1346499
coef_one = -33.7665655
coef_two = 6.2541999
time_step = 0.005
atom_mass = 0.0190534
friction = 1.0
heat_capacity = 0.02
diffusion_rate = 0.12


def padded_2(block, sides, width):
    for axis, dim in sides:
        count = lax.axis_size(axis)
        forward = [(i, i + 1) for i in range(count - 1)]
        forward.append((count - 1, 0))
        backward = [(target, source) for source, target in forward]
        low = lax.ppermute(
            lax.slice_in_dim(block, block.shape[dim] - width, None, axis=dim), axis, forward
        )
        high = lax.ppermute(lax.slice_in_dim(block, 0, width, axis=dim), axis, backward)
        block = jnp.concatenate([low, block, high], axis=dim)
    return block


def lattice_sites():
    serial = jnp.arange(TILE, dtype=jnp.int32)
    cell_number = serial // 2
    half_step = (serial % 2).astype(jnp.float32) * 0.5
    corners = jnp.stack([cell_number // (CB * CB), cell_number // CB % CB, cell_number % CB])
    return lattice_edge * (corners.astype(jnp.float32) + half_step[None, :])


def plane_table(plane_total):
    serial = jnp.arange(TILE, dtype=jnp.int32)
    cell_number = serial // 2
    layer = 2 * (cell_number % CB) + serial % 2
    tiles = jnp.arange(TZ, dtype=jnp.int32)
    whole = tiles[:, None] * (2 * CB) + layer[None, :]
    return whole * plane_total // (2 * CB * TZ)


def pair_geometry(window, tile_index, neighbour_code, lattice):
    wide_y = BYT + 2
    depth_t = tile_index % TZ
    inner_y = tile_index // TZ % BYT
    inner_x = tile_index // (TZ * BYT)
    shift_x = neighbour_code // 9
    shift_y = neighbour_code // 3 % 3
    shift_z = neighbour_code % 3
    flattened = window.reshape(window.shape[0], (BXT + 2) * wide_y * TZ, TILE)
    own_index = ((inner_x + 1) * wide_y + inner_y + 1) * TZ + depth_t
    other_index = ((inner_x + shift_x) * wide_y + inner_y + shift_y) * TZ + (
        depth_t + shift_z - 1 + TZ
    ) % TZ
    own_tile = lax.dynamic_index_in_dim(flattened, own_index, 1, keepdims=False)
    other_tile = lax.dynamic_index_in_dim(flattened, other_index, 1, keepdims=False)
    offset = jnp.stack([shift_x - 1, shift_y - 1, shift_z - 1]).astype(jnp.float32) * (
        CB * lattice_edge
    )
    left = lattice + own_tile
    right = lattice + other_tile + offset[:, None]
    delta = left[:, :, None] - right[:, None, :]
    square = jnp.sum(delta * delta, axis=0)
    serial = jnp.arange(TILE, dtype=jnp.int32)
    same_atom = (neighbour_code == 13) & (serial[:, None] == serial[None, :])
    distance = jnp.sqrt(jnp.where(same_atom, 100.0, square))
    return (delta, distance, own_index, other_index)


def density_term(window, lattice, tile_index, neighbour_code):
    delta, distance, own_index, other_index = pair_geometry(
        window, tile_index, neighbour_code, lattice
    )
    dens_gap = distance - density_cut
    return jnp.sum(jnp.where(distance < density_cut, dens_gap * dens_gap, 0.0), axis=1)[None]


def force_term(window, embed_window, lattice, tile_index, neighbour_code):
    delta, distance, own_index, other_index = pair_geometry(
        window, tile_index, neighbour_code, lattice
    )
    flat_embed = embed_window.reshape((BXT + 2) * (BYT + 2) * TZ, TILE)
    own_embed = lax.dynamic_index_in_dim(flat_embed, own_index, 0, keepdims=False)
    other_embed = lax.dynamic_index_in_dim(flat_embed, other_index, 0, keepdims=False)
    pair_gap = distance - pair_cut
    poly = coef_zero + coef_one * distance + coef_two * distance * distance
    pair_slope = jnp.where(
        distance < pair_cut,
        2.0 * pair_gap * poly + pair_gap * pair_gap * (coef_one + 2.0 * coef_two * distance),
        0.0,
    )
    dens_gap = distance - density_cut
    dens_slope = jnp.where(distance < density_cut, 2.0 * dens_gap, 0.0)
    scalar = (pair_slope + (own_embed[:, None] + other_embed[None, :]) * dens_slope) / distance
    return -jnp.sum(scalar[None] * delta, axis=2)


def sweep_pairs(term_fn, channels, pair_table, pair_total):
    initial = jnp.zeros((channels, TILES, TILE), jnp.float32)

    def block_add(block_index, running):
        start = block_index * 27
        chosen = lax.dynamic_slice_in_dim(pair_table, start, 27, 1)
        live = start + jnp.arange(27, dtype=jnp.int32) < pair_total
        terms = jax.vmap(term_fn)(chosen[0], chosen[1])
        terms = jnp.where(live[:, None, None], terms, 0.0)
        return running.at[:, chosen[0]].add(jnp.swapaxes(terms, 0, 1))

    blocks = (pair_total + 26) // 27
    total = lax.fori_loop(0, blocks, block_add, initial)
    return total.reshape(channels, BXT, BYT, TZ, TILE)


def relax_slab(padded):
    center = padded[1:-1]
    beside_all = padded[2:] + padded[:-2] + jnp.roll(center, 1, 1) + jnp.roll(center, -1, 1)
    beside_all = beside_all + jnp.roll(center, 1, 2) + jnp.roll(center, -1, 2)
    return center + diffusion_rate * (beside_all - 6.0 * center)


def per_device(displacement, velocity, noise, electron_temp, pair_list, pair_count):
    lattice = lattice_sites()
    pair_table = pair_list[0, 0]
    pair_total = pair_count[0, 0]
    positions = displacement
    speeds = velocity
    across_x = lax.axis_size("gx")
    across_y = lax.axis_size("gy")
    owners = across_x * across_y
    slab_depth = electron_temp.shape[0]
    plane_total = slab_depth * owners
    planes = plane_table(plane_total).reshape(-1)
    heat_field = electron_temp
    for step_index in range(STEPS):
        arrived = lax.all_to_all(
            heat_field.reshape(slab_depth, owners),
            ("gx", "gy"),
            split_axis=1,
            concat_axis=0,
            tiled=True,
        )
        column = arrived.reshape(-1)
        column_temp = jnp.take(column, planes).reshape(TZ, TILE)
        local_temp = jnp.broadcast_to(column_temp, (BXT, BYT, TZ, TILE))
        window = padded_2(positions, (("gx", 1), ("gy", 2)), 1)
        density = sweep_pairs(partial(density_term, window, lattice), 1, pair_table, pair_total)
        embed_slope = -embed_scale / (2.0 * jnp.sqrt(density))
        embed_window = padded_2(embed_slope, (("gx", 1), ("gy", 2)), 1)
        force = sweep_pairs(
            partial(force_term, window, embed_window, lattice), 3, pair_table, pair_total
        )
        kicker = (
            jnp.sqrt(2.0 * friction * atom_mass * local_temp / time_step)[None] * noise[step_index]
        )
        speeds = speeds + time_step / atom_mass * (force - friction * atom_mass * speeds + kicker)
        positions = positions + time_step * speeds
        power = friction * atom_mass * time_step * jnp.sum(speeds * speeds, axis=0)
        tile_power = jnp.sum(power, axis=(0, 1)).reshape(-1)
        energy = jnp.zeros((plane_total,), jnp.float32).at[planes].add(tile_power)
        arrived = lax.all_to_all(
            energy.reshape(plane_total, 1), ("gx", "gy"), split_axis=0, concat_axis=1, tiled=True
        )
        heat_field = heat_field + arrived.reshape(slab_depth, across_x, across_y) / heat_capacity
        for sub_index in range(SUB):
            heat_field = relax_slab(padded_2(heat_field, ((("gx", "gy"), 0),), 1))
    return (positions, speeds, heat_field)


def solution(mesh):
    placed = (
        P(None, "gx", "gy", None, None),
        P(None, "gx", "gy", None, None),
        P(None, None, "gx", "gy", None, None),
        P(("gx", "gy"), None, None),
        P("gx", "gy", None, None),
        P("gx", "gy"),
    )
    return jax.shard_map(
        per_device,
        mesh=mesh,
        in_specs=placed,
        out_specs=(
            P(None, "gx", "gy", None, None),
            P(None, "gx", "gy", None, None),
            P(("gx", "gy"), None, None),
        ),
        check_vma=False,
    )
```

profile of v0, /device:TPU:0, one launch (start us, length us, event | category | flops | bytes accessed | tf_op | source)
XLA Modules:
  0.0 1365.4 jit_solution(15956714869805647130)
XLA Ops:
  2.0 7.3 all-to-all-start
  23.9 26.7 %while.124 = (s32[]{:T(128)}, f32[1,12,128]{2,1,0:T(8,128)S(1)}, s32[]{:T(128)}, s32[2,324]{1,0:T(2,128)}, s32[]{:T(128)}, /*index=5*/f32[3,128]{1,0:T(4,128)S(1...) while((s32[]{:T(128)}, f32[1,12,128]{2,1,0:T(8,128)S(1)}, ...), condition=%wide.region_4.5_spmd, body=%wide.region_0.4_spmd.sunk | while | flops 6690088 | bytes 4029420 | solution.py:131
  51.3 48.2 %collective-permute-start.5 = (f32[1,1,2,3,128]{4,0,3,2,1:T(1,128)S(1)}, f32[1,1,2,3,128]{4,0,3,2,1:T(1,128)S(1)}, u32[]{:S(2)}, u32[]{:S(2)}) collective-permute-start(f32[1,1,2,3,128]{4,0,3,2,1:T(1,128)S(1)} %get-tuple-element.2171), channel_id=1, source_target_pairs={{8,0},{16,8},{24,16},{0,24},{9,1},{17,9},{25,17},{1,25},{10,2},{18... | collective-permute-start | bytes 9224 | tf_op jit(solution)/shard_map/ppermute | solution.py:41
  101.4 20.3 %fusion.345 = (f32[3,128]{1,0:T(4,128)S(1)}, pred[384]{0:T(512)(128)(4,1)S(1)}, pred[384]{0:T(512)(128)(4,1)S(1)}, pred[384]{0:T(512)(128)(4,1)S(1)}, pred[384]{...) fusion(f32[]{:T(128)} %bitcast.156, ...), kind=kLoop, calls=%fused_computation.778 | loop fusion | flops 30720 | bytes 14476 | tf_op jit(solution)/shard_map/sqrt | solution.py:174
  122.4 54.1 %while.128 = (s32[]{:T(128)}, f32[3,12,128]{2,0,1:T(4,128)S(1)}, s32[]{:T(128)}, s32[2,324]{1,0:T(2,128)}, s32[]{:T(128)}, /*index=5*/f32[3,128]{1,0:T(4,128)S(1...) while((s32[]{:T(128)}, f32[3,12,128]{2,0,1:T(4,128)S(1)}, ...), condition=%wide.wide.region_9.10_spmd, body=%wide.wide.region_5.9_spmd.sunk | while | flops 18651360 | bytes 7947439 | solution.py:131
  181.2 117.3 %all-to-all-start.1 = ((f32[32,1,1]{2,1,0:T(1,128)}), f32[32,1,1]{2,1,0:T(1,128)S(1)}, u32[]{:S(2)}, u32[]{:S(2)}) async-start(f32[32,1,1]{2,1,0:T(1,128)} %copy.165), calls=%async_computation.1 | async-start | bytes 32768 | tf_op jit(solution)/shard_map/all_to_all | solution.py:181
  308.0 5.3 collective-permute-done.17
  314.8 5.3 collective-permute-done.19
  321.7 5.3 collective-permute-done.21
  328.5 5.3 collective-permute-done.23
  335.3 5.3 collective-permute-done.25
  342.2 5.3 collective-permute-done.27
  351.0 7.1 all-to-all-done.2
  363.7 26.7 %while.125 = (s32[]{:T(128)}, f32[1,12,128]{2,1,0:T(8,128)S(1)}, s32[]{:T(128)}, s32[2,324]{1,0:T(2,128)}, s32[]{:T(128)}, /*index=5*/f32[3,128]{1,0:T(4,128)S(1...) while((s32[]{:T(128)}, f32[1,12,128]{2,1,0:T(8,128)S(1)}, ...), condition=%wide.region_14.16_spmd, body=%wide.region_10.15_spmd.sunk | while | flops 6690088 | bytes 4029420 | solution.py:131
  391.2 47.3 %collective-permute-start.13 = (f32[1,1,2,3,128]{4,0,3,2,1:T(1,128)S(1)}, f32[1,1,2,3,128]{4,0,3,2,1:T(1,128)S(1)}, u32[]{:S(2)}, u32[]{:S(2)}) collective-permute-start(f32[1,1,2,3,128]{4,0,3,2,1:T(1,128)S(1)} %get-tuple-element.2169), channel_id=1, source_target_pairs={{8,0},{16,8},{24,16},{0,24},{9,1},{17,9},{25,17},{1,25},{10,2},{18... | collective-permute-start | bytes 9224 | tf_op jit(solution)/shard_map/ppermute | solution.py:41
  441.0 20.2 %fusion.343 = f32[3,128]{1,0:T(4,128)S(1)} fusion(pred[384]{0:T(512)(128)(4,1)S(1)} %get-tuple-element.2084, pred[384]{0:T(512)(128)(4,1)S(1)} %get-tuple-element.2083, pred[384]{0:T(512)(128)(4,1)S(1)} %get-tuple-element.2082, pred[384]{0:T(512)(128)(4,1)S(1)} %get-tuple-element.2081, pred[384]{0:T(512)(128)(4,1)S(1)} %get-tuple-element.2080, ...), kind=kLoop, calls=%fused_computation.775 | loop fusion | flops 12672 | bytes 13952 | tf_op jit(solution)/shard_map/sqrt | solution.py:174
  461.9 54.1 %while.129 = (s32[]{:T(128)}, f32[3,12,128]{2,0,1:T(4,128)S(1)}, s32[]{:T(128)}, s32[2,324]{1,0:T(2,128)}, s32[]{:T(128)}, /*index=5*/f32[3,128]{1,0:T(4,128)S(1...) while((s32[]{:T(128)}, f32[3,12,128]{2,0,1:T(4,128)S(1)}, ...), condition=%wide.wide.region_19.21_spmd, body=%wide.wide.region_15.20_spmd.sunk | while | flops 18651360 | bytes 7947439 | solution.py:131
  520.7 116.9 %all-to-all-start.3 = ((f32[32,1,1]{2,1,0:T(1,128)}), f32[32,1,1]{2,1,0:T(1,128)S(1)}, u32[]{:S(2)}, u32[]{:S(2)}) async-start(f32[32,1,1]{2,1,0:T(1,128)} %copy.170), calls=%async_computation.3 | async-start | bytes 32768 | tf_op jit(solution)/shard_map/all_to_all | solution.py:181
  647.1 5.3 collective-permute-done.37
  653.9 5.3 collective-permute-done.39
  660.8 5.3 collective-permute-done.41
  667.6 5.3 collective-permute-done.43
  674.5 5.3 collective-permute-done.45
  681.3 5.3 collective-permute-done.47
  689.9 7.1 all-to-all-done.4
  702.6 26.9 %while.126 = (s32[]{:T(128)}, f32[1,12,128]{2,1,0:T(8,128)S(1)}, s32[]{:T(128)}, s32[2,324]{1,0:T(2,128)}, s32[]{:T(128)}, /*index=5*/f32[3,128]{1,0:T(4,128)S(1...) while((s32[]{:T(128)}, f32[1,12,128]{2,1,0:T(8,128)S(1)}, ...), condition=%wide.region_27.29_spmd, body=%wide.region_23.28_spmd.sunk | while | flops 6690088 | bytes 4029420 | solution.py:131
  730.3 47.3 %collective-permute-start.33 = (f32[1,1,2,3,128]{4,0,3,2,1:T(1,128)S(1)}, f32[1,1,2,3,128]{4,0,3,2,1:T(1,128)S(1)}, u32[]{:S(2)}, u32[]{:S(2)}) collective-permute-start(f32[1,1,2,3,128]{4,0,3,2,1:T(1,128)S(1)} %get-tuple-element.2167), channel_id=1, source_target_pairs={{8,0},{16,8},{24,16},{0,24},{9,1},{17,9},{25,17},{1,25},{10,2},{18... | collective-permute-start | bytes 9224 | tf_op jit(solution)/shard_map/ppermute | solution.py:41
  780.2 20.2 %fusion.341 = f32[3,128]{1,0:T(4,128)S(1)} fusion(pred[384]{0:T(512)(128)(4,1)S(1)} %get-tuple-element.2084, pred[384]{0:T(512)(128)(4,1)S(1)} %get-tuple-element.2083, pred[384]{0:T(512)(128)(4,1)S(1)} %get-tuple-element.2082, pred[384]{0:T(512)(128)(4,1)S(1)} %get-tuple-element.2081, pred[384]{0:T(512)(128)(4,1)S(1)} %get-tuple-element.2080, ...), kind=kLoop, calls=%fused_computation.772 | loop fusion | flops 12672 | bytes 13952 | tf_op jit(solution)/shard_map/sqrt | solution.py:174
  801.1 54.1 %while.130 = (s32[]{:T(128)}, f32[3,12,128]{2,0,1:T(4,128)S(1)}, s32[]{:T(128)}, s32[2,324]{1,0:T(2,128)}, s32[]{:T(128)}, /*index=5*/f32[3,128]{1,0:T(4,128)S(1...) while((s32[]{:T(128)}, f32[3,12,128]{2,0,1:T(4,128)S(1)}, ...), condition=%wide.wide.region_32.34_spmd, body=%wide.wide.region_28.33_spmd.sunk | while | flops 18651360 | bytes 7947439 | solution.py:131
  859.8 116.8 %all-to-all-start.5 = ((f32[32,1,1]{2,1,0:T(1,128)}), f32[32,1,1]{2,1,0:T(1,128)S(1)}, u32[]{:S(2)}, u32[]{:S(2)}) async-start(f32[32,1,1]{2,1,0:T(1,128)} %copy.175), calls=%async_computation.5 | async-start | bytes 32768 | tf_op jit(solution)/shard_map/all_to_all | solution.py:181
  986.2 5.3 collective-permute-done.57
  993.0 5.3 collective-permute-done.59
  999.9 5.3 collective-permute-done.61
  1006.7 5.3 collective-permute-done.63
  1013.5 5.3 collective-permute-done.65
  1020.4 5.3 collective-permute-done.67
  1029.0 7.1 all-to-all-done.6
  1041.7 26.9 %while.127 = (s32[]{:T(128)}, f32[1,12,128]{2,1,0:T(8,128)S(1)}, s32[]{:T(128)}, s32[2,324]{1,0:T(2,128)}, s32[]{:T(128)}, /*index=5*/f32[3,128]{1,0:T(4,128)S(1...) while((s32[]{:T(128)}, f32[1,12,128]{2,1,0:T(8,128)S(1)}, ...), condition=%wide.region_40.42_spmd, body=%wide.region_36.41_spmd.sunk | while | flops 6690088 | bytes 4029420 | solution.py:131
  1069.4 47.3 %collective-permute-start.53 = (f32[1,1,2,3,128]{4,0,3,2,1:T(1,128)S(1)}, f32[1,1,2,3,128]{4,0,3,2,1:T(1,128)S(1)}, u32[]{:S(2)}, u32[]{:S(2)}) collective-permute-start(f32[1,1,2,3,128]{4,0,3,2,1:T(1,128)S(1)} %get-tuple-element.2165), channel_id=1, source_target_pairs={{8,0},{16,8},{24,16},{0,24},{9,1},{17,9},{25,17},{1,25},{10,2},{18... | collective-permute-start | bytes 9224 | tf_op jit(solution)/shard_map/ppermute | solution.py:41
  1119.3 20.2 %fusion.339 = f32[3,128]{1,0:T(4,128)S(1)} fusion(pred[384]{0:T(512)(128)(4,1)S(1)} %get-tuple-element.2084, pred[384]{0:T(512)(128)(4,1)S(1)} %get-tuple-element.2083, pred[384]{0:T(512)(128)(4,1)S(1)} %get-tuple-element.2082, pred[384]{0:T(512)(128)(4,1)S(1)} %get-tuple-element.2081, pred[384]{0:T(512)(128)(4,1)S(1)} %get-tuple-element.2080, ...), kind=kLoop, calls=%fused_computation.769 | loop fusion | flops 12672 | bytes 13952 | tf_op jit(solution)/shard_map/sqrt | solution.py:174
  1140.2 54.1 %while.131 = (s32[]{:T(128)}, f32[3,12,128]{2,0,1:T(4,128)S(1)}, s32[]{:T(128)}, s32[2,324]{1,0:T(2,128)}, s32[]{:T(128)}, /*index=5*/f32[3,128]{1,0:T(4,128)S(1...) while((s32[]{:T(128)}, f32[3,12,128]{2,0,1:T(4,128)S(1)}, ...), condition=%wide.wide.region_45.47_spmd, body=%wide.wide.region_41.46_spmd.sunk | while | flops 18651360 | bytes 7947439 | solution.py:131
  1198.9 116.8 %all-to-all-start.7 = ((f32[32,1,1]{2,1,0:T(1,128)}), f32[32,1,1]{2,1,0:T(1,128)S(1)}, u32[]{:S(2)}, u32[]{:S(2)}) async-start(f32[32,1,1]{2,1,0:T(1,128)} %copy.179), calls=%async_computation.7 | async-start | bytes 32768 | tf_op jit(solution)/shard_map/all_to_all | solution.py:181
  1317.0 5.9 all-to-all-done.7
  1324.8 5.3 collective-permute-done.69
  1331.6 5.3 collective-permute-done.71
  1338.5 5.3 collective-permute-done.73
  1345.3 5.3 collective-permute-done.75
  1352.2 5.3 collective-permute-done.77
  (978 shorter events, 464.5 us)
Async XLA Ops:
  2.0 14.4 %all-to-all-start = ((f32[1,32,1]{2,0,1:T(1,128)}), f32[1,32,1]{2,0,1:T(1,128)S(1)}, u32[]{:S(2)}, u32[]{:S(2)}) async-start(f32[1,32,1]{2,0,1:T(1,128)} %all_to_all.96), calls=%async_computation | async-start | bytes 32768 | tf_op jit(solution)/shard_map/all_to_all | solution.py:156
  10.1 6.7 collective-permute-start
  50.6 49.8 %collective-permute-start.4 = (f32[1,1,2,3,128]{4,0,3,2,1:T(1,128)S(1)}, f32[1,1,2,3,128]{4,0,3,2,1:T(1,128)S(1)}, u32[]{:S(2)}, u32[]{:S(2)}) collective-permute-start(f32[1,1,2,3,128]{4,0,3,2,1:T(1,128)S(1)} %get-tuple-element.2172), channel_id=1, source_target_pairs={{0,8},{8,16},{16,24},{24,0},{1,9},{9,17},{17,25},{25,1},{2,10},{10... | collective-permute-start | bytes 9224 | tf_op jit(solution)/shard_map/ppermute | solution.py:38
  51.3 49.5 %collective-permute-start.5 = (f32[1,1,2,3,128]{4,0,3,2,1:T(1,128)S(1)}, f32[1,1,2,3,128]{4,0,3,2,1:T(1,128)S(1)}, u32[]{:S(2)}, u32[]{:S(2)}) collective-permute-start(f32[1,1,2,3,128]{4,0,3,2,1:T(1,128)S(1)} %get-tuple-element.2171), channel_id=1, source_target_pairs={{8,0},{16,8},{24,16},{0,24},{9,1},{17,9},{25,17},{1,25},{10,2},{18... | collective-permute-start | bytes 9224 | tf_op jit(solution)/shard_map/ppermute | solution.py:41
  100.8 20.8 %collective-permute-start.7 = (f32[1,4,1,3,128]{4,0,3,2,1:T(1,128)S(1)}, f32[1,4,1,3,128]{4,0,3,2,1:T(1,128)S(1)}, u32[]{:S(2)}, u32[]{:S(2)}) collective-permute-start(f32[1,4,1,3,128]{4,0,3,2,1:T(1,128)S(1)} %get-tuple-element.2164), channel_id=1, source_target_pairs={{1,0},{2,1},{3,2},{4,3},{5,4},{6,5},{7,6},{0,7},{9,8},{10,9},{11,1... | collective-permute-start | bytes 18440 | tf_op jit(solution)/shard_map/ppermute | solution.py:41
  101.2 20.5 %collective-permute-start.6 = (f32[1,4,1,3,128]{4,0,3,2,1:T(1,128)S(1)}, f32[1,4,1,3,128]{4,0,3,2,1:T(1,128)S(1)}, u32[]{:S(2)}, u32[]{:S(2)}) collective-permute-start(f32[1,4,1,3,128]{4,0,3,2,1:T(1,128)S(1)} %get-tuple-element.2163), channel_id=1, source_target_pairs={{0,1},{1,2},{2,3},{3,4},{4,5},{5,6},{6,7},{7,0},{8,9},{9,10},{10,1... | collective-permute-start | bytes 18440 | tf_op jit(solution)/shard_map/ppermute | solution.py:38
  181.2 124.4 %all-to-all-start.1 = ((f32[32,1,1]{2,1,0:T(1,128)}), f32[32,1,1]{2,1,0:T(1,128)S(1)}, u32[]{:S(2)}, u32[]{:S(2)}) async-start(f32[32,1,1]{2,1,0:T(1,128)} %copy.165), calls=%async_computation.1 | async-start | bytes 32768 | tf_op jit(solution)/shard_map/all_to_all | solution.py:181
  298.5 60.0 %collective-permute-start.9 = (f32[3,1,2,3,128]{4,0,3,2,1:T(4,128)S(1)}, f32[3,1,2,3,128]{4,0,3,2,1:T(4,128)S(1)}, u32[]{:S(2)}, u32[]{:S(2)}) collective-permute-start(f32[3,1,2,3,128]{4,0,3,2,1:T(4,128)S(1)} %get-tuple-element.2154), channel_id=1, source_target_pairs={{8,0},{16,8},{24,16},{0,24},{9,1},{17,9},{25,17},{1,25},{10,2},{18... | collective-permute-start | bytes 27656 | tf_op jit(solution)/shard_map/ppermute | solution.py:41
  301.2 57.3 %collective-permute-start.8 = (f32[3,1,2,3,128]{4,0,3,2,1:T(4,128)S(1)}, f32[3,1,2,3,128]{4,0,3,2,1:T(4,128)S(1)}, u32[]{:S(2)}, u32[]{:S(2)}) collective-permute-start(f32[3,1,2,3,128]{4,0,3,2,1:T(4,128)S(1)} %get-tuple-element.2153), channel_id=1, source_target_pairs={{0,8},{8,16},{16,24},{24,0},{1,9},{9,17},{17,25},{25,1},{2,10},{10... | collective-permute-start | bytes 27656 | tf_op jit(solution)/shard_map/ppermute | solution.py:38
  313.5 6.6 collective-permute-start.19
  327.2 6.6 collective-permute-start.23
  340.9 6.6 collective-permute-start.27
  348.3 9.9 all-to-all-start.2
  390.4 48.9 %collective-permute-start.12 = (f32[1,1,2,3,128]{4,0,3,2,1:T(1,128)S(1)}, f32[1,1,2,3,128]{4,0,3,2,1:T(1,128)S(1)}, u32[]{:S(2)}, u32[]{:S(2)}) collective-permute-start(f32[1,1,2,3,128]{4,0,3,2,1:T(1,128)S(1)} %get-tuple-element.2170), channel_id=1, source_target_pairs={{0,8},{8,16},{16,24},{24,0},{1,9},{9,17},{17,25},{25,1},{2,10},{10... | collective-permute-start | bytes 9224 | tf_op jit(solution)/shard_map/ppermute | solution.py:38
  391.2 48.6 %collective-permute-start.13 = (f32[1,1,2,3,128]{4,0,3,2,1:T(1,128)S(1)}, f32[1,1,2,3,128]{4,0,3,2,1:T(1,128)S(1)}, u32[]{:S(2)}, u32[]{:S(2)}) collective-permute-start(f32[1,1,2,3,128]{4,0,3,2,1:T(1,128)S(1)} %get-tuple-element.2169), channel_id=1, source_target_pairs={{8,0},{16,8},{24,16},{0,24},{9,1},{17,9},{25,17},{1,25},{10,2},{18... | collective-permute-start | bytes 9224 | tf_op jit(solution)/shard_map/ppermute | solution.py:41
  439.8 21.4 %collective-permute-start.15 = (f32[1,4,1,3,128]{4,0,3,2,1:T(1,128)S(1)}, f32[1,4,1,3,128]{4,0,3,2,1:T(1,128)S(1)}, u32[]{:S(2)}, u32[]{:S(2)}) collective-permute-start(f32[1,4,1,3,128]{4,0,3,2,1:T(1,128)S(1)} %get-tuple-element.2162), channel_id=1, source_target_pairs={{1,0},{2,1},{3,2},{4,3},{5,4},{6,5},{7,6},{0,7},{9,8},{10,9},{11,1... | collective-permute-start | bytes 18440 | tf_op jit(solution)/shard_map/ppermute | solution.py:41
  441.0 20.2 %collective-permute-start.14 = (f32[1,4,1,3,128]{4,0,3,2,1:T(1,128)S(1)}, f32[1,4,1,3,128]{4,0,3,2,1:T(1,128)S(1)}, u32[]{:S(2)}, u32[]{:S(2)}) collective-permute-start(f32[1,4,1,3,128]{4,0,3,2,1:T(1,128)S(1)} %get-tuple-element.2161), channel_id=1, source_target_pairs={{0,1},{1,2},{2,3},{3,4},{4,5},{5,6},{6,7},{7,0},{8,9},{9,10},{10,1... | collective-permute-start | bytes 18440 | tf_op jit(solution)/shard_map/ppermute | solution.py:38
  520.7 124.0 %all-to-all-start.3 = ((f32[32,1,1]{2,1,0:T(1,128)}), f32[32,1,1]{2,1,0:T(1,128)S(1)}, u32[]{:S(2)}, u32[]{:S(2)}) async-start(f32[32,1,1]{2,1,0:T(1,128)} %copy.170), calls=%async_computation.3 | async-start | bytes 32768 | tf_op jit(solution)/shard_map/all_to_all | solution.py:181
  637.6 59.8 %collective-permute-start.29 = (f32[3,1,2,3,128]{4,0,3,2,1:T(4,128)S(1)}, f32[3,1,2,3,128]{4,0,3,2,1:T(4,128)S(1)}, u32[]{:S(2)}, u32[]{:S(2)}) collective-permute-start(f32[3,1,2,3,128]{4,0,3,2,1:T(4,128)S(1)} %get-tuple-element.2152), channel_id=1, source_target_pairs={{8,0},{16,8},{24,16},{0,24},{9,1},{17,9},{25,17},{1,25},{10,2},{18... | collective-permute-start | bytes 27656 | tf_op jit(solution)/shard_map/ppermute | solution.py:41
  640.3 57.1 %collective-permute-start.28 = (f32[3,1,2,3,128]{4,0,3,2,1:T(4,128)S(1)}, f32[3,1,2,3,128]{4,0,3,2,1:T(4,128)S(1)}, u32[]{:S(2)}, u32[]{:S(2)}) collective-permute-start(f32[3,1,2,3,128]{4,0,3,2,1:T(4,128)S(1)} %get-tuple-element.2151), channel_id=1, source_target_pairs={{0,8},{8,16},{16,24},{24,0},{1,9},{9,17},{17,25},{25,1},{2,10},{10... | collective-permute-start | bytes 27656 | tf_op jit(solution)/shard_map/ppermute | solution.py:38
  645.8 6.6 collective-permute-start.37
  652.6 6.6 collective-permute-start.39
  659.5 6.6 collective-permute-start.41
  666.3 6.6 collective-permute-start.43
  673.2 6.6 collective-permute-start.45
  680.0 6.6 collective-permute-start.47
  687.4 9.6 all-to-all-start.4
  729.5 48.9 %collective-permute-start.32 = (f32[1,1,2,3,128]{4,0,3,2,1:T(1,128)S(1)}, f32[1,1,2,3,128]{4,0,3,2,1:T(1,128)S(1)}, u32[]{:S(2)}, u32[]{:S(2)}) collective-permute-start(f32[1,1,2,3,128]{4,0,3,2,1:T(1,128)S(1)} %get-tuple-element.2168), channel_id=1, source_target_pairs={{0,8},{8,16},{16,24},{24,0},{1,9},{9,17},{17,25},{25,1},{2,10},{10... | collective-permute-start | bytes 9224 | tf_op jit(solution)/shard_map/ppermute | solution.py:38
  730.3 48.6 %collective-permute-start.33 = (f32[1,1,2,3,128]{4,0,3,2,1:T(1,128)S(1)}, f32[1,1,2,3,128]{4,0,3,2,1:T(1,128)S(1)}, u32[]{:S(2)}, u32[]{:S(2)}) collective-permute-start(f32[1,1,2,3,128]{4,0,3,2,1:T(1,128)S(1)} %get-tuple-element.2167), channel_id=1, source_target_pairs={{8,0},{16,8},{24,16},{0,24},{9,1},{17,9},{25,17},{1,25},{10,2},{18... | collective-permute-start | bytes 9224 | tf_op jit(solution)/shard_map/ppermute | solution.py:41
  778.9 21.5 %collective-permute-start.35 = (f32[1,4,1,3,128]{4,0,3,2,1:T(1,128)S(1)}, f32[1,4,1,3,128]{4,0,3,2,1:T(1,128)S(1)}, u32[]{:S(2)}, u32[]{:S(2)}) collective-permute-start(f32[1,4,1,3,128]{4,0,3,2,1:T(1,128)S(1)} %get-tuple-element.2160), channel_id=1, source_target_pairs={{1,0},{2,1},{3,2},{4,3},{5,4},{6,5},{7,6},{0,7},{9,8},{10,9},{11,1... | collective-permute-start | bytes 18440 | tf_op jit(solution)/shard_map/ppermute | solution.py:41
  780.2 20.2 %collective-permute-start.34 = (f32[1,4,1,3,128]{4,0,3,2,1:T(1,128)S(1)}, f32[1,4,1,3,128]{4,0,3,2,1:T(1,128)S(1)}, u32[]{:S(2)}, u32[]{:S(2)}) collective-permute-start(f32[1,4,1,3,128]{4,0,3,2,1:T(1,128)S(1)} %get-tuple-element.2159), channel_id=1, source_target_pairs={{0,1},{1,2},{2,3},{3,4},{4,5},{5,6},{6,7},{7,0},{8,9},{9,10},{10,1... | collective-permute-start | bytes 18440 | tf_op jit(solution)/shard_map/ppermute | solution.py:38
  859.8 123.9 %all-to-all-start.5 = ((f32[32,1,1]{2,1,0:T(1,128)}), f32[32,1,1]{2,1,0:T(1,128)S(1)}, u32[]{:S(2)}, u32[]{:S(2)}) async-start(f32[32,1,1]{2,1,0:T(1,128)} %copy.175), calls=%async_computation.5 | async-start | bytes 32768 | tf_op jit(solution)/shard_map/all_to_all | solution.py:181
  976.7 59.8 %collective-permute-start.49 = (f32[3,1,2,3,128]{4,0,3,2,1:T(4,128)S(1)}, f32[3,1,2,3,128]{4,0,3,2,1:T(4,128)S(1)}, u32[]{:S(2)}, u32[]{:S(2)}) collective-permute-start(f32[3,1,2,3,128]{4,0,3,2,1:T(4,128)S(1)} %get-tuple-element.2150), channel_id=1, source_target_pairs={{8,0},{16,8},{24,16},{0,24},{9,1},{17,9},{25,17},{1,25},{10,2},{18... | collective-permute-start | bytes 27656 | tf_op jit(solution)/shard_map/ppermute | solution.py:41
  979.4 57.1 %collective-permute-start.48 = (f32[3,1,2,3,128]{4,0,3,2,1:T(4,128)S(1)}, f32[3,1,2,3,128]{4,0,3,2,1:T(4,128)S(1)}, u32[]{:S(2)}, u32[]{:S(2)}) collective-permute-start(f32[3,1,2,3,128]{4,0,3,2,1:T(4,128)S(1)} %get-tuple-element.2149), channel_id=1, source_target_pairs={{0,8},{8,16},{16,24},{24,0},{1,9},{9,17},{17,25},{25,1},{2,10},{10... | collective-permute-start | bytes 27656 | tf_op jit(solution)/shard_map/ppermute | solution.py:38
  984.9 6.6 collective-permute-start.57
  991.7 6.6 collective-permute-start.59
  998.5 6.6 collective-permute-start.61
  1012.2 6.6 collective-permute-start.65
  1026.5 9.6 all-to-all-start.6
  1068.7 48.9 %collective-permute-start.52 = (f32[1,1,2,3,128]{4,0,3,2,1:T(1,128)S(1)}, f32[1,1,2,3,128]{4,0,3,2,1:T(1,128)S(1)}, u32[]{:S(2)}, u32[]{:S(2)}) collective-permute-start(f32[1,1,2,3,128]{4,0,3,2,1:T(1,128)S(1)} %get-tuple-element.2166), channel_id=1, source_target_pairs={{0,8},{8,16},{16,24},{24,0},{1,9},{9,17},{17,25},{25,1},{2,10},{10... | collective-permute-start | bytes 9224 | tf_op jit(solution)/shard_map/ppermute | solution.py:38
  1069.4 48.6 %collective-permute-start.53 = (f32[1,1,2,3,128]{4,0,3,2,1:T(1,128)S(1)}, f32[1,1,2,3,128]{4,0,3,2,1:T(1,128)S(1)}, u32[]{:S(2)}, u32[]{:S(2)}) collective-permute-start(f32[1,1,2,3,128]{4,0,3,2,1:T(1,128)S(1)} %get-tuple-element.2165), channel_id=1, source_target_pairs={{8,0},{16,8},{24,16},{0,24},{9,1},{17,9},{25,17},{1,25},{10,2},{18... | collective-permute-start | bytes 9224 | tf_op jit(solution)/shard_map/ppermute | solution.py:41
  1118.0 21.5 %collective-permute-start.55 = (f32[1,4,1,3,128]{4,0,3,2,1:T(1,128)S(1)}, f32[1,4,1,3,128]{4,0,3,2,1:T(1,128)S(1)}, u32[]{:S(2)}, u32[]{:S(2)}) collective-permute-start(f32[1,4,1,3,128]{4,0,3,2,1:T(1,128)S(1)} %get-tuple-element.2158), channel_id=1, source_target_pairs={{1,0},{2,1},{3,2},{4,3},{5,4},{6,5},{7,6},{0,7},{9,8},{10,9},{11,1... | collective-permute-start | bytes 18440 | tf_op jit(solution)/shard_map/ppermute | solution.py:41
  1119.3 20.2 %collective-permute-start.54 = (f32[1,4,1,3,128]{4,0,3,2,1:T(1,128)S(1)}, f32[1,4,1,3,128]{4,0,3,2,1:T(1,128)S(1)}, u32[]{:S(2)}, u32[]{:S(2)}) collective-permute-start(f32[1,4,1,3,128]{4,0,3,2,1:T(1,128)S(1)} %get-tuple-element.2157), channel_id=1, source_target_pairs={{0,1},{1,2},{2,3},{3,4},{4,5},{5,6},{6,7},{7,0},{8,9},{9,10},{10,1... | collective-permute-start | bytes 18440 | tf_op jit(solution)/shard_map/ppermute | solution.py:38
  1198.9 124.0 %all-to-all-start.7 = ((f32[32,1,1]{2,1,0:T(1,128)}), f32[32,1,1]{2,1,0:T(1,128)S(1)}, u32[]{:S(2)}, u32[]{:S(2)}) async-start(f32[32,1,1]{2,1,0:T(1,128)} %copy.179), calls=%async_computation.7 | async-start | bytes 32768 | tf_op jit(solution)/shard_map/all_to_all | solution.py:181
  1323.5 6.6 collective-permute-start.69
  1330.3 6.6 collective-permute-start.71
  1337.2 6.6 collective-permute-start.73
  1344.0 6.6 collective-permute-start.75
  (47 other events, 407.1 us)
where the time goes:
time: 1380 us; the launch traced here: 1370 us
  starting transfers between devices  704 us (51%)
  other arithmetic  330 us (24%)
  waiting for transfers between devices  211 us (15%)
  local copies, waits for them, and re-layouts  115 us (8%)
    all_to_all x4, starting transfers between devices, per_device(): lax.all_to_all(energy.reshape(plane_total, 1), ('gx', 'gy'), split_axis=0...  468 us
    ppermute x40, starting transfers between devices, padded_2(): lax.ppermute(lax.slice_in_dim(block, 0, width, axis=dim), axis, backward)  206 us
    ppermute x40, waiting for transfers between devices, padded_2(): lax.ppermute(lax.slice_in_dim(block, block.shape[dim] - width, None, axis...  145 us
    sqrt x4, other arithmetic, per_device(): jnp.sqrt(2.0 * friction * atom_mass * local_temp / time_step)[None]  80.9 us
    reduce_sum x32, other arithmetic, pair_geometry(): square = jnp.sum(delta * delta, axis=0)  55.5 us
    reduce_sum x16, other arithmetic, force_term(): return -jnp.sum(scalar[None] * delta, axis=2)  50.3 us
    scatter-add x32, other arithmetic, block_add(): return running.at[:, chosen[0]].add(jnp.swapaxes(terms, 0, 1))  39.8 us
    div x16, other arithmetic, force_term(): (pair_slope + (own_embed[:, None] + other_embed[None, :]) * dens_slope) /...  36.4 us
  transfers between devices with their start and end apart: 88, of which 72 were waited for; matrix products, arithmetic and copies ran while one was open for 7% of the time, Pallas kernels for 0%

commit v1 on v0

--- a/solution.py
+++ b/solution.py
@@ -3,6 +3,8 @@
 import jax
 import jax.numpy as jnp
 from jax import lax
+from jax.experimental import pallas as pl
+from jax.experimental.pallas import tpu as pltpu
 from jax.sharding import PartitionSpec as P
 
 CB = 4
@@ -139,52 +141,794 @@
     return center + diffusion_rate * (beside_all - 6.0 * center)
 
 
+def one_step(lattice, pair_table, pair_total, planes, owners, across, carry, noise_now):
+    positions, speeds, heat_field = carry
+    slab_depth = heat_field.shape[0]
+    plane_total = slab_depth * owners
+    arrived = lax.all_to_all(
+        heat_field.reshape(slab_depth, owners), ("gx", "gy"), split_axis=1, concat_axis=0, tiled=True
+    )
+    column = arrived.reshape(-1)
+    column_temp = jnp.take(column, planes).reshape(TZ, TILE)
+    local_temp = jnp.broadcast_to(column_temp, (BXT, BYT, TZ, TILE))
+    window = padded_2(positions, (("gx", 1), ("gy", 2)), 1)
+    density = sweep_pairs(partial(density_term, window, lattice), 1, pair_table, pair_total)
+    embed_slope = -embed_scale / (2.0 * jnp.sqrt(density))
+    embed_window = padded_2(embed_slope, (("gx", 1), ("gy", 2)), 1)
+    force = sweep_pairs(partial(force_term, window, embed_window, lattice), 3, pair_table, pair_total)
+    kicker = jnp.sqrt(2.0 * friction * atom_mass * local_temp / time_step)[None] * noise_now
+    speeds = speeds + time_step / atom_mass * (force - friction * atom_mass * speeds + kicker)
+    positions = positions + time_step * speeds
+    power = friction * atom_mass * time_step * jnp.sum(speeds * speeds, axis=0)
+    tile_power = jnp.sum(power, axis=(0, 1)).reshape(-1)
+    energy = jnp.zeros((plane_total,), jnp.float32).at[planes].add(tile_power)
+    arrived = lax.all_to_all(
+        energy.reshape(plane_total, 1), ("gx", "gy"), split_axis=0, concat_axis=1, tiled=True
+    )
+    heat_field = heat_field + arrived.reshape(slab_depth, *across) / heat_capacity
+
+    def relax(sub_index, heat):
+        return relax_slab(padded_2(heat, ((("gx", "gy"), 0),), 1))
+
+    heat_field = lax.fori_loop(0, SUB, relax, heat_field)
+    return (positions, speeds, heat_field)
+
+
+def whole_sweep(displacement, velocity, noise, electron_temp, pair_list, pair_count):
+    across = (lax.axis_size("gx"), lax.axis_size("gy"))
+    owners = across[0] * across[1]
+    planes = plane_table(electron_temp.shape[0] * owners).reshape(-1)
+    step = partial(
+        one_step, lattice_sites(), pair_list[0, 0], pair_count[0, 0], planes, owners, across
+    )
+    return lax.fori_loop(
+        0,
+        STEPS,
+        lambda n, carry: step(carry, lax.dynamic_index_in_dim(noise, n, 0, keepdims=False)),
+        (displacement, velocity, electron_temp),
+    )
+
+
+NEAR_SHELLS = (3, 4, 8)
+FAR_SHELLS = (11, 12)
+NEAR_LIMIT = 0.2900
+FAR_LIMIT = 0.8170
+HALF = 0.5 * lattice_edge
+FAR_AWAY = 1.0e6
+ROWS = 24
+BASE = 4
+WIDTH = 16
+
+
+def site_offsets(shells):
+    span = range(-3, 4)
+    found = []
+    for x in span:
+        for y in span:
+            for z in span:
+                if x % 2 == y % 2 == z % 2 and x * x + y * y + z * z in shells:
+                    found.append((x, y, z))
+    return found
+
+
+def grouped(offsets):
+    table = {}
+    for x, y, z in offsets:
+        table.setdefault((y, z), []).append(x)
+    return sorted(table.items())
+
+
+NEAR = site_offsets(NEAR_SHELLS)
+FAR = site_offsets(FAR_SHELLS)
+MASK_SLOT = {offset: slot for slot, offset in enumerate(NEAR + FAR)}
+MASKS = len(MASK_SLOT)
+
+
+def sign(value):
+    return (value > 0) - (value < 0)
+
+
+def sources(dy, dz):
+    s = sign(dz)
+    if dy % 2 == 0:
+        k = dy // 2
+        out = [(None, 0, dz + 8 * k, 0)]
+        if s:
+            out.append((None, s, dz - 8 * s + 8 * k, 0))
+        return out
+    low = (dy - 1) // 2
+    out = [(0, 0, dz + 8 * low, 0), (1, 0, dz + 8 * (low + 1), 1)]
+    for parity, k in ((0, low), (1, low + 1)):
+        if any(not 0 <= iz + dz < 8 for iz in range(parity, 8, 2)):
+            out.append((parity, s, dz - 8 * s + 8 * k, parity))
+    return out
+
+
+def lane_shifts(groups):
+    return sorted({shift for (dy, dz), _ in groups for _, _, shift, _ in sources(dy, dz)})
+
+
+def lanes_of(shape=(8, 128)):
+    return lax.broadcasted_iota(jnp.int32, shape, len(shape) - 1)
+
+
+def rows_of(shape=(8, 128)):
+    return lax.broadcasted_iota(jnp.int32, shape, len(shape) - 2)
+
+
+def turn(value, amount):
+    amount = (-amount) % 128
+    return value if amount == 0 else pltpu.roll(value, amount, value.ndim - 1)
+
+
+class Chunk:
+    def __init__(self, owners, cells):
+        self.cells = cells
+        self.owners = owners
+        self.narrow = owners <= 32
+        self.rows = WIDTH if self.narrow else WIDTH + 8
+        if self.narrow:
+            self.tail = 8 if cells == 2 else 14
+            self.tail_lane = 96
+        else:
+            self.tail = WIDTH
+            self.tail_lane = 0
+        self.slots = 128 // (8 * cells)
+
+    def row_home(self, plane):
+        if plane == 8:
+            return (9 if False else 4 * self.cells, 0) if self.cells == 3 else (8, 0)
+        return (self.cells * (plane // 2), plane % 2)
+
+
+def to_own(lane, first, second, cx):
+    both = jnp.where(lane < 64, turn(first, 32 * cx - 32), turn(second, 32 * cx - 64))
+    return jnp.where((lane >= 32) & (lane < 96), both, 0.0)
+
+
+def spread(value, lane, chunk):
+    if not chunk.narrow:
+        return value
+    value = jnp.where(lane >= 96, value, 0.0)
+    value = value + pltpu.roll(value, 64, 1)
+    return value + pltpu.roll(value, 32, 1)
+
+
+def place_halo(own, send_ref, chunk, neighbours, tails):
+    w = chunk.cells
+    lane = lanes_of()
+    row16 = rows_of((16, 128))
+    lane16 = lanes_of((16, 128))
+    in_tail = lane16 >= chunk.tail_lane
+    common = jnp.zeros((16, 128), jnp.float32)
+    if chunk.narrow:
+        for extra, value in tails:
+            common = jnp.where(in_tail & (row16 == chunk.tail + extra), value, common)
+        block = common
+    else:
+        block = common
+
+    def fill(index, carry):
+        base = pl.multiple_of(index * chunk.rows, 8)
+        send_ref[pl.ds(base, 16), :] = block
+        if not chunk.narrow:
+            rows8 = rows_of()
+            late = jnp.zeros((8, 128), jnp.float32)
+            for extra, value in tails:
+                late = jnp.where(rows8 == extra, value, late)
+            send_ref[pl.ds(base + 16, 8), :] = late
+        return carry
+
+    lax.fori_loop(0, chunk.owners, fill, 0, unroll=False)
+
+    for sy in (-1, 1):
+        start = 96 - 8 * w if sy == 1 else 32
+        for g in range(2):
+            packed = common[8 * g : 8 * g + 8]
+            for plane in range(g * chunk.slots, min(9, (g + 1) * chunk.slots)):
+                slot = 8 * w * (plane - g * chunk.slots)
+                here = (lane >= slot) & (lane < slot + 8 * w)
+                packed = jnp.where(here, turn(own(plane), start - slot), packed)
+            for sx in (-1, 0, 1):
+                base = pl.multiple_of(neighbours[(sx, sy)] * chunk.rows, 8)
+                send_ref[pl.ds(base + 8 * g, 8), :] = packed
+    for sx in (-1, 1):
+        base = pl.multiple_of(neighbours[(sx, 0)] * chunk.rows, 8)
+        first = 8 - w if sx == 1 else 0
+        for plane in range(9):
+            home, half = chunk.row_home(plane)
+            value = turn(own(plane), 32 if half == 0 else -32)[first : first + w]
+            here = lanes_of((w, 128)) < 64 if half == 0 else lanes_of((w, 128)) >= 64
+            pltpu.store(send_ref.at[pl.ds(base + home, w), :], value, mask=here)
+
+
+def build_window(own, recv_ref, window, chunk, neighbours):
+    w = chunk.cells
+    lane = lanes_of()
+    zero = jnp.zeros((8, 128), jnp.float32)
+    for plane in range(9):
+        at = plane * ROWS
+        window[at : at + 8, :] = zero
+        window[at + 16 : at + 24, :] = zero
+        centre = own(plane)
+        for sy in (-1, 1):
+            g, slot = divmod(plane, chunk.slots)
+            slot *= 8 * w
+            target = 32 - 8 * w if sy == -1 else 96
+            here = (lane >= target) & (lane < target + 8 * w)
+            for sx in (-1, 0, 1):
+                base = pl.multiple_of(neighbours[(sx, sy)] * chunk.rows, 8)
+                piece = turn(recv_ref[pl.ds(base + 8 * g, 8), :], slot - target)
+                if sx == 0:
+                    centre = jnp.where(here, piece, centre)
+                    continue
+                piece = jnp.where(here, piece, 0.0)
+                if sx == -1:
+                    old = window[at : at + 8, :]
+                    window[at : at + 8, :] = jnp.where(here, piece, old)
+                else:
+                    old = window[at + 16 : at + 24, :]
+                    window[at + 16 : at + 24, :] = jnp.where(here, piece, old)
+        window[at + 8 : at + 16, :] = centre
+        home, half = chunk.row_home(plane)
+        here = (lanes_of((w, 128)) >= 32) & (lanes_of((w, 128)) < 96)
+        for sx in (-1, 1):
+            base = pl.multiple_of(neighbours[(sx, 0)] * chunk.rows, 8)
+            piece = turn(recv_ref[pl.ds(base + home, w), :], -32 if half == 0 else 32)
+            row = at + (8 - w if sx == -1 else 16)
+            pltpu.store(window.at[row : row + w, :], piece, mask=here)
+
+
+def shifted_planes(planes, source, rolled, out, groups, shifts, constants):
+    slot_of = {shift: n for n, shift in enumerate(shifts)}
+    size = planes * ROWS
+
+    def roll_all(plane, carry):
+        at = pl.multiple_of(plane * ROWS, 8)
+        value = source[pl.ds(at, ROWS), :]
+        for shift in shifts:
+            rolled[pl.ds(pl.multiple_of(slot_of[shift] * size + at, 8), ROWS), :] = turn(value, shift)
+        return carry
+
+    lax.fori_loop(0, planes, roll_all, 0)
+    count = planes // TZ
+    half_layer = lanes_of((16, 128)) % 8
+    parity = half_layer % 2
+
+    def build(t, carry):
+        for n, ((dy, dz), _) in enumerate(groups):
+            carried = (half_layer + dz >= 8) | (half_layer + dz < 0)
+            for c in range(count):
+                value = None
+                for want, carry_z, shift, down in sources(dy, dz):
+                    tz = t
+                    if carry_z == 1:
+                        tz = jnp.where(t == TZ - 1, 0, t + 1)
+                    elif carry_z == -1:
+                        tz = jnp.where(t == 0, TZ - 1, t - 1)
+                    row = slot_of[shift] * size + (c * TZ + tz) * ROWS
+                    piece = rolled[pl.ds(pl.multiple_of(row, 8) + BASE + down, 16), :]
+                    if value is None:
+                        value = piece
+                        continue
+                    here = None
+                    if want is not None:
+                        here = parity == want
+                    if carry_z:
+                        here = carried if here is None else here & carried
+                    value = jnp.where(here, piece, value)
+                shift_by = constants(c, dy, dz)
+                if shift_by:
+                    value = value + shift_by
+                at = pl.multiple_of(n * size + (c * TZ + t) * ROWS, 8)
+                out[pl.ds(at + BASE, 16), :] = value
+        return carry
+
+    lax.fori_loop(0, TZ, build, 0)
+
+
+def coordinate_shift(c, dy, dz):
+    return (0.0, HALF * dy, HALF * dz)[c]
+
+
+def no_shift(c, dy, dz):
+    return 0.0
+
+
+def row_start(dx):
+    return dx // 2 if dx % 2 == 0 else (dx - 1) // 2
+
+
+def densities(window, moved, masks, slope, groups):
+    size = 9 * ROWS
+
+    def at_t(t, carry):
+        for block in range(2):
+            at = BASE + 8 * block
+            own = [window[pl.ds(pl.multiple_of((c * TZ + t) * ROWS, 8) + at, 8), :] for c in range(3)]
+            total = jnp.zeros((8, 128), jnp.float32)
+            for n, ((dy, dz), dxs) in enumerate(groups):
+                for dx in dxs:
+                    down = row_start(dx)
+                    other = [
+                        moved[pl.ds(pl.multiple_of(n * size + (c * TZ + t) * ROWS, 8) + at + down, 8), :]
+                        for c in range(3)
+                    ]
+                    away = masks(dx, dy, dz, t, 8 * block)
+                    ex = (own[0] - HALF * dx) - other[0]
+                    ey = own[1] - other[1]
+                    ez = own[2] - other[2]
+                    square = ex * ex + ey * ey + (ez * ez + away)
+                    distance = square * lax.rsqrt(square)
+                    gap = jnp.minimum(distance - density_cut, 0.0)
+                    total = total + gap * gap
+            slope[pl.ds(pl.multiple_of(t * ROWS, 8) + at, 8), :] = -embed_scale * lax.rsqrt(total)
+        return carry
+
+    lax.fori_loop(0, TZ, at_t, 0)
+
+
+def forces(t, window, moved, slope, slope_moved, masks, groups):
+    size = 9 * ROWS
+    at = BASE + 4
+    own = [window[pl.ds(pl.multiple_of((c * TZ + t) * ROWS, 8) + at, 8), :] for c in range(3)]
+    own_slope = slope[pl.ds(pl.multiple_of(t * ROWS, 8) + at, 8), :]
+    total = [jnp.zeros((8, 128), jnp.float32) for _ in range(3)]
+    first = 2.0 * (coef_zero + coef_one * pair_cut + coef_two * pair_cut * pair_cut)
+    second = 3.0 * (coef_one + 2.0 * coef_two * pair_cut)
+    third = 4.0 * coef_two
+    for n, ((dy, dz), dxs) in enumerate(groups):
+        for dx in dxs:
+            down = row_start(dx)
+            other = [
+                moved[pl.ds(pl.multiple_of(n * size + (c * TZ + t) * ROWS, 8) + at + down, 8), :]
+                for c in range(3)
+            ]
+            other_slope = slope_moved[
+                pl.ds(pl.multiple_of(n * TZ * ROWS + t * ROWS, 8) + at + down, 8), :
+            ]
+            away = masks(dx, dy, dz, t, 4)
+            ex = (own[0] - HALF * dx) - other[0]
+            ey = own[1] - other[1]
+            ez = own[2] - other[2]
+            square = ex * ex + ey * ey + (ez * ez + away)
+            inverse = lax.rsqrt(square)
+            distance = square * inverse
+            gap = jnp.minimum(distance - density_cut, 0.0)
+            near = jnp.minimum(distance - pair_cut, 0.0)
+            slope_sum = (own_slope + other_slope) * gap
+            slope_sum = slope_sum + near * (first + near * (second + third * near))
+            scalar = slope_sum * inverse
+            total[0] = total[0] - scalar * ex
+            total[1] = total[1] - scalar * ey
+            total[2] = total[2] - scalar * ez
+    return total
+
+
+def diffuse_grid(grid, across):
+    nx, ny = across
+    for _ in range(SUB):
+        columns = []
+        for x in range(nx):
+            heat = grid[x]
+            beside = grid[(x + 1) % nx] + grid[(x - 1) % nx]
+            beside = beside + pltpu.roll(heat, 1, 0) + pltpu.roll(heat, ny - 1, 0)
+            beside = beside + pltpu.roll(heat, 1, 1) + pltpu.roll(heat, 127, 1)
+            columns.append(heat + diffusion_rate * (beside - 6.0 * heat))
+        grid = columns
+    return grid
+
+
+def layer_matrix(t, plane_total, rows_are_layers):
+    rows = rows_of((128, 128))
+    lanes = lanes_of((128, 128))
+    layer, plane = (rows, lanes) if rows_are_layers else (lanes, rows)
+    found = (2 * CB * t + layer % 8) * plane_total // (2 * CB * TZ)
+    if rows_are_layers:
+        plane = plane % plane_total
+    return jnp.where(found == plane, 1.0, 0.0)
+
+
+def exact_dot(a, b):
+    return jnp.dot(a, b, precision=lax.Precision.HIGHEST, preferred_element_type=jnp.float32)
+
+
+def neighbour_ids(across):
+    nx, ny = across
+    bx, by = lax.axis_index("gx"), lax.axis_index("gy")
+    ids = {}
+    for sx in (-1, 0, 1):
+        for sy in (-1, 0, 1):
+            ids[(sx, sy)] = lax.rem(bx + sx + nx, nx) * ny + lax.rem(by + sy + ny, ny)
+    return ids
+
+
+def prepare(across, chunk, disp, vel, noise, heat, pairs, count, send, own_u, own_v, own_noise, live, lists):
+    owners = across[0] * across[1]
+    lane3 = lanes_of((TZ, 128))
+
+    def convert(read, out, first):
+        for c in range(3):
+            for ix in range(BXT):
+                rows = [read(c, ix, iy) for iy in range(BYT)]
+                for cx in range(CB):
+                    start = first + c * TZ * 8 + CB * ix + cx
+                    out[pl.ds(start, TZ, stride=8), :] = to_own(lane3, rows[0], rows[1], cx)
+
+    convert(lambda c, ix, iy: disp[c, ix, iy], own_u, 0)
+    convert(lambda c, ix, iy: vel[c, ix, iy], own_v, 0)
+    for n in range(STEPS):
+        convert(lambda c, ix, iy: noise[n, c, ix, iy], own_noise, n * 72)
+
+    slots = pairs.shape[3]
+    width = lists.shape[1]
+    lists[...] = jnp.full(lists.shape, -1, jnp.int32)
+    lists[0:2, 0:slots] = pairs[0, 0]
+    tile = lists[0:1, :]
+    code = lists[1:2, :]
+    valid = (lanes_of((1, width)) < count[0, 0]) & (tile >= 0)
+    column = jnp.where(tile >= 3, 1, 0) + jnp.where(tile >= 6, 1, 0) + jnp.where(tile >= 9, 1, 0)
+    depth = jnp.where(valid, tile - 3 * column, -1)
+    place = 32 * column + code
+    left = jnp.where(rows_of((8, width)) == depth, 1.0, 0.0)
+    right = jnp.where(rows_of((128, width)) == place, 1.0, 0.0)
+    found = lax.dot_general(
+        left, right, (((1,), (1,)), ((), ())), preferred_element_type=jnp.float32
+    )
+    live[...] = found
+
+    nx, ny = across
+    lane_n = lanes_of((nx, 128))
+    pick = jnp.where(lanes_of((ny, 128)) % ny == rows_of((ny, 128)), 1.0, 0.0)
+    field = exact_dot(heat[0], pick)
+    field = jnp.where(lane_n % owners // ny == rows_of((nx, 128)), field, 0.0)
+    field = jnp.sum(field, axis=0, keepdims=True)
+
+    ids = neighbour_ids(across)
+    place_halo(lambda plane: own_u[8 * plane : 8 * plane + 8, :], send, chunk, ids, [(0, field)])
+    lanes_live = lanes_of((TZ, 128))
+    middle = (lanes_live >= 32) & (lanes_live < 96)
+    for key, ident in ids.items():
+        if key == (0, 0):
+            continue
+        base = pl.multiple_of(ident * chunk.rows, 8)
+        if chunk.narrow:
+            pltpu.store(send.at[pl.ds(base + 10, TZ), :], turn(found[:TZ], -32), mask=middle)
+            pltpu.store(send.at[pl.ds(base + 13, TZ), :], turn(found[:TZ], 32), mask=middle)
+        else:
+            send[pl.ds(base + chunk.tail + 2, TZ), :] = found[:TZ]
+
+
+def make_masks(chunk, across, recv, live, masks_ref, table, spread_ref, cases):
+    ids = neighbour_ids(across)
+    lane3 = lanes_of((TZ, 128))
+    tables = {}
+    for key, ident in ids.items():
+        base = pl.multiple_of(ident * chunk.rows, 8)
+        if key == (0, 0):
+            tables[key] = live[0:TZ, :]
+        elif chunk.narrow:
+            low = turn(recv[pl.ds(base + 10, TZ), :], 32)
+            high = turn(recv[pl.ds(base + 13, TZ), :], -32)
+            tables[key] = jnp.where(lane3 < 64, low, high)
+        else:
+            tables[key] = recv[pl.ds(base + chunk.tail + 2, TZ), :]
+    table[...] = jnp.zeros((128, 128), jnp.float32)
+    lane1 = lanes_of((1, 128))
+    for x in range(4):
+        for y in range(4):
+            value = tables[((-1, 0, 0, 1)[x], (-1, 0, 0, 1)[y])]
+            g = (1, 0, 1, 0)[x] * 2 + (1, 0, 1, 0)[y]
+            row = jnp.zeros((1, 128), jnp.float32)
+            for t in range(TZ):
+                here = (lane1 >= 32 * t) & (lane1 < 32 * t + 32)
+                row = jnp.where(here, turn(value[t : t + 1], 32 * g - 32 * t), row)
+            table[4 * x + y : 4 * x + y + 1, :] = row
+    by_code = jnp.transpose(table[...])
+    big = (128, 128)
+    for x in range(4):
+        pick = jnp.where(rows_of(big) == 4 * x + lanes_of(big) // 32, 1.0, 0.0)
+        alive = jnp.dot(by_code, pick, preferred_element_type=jnp.float32)
+        spread_ref[128 * x : 128 * x + 128, :] = FAR_AWAY * (1.0 - alive)
+
+    lane = lanes_of()
+    half_layer = lane % 8
+    parity = lane % 2
+    cell_y = lane // 8 % 4
+    low_rows = rows_of() < 4
+
+    def crossing(position, step):
+        return (position + step < 0) | (position + step >= 8)
+
+    groups = grouped(NEAR + FAR)
+
+    def at_t(t, carry):
+        for code in range(27):
+            for block in range(2):
+                first, second = [
+                    spread_ref[pl.ds(128 * x + 32 * t + code, 1), :] for x in (2 * block, 2 * block + 1)
+                ]
+                cases[16 * code + 8 * block : 16 * code + 8 * block + 8, :] = jnp.where(
+                    low_rows, jnp.broadcast_to(first, (8, 128)), jnp.broadcast_to(second, (8, 128))
+                )
+
+        def case(ex, ey, ez, block):
+            code = 9 * (ex + 1) + 3 * (ey + 1) + ez + 1
+            return cases[16 * code + 8 * block : 16 * code + 8 * block + 8, :]
+
+        for dz in sorted({key[1] for key, _ in groups}):
+            cross_z = crossing(half_layer, dz)
+            in_z = {}
+
+            def level_z(ex, ey, block):
+                if (ex, ey, block) not in in_z:
+                    value = case(ex, ey, 0, block)
+                    if dz:
+                        value = jnp.where(cross_z, case(ex, ey, sign(dz), block), value)
+                    in_z[(ex, ey, block)] = value
+                return in_z[(ex, ey, block)]
+
+            for (dy, other_z), dxs in groups:
+                if other_z != dz:
+                    continue
+                cross_y = crossing(2 * cell_y + parity, dy)
+                in_y = {}
+
+                def level_y(ex, block):
+                    if (ex, block) not in in_y:
+                        value = level_z(ex, 0, block)
+                        if dy:
+                            value = jnp.where(cross_y, level_z(ex, sign(dy), block), value)
+                        in_y[(ex, block)] = value
+                    return in_y[(ex, block)]
+
+                for dx in dxs:
+                    cross_x = crossing(2 * (rows_of() % 4) + parity, dx)
+                    for block in range(2):
+                        value = level_y(0, block)
+                        if dx:
+                            value = jnp.where(cross_x, level_y(sign(dx), block), value)
+                        at = (MASK_SLOT[(dx, dy, dz)] * TZ + t) * 16 + 8 * block
+                        masks_ref[pl.ds(pl.multiple_of(at, 8), 8), :] = value
+        return carry
+
+    lax.fori_loop(0, TZ, at_t, 0)
+
+
+def step_kernel(
+    step,
+    across,
+    arriving,
+    leaving,
+    groups,
+    limit,
+    recv,
+    in_u,
+    in_v,
+    in_noise,
+    *rest,
+):
+    nx, ny = across
+    owners = nx * ny
+    plane_total = owners
+    rest = list(rest)
+    if step == 0:
+        live = rest.pop(0)
+    else:
+        masks_ref = rest.pop(0)
+        in_grid = rest.pop(0)
+        in_bad = rest.pop(0)
+    send, out_u, out_v = rest[:3]
+    rest = rest[3:]
+    out_grid = rest.pop(0)
+    out_bad = rest.pop(0)
+    if step == 0:
+        masks_ref = rest.pop(0)
+    window, rolled, moved, slope, slope_moved = rest[:5]
+    extra = rest[5:]
+    ids = neighbour_ids(across)
+    lane = lanes_of()
+    lane1 = lanes_of((1, 128))
+
+    tail = recv[pl.ds(arriving.tail, owners, stride=arriving.rows), :]
+    tail = spread(tail, lanes_of((owners, 128)), arriving)
+    if step == 0:
+        table = extra[0]
+        table[...] = jnp.zeros((128, 128), jnp.float32)
+        table[0:owners, :] = tail
+        turned = jnp.transpose(table[...])[:owners]
+        reach = 128
+        while reach > owners:
+            reach //= 2
+            turned = turned + pltpu.roll(turned, reach, 1)
+        grid = [turned[ny * x : ny * x + ny] for x in range(nx)]
+        out_bad[...] = jnp.zeros((8, 128), jnp.float32)
+        make_masks(arriving, across, recv, live, masks_ref, *extra)
+    else:
+        grid = [
+            in_grid[ny * x : ny * x + ny, :] + tail[ny * x : ny * x + ny] * (1.0 / heat_capacity)
+            for x in range(nx)
+        ]
+        grid = diffuse_grid(grid, across)
+        furthest = recv[pl.ds(arriving.tail + 1, owners, stride=arriving.rows), :]
+        furthest = jnp.where(lanes_of((owners, 128)) >= arriving.tail_lane, furthest, 0.0)
+        reached = jnp.max(furthest, axis=0, keepdims=True)
+        reached = jnp.max(reached, axis=1, keepdims=True)
+        over = jnp.broadcast_to(jnp.where(reached > limit, 1.0, 0.0), (8, 128))
+        out_bad[...] = jnp.maximum(in_bad[...], over)
+    for x in range(nx):
+        out_grid[ny * x : ny * x + ny, :] = grid[x]
+    column = out_grid[pl.ds(ids[(0, 0)], 1), :]
+    column = jnp.broadcast_to(jnp.where(lane1 < plane_total, column, 0.0), (8, 128))
+
+    def masks(dx, dy, dz, t, row):
+        at = (MASK_SLOT[(dx, dy, dz)] * TZ + t) * 16
+        return masks_ref[pl.ds(pl.multiple_of(at, 8) + row, 8), :]
+
+    def own_u(plane):
+        return in_u[8 * plane : 8 * plane + 8, :]
+
+    build_window(own_u, recv, window, arriving, ids)
+    shifts = lane_shifts(groups)
+    shifted_planes(9, window, rolled, moved, groups, shifts, coordinate_shift)
+    densities(window, moved, masks, slope, groups)
+    shifted_planes(3, slope, rolled, slope_moved, groups, shifts, no_shift)
+
+    active = (lane >= 32) & (lane < 96)
+    power = []
+    furthest = jnp.zeros((8, 128), jnp.float32)
+    for t in range(TZ):
+        local = exact_dot(column, layer_matrix(t, plane_total, False))[0:1]
+        kick = jnp.sqrt(local * (2.0 * friction * atom_mass / time_step))
+        force = forces(t, window, moved, slope, slope_moved, masks, groups)
+        layer = jnp.zeros((8, 128), jnp.float32)
+        for c in range(3):
+            at = 8 * (c * TZ + t)
+            speed = in_v[at : at + 8, :]
+            push = force[c] - friction * atom_mass * speed + kick * in_noise[72 * step + at : 72 * step + at + 8, :]
+            speed = speed + time_step / atom_mass * push
+            speed = jnp.where(active, speed, 0.0)
+            place = own_u(c * TZ + t) + time_step * speed
+            out_v[at : at + 8, :] = speed
+            out_u[at : at + 8, :] = place
+            layer = layer + speed * speed
+            furthest = jnp.maximum(furthest, jnp.abs(place))
+        power.append(jnp.sum(layer, axis=0, keepdims=True))
+    energy = jnp.zeros((8, 128), jnp.float32)
+    for t in range(TZ):
+        energy = energy + exact_dot(
+            jnp.broadcast_to(power[t], (8, 128)), layer_matrix(t, plane_total, True)
+        )
+    energy = energy[0:1] * (friction * atom_mass * time_step)
+    if leaving is None:
+        send[...] = jnp.broadcast_to(energy, (owners, 128))
+        return
+    furthest = jnp.max(furthest, axis=0, keepdims=True)
+    furthest = jnp.broadcast_to(jnp.max(furthest, axis=1, keepdims=True), (1, 128))
+    place_halo(
+        lambda plane: out_u[8 * plane : 8 * plane + 8, :],
+        send,
+        leaving,
+        ids,
+        [(0, energy), (1, furthest)],
+    )
+
+
+def finish(across, recv, in_grid, in_u, in_v, heat, new_u, new_v):
+    nx, ny = across
+    owners = nx * ny
+    grid = [
+        in_grid[ny * x : ny * x + ny, :] + recv[ny * x : ny * x + ny, :] * (1.0 / heat_capacity)
+        for x in range(nx)
+    ]
+    grid = diffuse_grid(grid, across)
+    me = lax.axis_index("gx") * ny + lax.axis_index("gy")
+    flat = rows_of((ny, 128)) == lanes_of((ny, 128))
+    for x in range(nx):
+        mine = jnp.where(lanes_of((ny, 128)) == me, grid[x], 0.0)
+        mine = jnp.broadcast_to(jnp.sum(mine, axis=1, keepdims=True), (ny, 128))
+        row = jnp.sum(jnp.where(flat, mine, 0.0), axis=0, keepdims=True)
+        heat[x : x + 1, :] = row
+    lane3 = lanes_of((TZ, 128))
+    for source, out in ((in_u, new_u), (in_v, new_v)):
+        for c in range(3):
+            for ix in range(BXT):
+                rows = [source[pl.ds(c * TZ * 8 + CB * ix + cx, TZ, stride=8), :] for cx in range(CB)]
+                for iy in range(BYT):
+                    value = None
+                    for cx in range(CB):
+                        piece = turn(rows[cx], 32 + 32 * iy - 32 * cx)
+                        value = piece if value is None else jnp.where(lane3 >= 32 * cx, piece, value)
+                    out[c, ix, iy] = value
+
+
+def exchange(value):
+    return lax.all_to_all(value, ("gx", "gy"), split_axis=0, concat_axis=0, tiled=True)
+
+
+VMEM_BYTES = 24 * 1024 * 1024
+
+
+def call(kernel, outs, scratch, operands, smem=(), name=None):
+    specs = [
+        pl.BlockSpec(memory_space=pltpu.SMEM if n in smem else pltpu.VMEM)
+        for n in range(len(operands))
+    ]
+    return pl.pallas_call(
+        kernel,
+        out_shape=[jax.ShapeDtypeStruct(shape, jnp.float32) for shape in outs],
+        in_specs=specs,
+        out_specs=[pl.BlockSpec(memory_space=pltpu.VMEM)] * len(outs),
+        scratch_shapes=scratch,
+        compiler_params=pltpu.CompilerParams(vmem_limit_bytes=VMEM_BYTES),
+        name=name,
+    )(*operands)
+
+
+def stencil_steps(displacement, velocity, noise, electron_temp, pair_list, pair_count):
+    across = (lax.axis_size("gx"), lax.axis_size("gy"))
+    owners = across[0] * across[1]
+    f32 = jnp.float32
+    slots = pair_list.shape[-1]
+    two, three = Chunk(owners, 2), Chunk(owners, 3)
+    send, own_u, own_v, own_noise, live = call(
+        partial(prepare, across, two),
+        [(owners * two.rows, 128), (72, 128), (72, 128), (72 * STEPS, 128), (8, 128)],
+        [pltpu.VMEM((8, (slots + 127) // 128 * 128), jnp.int32)],
+        (displacement, velocity, noise, electron_temp, pair_list, pair_count),
+        smem=(5,),
+        name="prepare",
+    )
+    near, far = grouped(NEAR), grouped(NEAR + FAR)
+    grid_shape = (owners, 128)
+    plan = [(two, two, near, 1.0), (two, three, near, NEAR_LIMIT), (three, three, far, FAR_LIMIT), (three, None, far, FAR_LIMIT)]
+    masks = grid = bad = None
+    for step, (arriving, leaving, groups, limit) in enumerate(plan):
+        recv = exchange(send)
+        send_shape = (owners, 128) if leaving is None else (owners * leaving.rows, 128)
+        outs = [send_shape, (72, 128), (72, 128), grid_shape, (8, 128)]
+        scratch = [
+            pltpu.VMEM((9 * ROWS, 128), f32),
+            pltpu.VMEM((len(lane_shifts(groups)) * 9 * ROWS, 128), f32),
+            pltpu.VMEM((len(groups) * 9 * ROWS, 128), f32),
+            pltpu.VMEM((3 * ROWS, 128), f32),
+            pltpu.VMEM((len(groups) * 3 * ROWS, 128), f32),
+        ]
+        if step == 0:
+            outs.append((MASKS * TZ * 16, 128))
+            scratch += [
+                pltpu.VMEM((128, 128), f32),
+                pltpu.VMEM((512, 128), f32),
+                pltpu.VMEM((27 * 16, 128), f32),
+            ]
+            operands = (recv, own_u, own_v, own_noise, live)
+        else:
+            operands = (recv, own_u, own_v, own_noise, masks, grid, bad)
+        got = call(
+            partial(step_kernel, step, across, arriving, leaving, groups, limit),
+            outs,
+            scratch,
+            operands,
+            name=f"step{step}",
+        )
+        send, own_u, own_v, grid, bad = got[:5]
+        if step == 0:
+            masks = got[5]
+    recv = exchange(send)
+    heat, new_u, new_v = call(
+        partial(finish, across),
+        [(across[0], 128), displacement.shape, velocity.shape],
+        [],
+        (recv, grid, own_u, own_v),
+        name="finish",
+    )
+    return bad[0, 0], new_u, new_v, heat[:, : across[1]].reshape(electron_temp.shape)
+
+
 def per_device(displacement, velocity, noise, electron_temp, pair_list, pair_count):
-    lattice = lattice_sites()
-    pair_table = pair_list[0, 0]
-    pair_total = pair_count[0, 0]
-    positions = displacement
-    speeds = velocity
-    across_x = lax.axis_size("gx")
-    across_y = lax.axis_size("gy")
-    owners = across_x * across_y
-    slab_depth = electron_temp.shape[0]
-    plane_total = slab_depth * owners
-    planes = plane_table(plane_total).reshape(-1)
-    heat_field = electron_temp
-    for step_index in range(STEPS):
-        arrived = lax.all_to_all(
-            heat_field.reshape(slab_depth, owners),
-            ("gx", "gy"),
-            split_axis=1,
-            concat_axis=0,
-            tiled=True,
-        )
-        column = arrived.reshape(-1)
-        column_temp = jnp.take(column, planes).reshape(TZ, TILE)
-        local_temp = jnp.broadcast_to(column_temp, (BXT, BYT, TZ, TILE))
-        window = padded_2(positions, (("gx", 1), ("gy", 2)), 1)
-        density = sweep_pairs(partial(density_term, window, lattice), 1, pair_table, pair_total)
-        embed_slope = -embed_scale / (2.0 * jnp.sqrt(density))
-        embed_window = padded_2(embed_slope, (("gx", 1), ("gy", 2)), 1)
-        force = sweep_pairs(
-            partial(force_term, window, embed_window, lattice), 3, pair_table, pair_total
-        )
-        kicker = (
-            jnp.sqrt(2.0 * friction * atom_mass * local_temp / time_step)[None] * noise[step_index]
-        )
-        speeds = speeds + time_step / atom_mass * (force - friction * atom_mass * speeds + kicker)
-        positions = positions + time_step * speeds
-        power = friction * atom_mass * time_step * jnp.sum(speeds * speeds, axis=0)
-        tile_power = jnp.sum(power, axis=(0, 1)).reshape(-1)
-        energy = jnp.zeros((plane_total,), jnp.float32).at[planes].add(tile_power)
-        arrived = lax.all_to_all(
-            energy.reshape(plane_total, 1), ("gx", "gy"), split_axis=0, concat_axis=1, tiled=True
-        )
-        heat_field = heat_field + arrived.reshape(slab_depth, across_x, across_y) / heat_capacity
-        for sub_index in range(SUB):
-            heat_field = relax_slab(padded_2(heat_field, ((("gx", "gy"), 0),), 1))
-    return (positions, speeds, heat_field)
+    given = (displacement, velocity, noise, electron_temp, pair_list, pair_count)
+    bad, new_u, new_v, heat = stencil_steps(*given)
+    return lax.cond(bad > 0.5, lambda: whole_sweep(*given), lambda: (new_u, new_v, heat))
 
 
 def solution(mesh):

time: 1380 us -> 91.4 us (0.07); the launches traced: 1370 us -> 90.9 us
  starting transfers between devices: 704 us -> 2.87 us
  other arithmetic: 330 us -> 0 us
  waiting for transfers between devices: 211 us -> 5.93 us
  local copies, waits for them, and re-layouts: 115 us -> 4.22 us
  blocking collectives: 0 us -> 55.2 us
  Pallas kernels: 0 us -> 20.4 us
    all_to_all x8 -> x1, starting transfers between devices: 483 us -> 2.87 us  [exchange(): lax.all_to_all(value, ('gx', 'gy'), split_axis=0, concat_axis=0, tiled=True)]
    ppermute x80 -> x0, starting transfers between devices: 221 us -> none  [the longest x40 206 us: padded_2(): lax.ppermute(lax.slice_in_dim(block, 0, width, axis=dim), axis, backward)]
    ppermute x80 -> x0, waiting for transfers between devices: 169 us -> none  [the longest x40 145 us: padded_2(): lax.ppermute(lax.slice_in_dim(block, block.shape[dim] - width, None, axis...]
    reduce_sum x72 -> x0, other arithmetic: 122 us -> none  [the longest x32 55.5 us: pair_geometry(): square = jnp.sum(delta * delta, axis=0)]
    sqrt x4 -> x0, other arithmetic: 80.9 us -> none  [per_device(): jnp.sqrt(2.0 * friction * atom_mass * local_temp / time_step)[None]]
    gather x104 -> x0, local copies, waits for them, and re-layouts: 70.7 us -> none  [the longest x32 21.6 us: pair_geometry(): own_tile = lax.dynamic_index_in_dim(flattened, own_index, 1, keepdims=False)]
    scatter-add x36 -> x0, other arithmetic: 55.3 us -> none  [the longest x32 39.8 us: block_add(): return running.at[:, chosen[0]].add(jnp.swapaxes(terms, 0, 1))]
    all_to_all x0 -> x4, blocking collectives: none -> 55.2 us  [exchange(): lax.all_to_all(value, ('gx', 'gy'), split_axis=0, concat_axis=0, tiled=True)]
  transfers between devices with their start and end apart: 88 -> 1, of which waited for: 72 -> 1; matrix products, arithmetic and copies ran while one was open for 7% -> 1% of each run, Pallas kernels for 0% -> 0%
where the time goes in v1:
time: 91.4 us; the launch traced here: 90.9 us
  blocking collectives  55.2 us (60%)
  Pallas kernels  20.4 us (22%)
  waiting for transfers between devices  5.93 us (6%)
  local copies, waits for them, and re-layouts  4.22 us (5%)
  starting transfers between devices  2.87 us (3%)
  between operations  2.05 us (2%)
    all_to_all x4, blocking collectives, exchange(): lax.all_to_all(value, ('gx', 'gy'), split_axis=0, concat_axis=0, tiled=True)  55.2 us
    pallas_call x6, Pallas kernels, call(): pl.pallas_call(kernel, out_shape=[jax.ShapeDtypeStruct(shape, jnp.float32...  20.4 us
    all_to_all x1, waiting for transfers between devices, exchange(): lax.all_to_all(value, ('gx', 'gy'), split_axis=0, concat_axis=0, tiled=True)  5.93 us
    unnamed x16, local copies, waits for them, and re-layouts  3.68 us
    all_to_all x1, starting transfers between devices, exchange(): lax.all_to_all(value, ('gx', 'gy'), split_axis=0, concat_axis=0, tiled=True)  2.87 us
  transfers between devices with their start and end apart: 1, of which 1 were waited for; matrix products, arithmetic and copies ran while one was open for 1% of the time, Pallas kernels for 0%

profile of v1, /device:TPU:0, one launch (start us, length us, event | category | flops | bytes accessed | tf_op | source)
XLA Modules:
  0.0 90.9 jit_solution(1368199568868132250)
XLA Ops:
  0.6 0.7 copy.173.heat
  1.3 0.9 %copy.92.noise = f32[4,3,2,2,3,128]{5,4,3,2,1,0:T(4,128)S(1)} copy(f32[4,3,2,2,3,128]{5,3,4,2,1,0:T(2,128)} %param.18) | data formatting | bytes 147456 | tf_op args[2]
  2.2 0.7 copy.90.disp
  3.0 0.7 copy.91.vel
  4.3 1.3 %prepare.1 = (f32[512,128]{1,0:T(8,128)S(1)}, f32[72,128]{1,0:T(8,128)S(1)}, f32[72,128]{1,0:T(8,128)S(1)}, f32[288,128]{1,0:T(8,128)S(1)}, f32[8,128]{1,0:T(8,128)S(1)}) custom-call(f32[3,2,2,3,128]{4,3,2,1,0:T(4,128)S(1)} %copy.90.disp, f32[3,2,2,3,128]{4,3,2,1,0:T(4,128)S(1)} %copy.91.vel, f32[4,3,2,2,3,128]{5,4,3,2,1,0:T(4,128)S(1)} %copy.92.noise, ...), custom_call_target="tpu_custom_call" | custom-call | tf_op jit(solution)/shard_map/prepare/pallas_call | solution.py:857
  5.6 17.1 %all_to_all.126 = f32[32,16,128]{2,1,0:T(8,128)S(1)} all-to-all(f32[32,16,128]{2,1,0:T(8,128)S(1)} %bitcast.396), channel_id=1, replica_groups=mesh['gx'=4,'gy'=8] {'gx','gy'}, dimensions={0} | all-to-all | bytes 524288 | tf_op jit(solution)/shard_map/all_to_all | solution.py:846
  22.8 4.0 %step0.1 = (f32[512,128]{1,0:T(8,128)S(1)}, f32[72,128]{1,0:T(8,128)S(1)}, f32[72,128]{1,0:T(8,128)S(1)}, f32[32,128]{1,0:T(8,128)S(1)}, f32[8,128]{1,0:T(8,128)S(1)}, /*index=5*/f32[2784,128]{1,0:T(8,128)S(1)}) custom-call(f32[512,128]{1,0:T(8,128)S(1)} %bitcast.389, f32[72,128]{1,0:T(8,128)S(1)} %get-tuple-element.1000.in_u, ...), custom_call_target="tpu_custom_call" | custom-call | tf_op jit(solution)/shard_map/step0/pallas_call | solution.py:857
  26.8 12.7 %all_to_all.127 = f32[32,16,128]{2,1,0:T(8,128)S(1)} all-to-all(f32[32,16,128]{2,1,0:T(8,128)S(1)} %bitcast.393), channel_id=1, replica_groups=mesh['gx'=4,'gy'=8] {'gx','gy'}, dimensions={0} | all-to-all | bytes 524288 | tf_op jit(solution)/shard_map/all_to_all | solution.py:846
  39.4 3.8 %step1.1 = (f32[512,128]{1,0:T(8,128)S(1)}, f32[72,128]{1,0:T(8,128)S(1)}, f32[72,128]{1,0:T(8,128)S(1)}, f32[32,128]{1,0:T(8,128)S(1)}, f32[8,128]{1,0:T(8,128)S(1)}) custom-call(f32[512,128]{1,0:T(8,128)S(1)} %bitcast.391, f32[72,128]{1,0:T(8,128)S(1)} %get-tuple-element.1005.in_u, f32[72,128]{1,0:T(8,128)S(1)} %get-tuple-element.1006.in_v, ...), custom_call_target="tpu_custom_call" | custom-call | tf_op jit(solution)/shard_map/step1/pallas_call | solution.py:857
  43.3 12.7 %all_to_all.128 = f32[32,16,128]{2,1,0:T(8,128)S(1)} all-to-all(f32[32,16,128]{2,1,0:T(8,128)S(1)} %bitcast.394), channel_id=1, replica_groups=mesh['gx'=4,'gy'=8] {'gx','gy'}, dimensions={0} | all-to-all | bytes 524288 | tf_op jit(solution)/shard_map/all_to_all | solution.py:846
  55.9 5.2 %step2.1 = (f32[512,128]{1,0:T(8,128)S(1)}, f32[72,128]{1,0:T(8,128)S(1)}, f32[72,128]{1,0:T(8,128)S(1)}, f32[32,128]{1,0:T(8,128)S(1)}, f32[8,128]{1,0:T(8,128)S(1)}) custom-call(f32[512,128]{1,0:T(8,128)S(1)} %bitcast.392, f32[72,128]{1,0:T(8,128)S(1)} %get-tuple-element.1011.in_u, f32[72,128]{1,0:T(8,128)S(1)} %get-tuple-element.1012.in_v, ...), custom_call_target="tpu_custom_call" | custom-call | tf_op jit(solution)/shard_map/step2/pallas_call | solution.py:857
  61.2 0.0 copy-start.2
  61.2 0.0 copy-start.3
  61.2 0.0 copy-start.4
  61.2 12.7 %all_to_all.129 = f32[32,16,128]{2,1,0:T(8,128)S(1)} all-to-all(f32[32,16,128]{2,1,0:T(8,128)S(1)} %bitcast.395), channel_id=1, replica_groups=mesh['gx'=4,'gy'=8] {'gx','gy'}, dimensions={0} | all-to-all | bytes 524288 | tf_op jit(solution)/shard_map/all_to_all | solution.py:846
  73.9 5.6 %step3.1 = (f32[32,128]{1,0:T(8,128)}, f32[72,128]{1,0:T(8,128)S(1)}, f32[72,128]{1,0:T(8,128)S(1)}, f32[32,128]{1,0:T(8,128)S(1)}, f32[8,128]{1,0:T(8,128)S(1)}) custom-call(f32[512,128]{1,0:T(8,128)S(1)} %bitcast.390, f32[72,128]{1,0:T(8,128)S(1)} %get-tuple-element.1016.in_u, f32[72,128]{1,0:T(8,128)S(1)} %get-tuple-element.1017.in_v, ...), custom_call_target="tpu_custom_call" | custom-call | tf_op jit(solution)/shard_map/step3/pallas_call | solution.py:857
  79.5 2.9 %all-to-all-start.6 = ((f32[32,1,128]{2,1,0:T(1,128)}), f32[32,1,128]{2,1,0:T(1,128)S(1)}, u32[]{:S(2)}, u32[]{:S(2)}) async-start(f32[32,1,128]{2,1,0:T(1,128)} %bitcast.43), calls=%async_computation.6 | async-start | bytes 32768 | tf_op jit(solution)/shard_map/all_to_all | solution.py:846
  82.3 0.5 slice.181
  83.5 5.9 %all-to-all-done.6 = f32[32,1,128]{2,1,0:T(1,128)S(1)} async-done(((f32[32,1,128]{2,1,0:T(1,128)}), f32[32,1,128]{2,1,0:T(1,128)S(1)}, u32[]{:S(2)}, u32[]{:S(2)}) %all-to-all-start.6) | async-done | bytes 16416 | tf_op jit(solution)/shard_map/all_to_all | solution.py:846
  89.4 0.5 finish.1
  90.0 0.0 copy-done.2
  90.0 0.0 copy-done.3
  90.0 0.0 copy-done.4
  90.0 0.2 conditional.1
  90.3 0.0 copy-start
  90.3 0.0 copy-start.5
  90.3 0.0 copy-start.6
  90.3 0.5 copy-done
  90.8 0.0 copy-done.5
  90.9 0.0 copy-done.6
  (3 shorter events, 0.0 us)
Async XLA Ops:
  61.2 28.8 %copy-start.2 = (s32[1,1,2,324]{3,2,1,0:T(2,128)S(1)}, s32[1,1,2,324]{3,2,1,0:T(2,128)}, u32[]{:S(2)}) copy-start(s32[1,1,2,324]{3,2,1,0:T(2,128)} %pairs.1) | copy-start | bytes 7780
  61.2 28.8 %copy-start.3 = (f32[3,2,2,3,128]{4,2,3,1,0:T(2,128)S(1)}, f32[3,2,2,3,128]{4,2,3,1,0:T(2,128)}, u32[]{:S(2)}) copy-start(f32[3,2,2,3,128]{4,2,3,1,0:T(2,128)} %param.16) | copy-start | bytes 55300
  61.2 28.8 %copy-start.4 = (f32[3,2,2,3,128]{4,2,3,1,0:T(2,128)S(1)}, f32[3,2,2,3,128]{4,2,3,1,0:T(2,128)}, u32[]{:S(2)}) copy-start(f32[3,2,2,3,128]{4,2,3,1,0:T(2,128)} %param.17) | copy-start | bytes 55300
  79.5 10.0 %all-to-all-start.6 = ((f32[32,1,128]{2,1,0:T(1,128)}), f32[32,1,128]{2,1,0:T(1,128)S(1)}, u32[]{:S(2)}, u32[]{:S(2)}) async-start(f32[32,1,128]{2,1,0:T(1,128)} %bitcast.43), calls=%async_computation.6 | async-start | bytes 32768 | tf_op jit(solution)/shard_map/all_to_all | solution.py:846
  90.3 0.6 copy-start
  90.3 0.6 copy-start.5
  90.3 0.6 copy-start.6

commit v2 on v1

v2 whole, which is shorter than its diff:
```python
from functools import partial

import jax
import jax.numpy as jnp
from jax import lax
from jax.experimental import pallas as pl
from jax.experimental.pallas import tpu as pltpu
from jax.sharding import PartitionSpec as P

CB = 4
TILE = 128
BXT = 2
BYT = 2
TZ = 3
TILES = 12
STEPS = 4
SUB = 6


lattice_edge = 3.1652
density_cut = 4.400224
embed_scale = 1.896373
pair_cut = 3.25
coef_zero = 47.1346499
coef_one = -33.7665655
coef_two = 6.2541999
time_step = 0.005
atom_mass = 0.0190534
friction = 1.0
heat_capacity = 0.02
diffusion_rate = 0.12


def padded_2(block, sides, width):
    for axis, dim in sides:
        count = lax.axis_size(axis)
        forward = [(i, i + 1) for i in range(count - 1)]
        forward.append((count - 1, 0))
        backward = [(target, source) for source, target in forward]
        low = lax.ppermute(
            lax.slice_in_dim(block, block.shape[dim] - width, None, axis=dim), axis, forward
        )
        high = lax.ppermute(lax.slice_in_dim(block, 0, width, axis=dim), axis, backward)
        block = jnp.concatenate([low, block, high], axis=dim)
    return block


def lattice_sites():
    serial = jnp.arange(TILE, dtype=jnp.int32)
    cell_number = serial // 2
    half_step = (serial % 2).astype(jnp.float32) * 0.5
    corners = jnp.stack([cell_number // (CB * CB), cell_number // CB % CB, cell_number % CB])
    return lattice_edge * (corners.astype(jnp.float32) + half_step[None, :])


def plane_table(plane_total):
    serial = jnp.arange(TILE, dtype=jnp.int32)
    cell_number = serial // 2
    layer = 2 * (cell_number % CB) + serial % 2
    tiles = jnp.arange(TZ, dtype=jnp.int32)
    whole = tiles[:, None] * (2 * CB) + layer[None, :]
    return whole * plane_total // (2 * CB * TZ)


def pair_geometry(window, tile_index, neighbour_code, lattice):
    wide_y = BYT + 2
    depth_t = tile_index % TZ
    inner_y = tile_index // TZ % BYT
    inner_x = tile_index // (TZ * BYT)
    shift_x = neighbour_code // 9
    shift_y = neighbour_code // 3 % 3
    shift_z = neighbour_code % 3
    flattened = window.reshape(window.shape[0], (BXT + 2) * wide_y * TZ, TILE)
    own_index = ((inner_x + 1) * wide_y + inner_y + 1) * TZ + depth_t
    other_index = ((inner_x + shift_x) * wide_y + inner_y + shift_y) * TZ + (
        depth_t + shift_z - 1 + TZ
    ) % TZ
    own_tile = lax.dynamic_index_in_dim(flattened, own_index, 1, keepdims=False)
    other_tile = lax.dynamic_index_in_dim(flattened, other_index, 1, keepdims=False)
    offset = jnp.stack([shift_x - 1, shift_y - 1, shift_z - 1]).astype(jnp.float32) * (
        CB * lattice_edge
    )
    left = lattice + own_tile
    right = lattice + other_tile + offset[:, None]
    delta = left[:, :, None] - right[:, None, :]
    square = jnp.sum(delta * delta, axis=0)
    serial = jnp.arange(TILE, dtype=jnp.int32)
    same_atom = (neighbour_code == 13) & (serial[:, None] == serial[None, :])
    distance = jnp.sqrt(jnp.where(same_atom, 100.0, square))
    return (delta, distance, own_index, other_index)


def density_term(window, lattice, tile_index, neighbour_code):
    delta, distance, own_index, other_index = pair_geometry(
        window, tile_index, neighbour_code, lattice
    )
    dens_gap = distance - density_cut
    return jnp.sum(jnp.where(distance < density_cut, dens_gap * dens_gap, 0.0), axis=1)[None]


def force_term(window, embed_window, lattice, tile_index, neighbour_code):
    delta, distance, own_index, other_index = pair_geometry(
        window, tile_index, neighbour_code, lattice
    )
    flat_embed = embed_window.reshape((BXT + 2) * (BYT + 2) * TZ, TILE)
    own_embed = lax.dynamic_index_in_dim(flat_embed, own_index, 0, keepdims=False)
    other_embed = lax.dynamic_index_in_dim(flat_embed, other_index, 0, keepdims=False)
    pair_gap = distance - pair_cut
    poly = coef_zero + coef_one * distance + coef_two * distance * distance
    pair_slope = jnp.where(
        distance < pair_cut,
        2.0 * pair_gap * poly + pair_gap * pair_gap * (coef_one + 2.0 * coef_two * distance),
        0.0,
    )
    dens_gap = distance - density_cut
    dens_slope = jnp.where(distance < density_cut, 2.0 * dens_gap, 0.0)
    scalar = (pair_slope + (own_embed[:, None] + other_embed[None, :]) * dens_slope) / distance
    return -jnp.sum(scalar[None] * delta, axis=2)


def sweep_pairs(term_fn, channels, pair_table, pair_total):
    initial = jnp.zeros((channels, TILES, TILE), jnp.float32)

    def block_add(block_index, running):
        start = block_index * 27
        chosen = lax.dynamic_slice_in_dim(pair_table, start, 27, 1)
        live = start + jnp.arange(27, dtype=jnp.int32) < pair_total
        terms = jax.vmap(term_fn)(chosen[0], chosen[1])
        terms = jnp.where(live[:, None, None], terms, 0.0)
        return running.at[:, chosen[0]].add(jnp.swapaxes(terms, 0, 1))

    blocks = (pair_total + 26) // 27
    total = lax.fori_loop(0, blocks, block_add, initial)
    return total.reshape(channels, BXT, BYT, TZ, TILE)


def relax_slab(padded):
    center = padded[1:-1]
    beside_all = padded[2:] + padded[:-2] + jnp.roll(center, 1, 1) + jnp.roll(center, -1, 1)
    beside_all = beside_all + jnp.roll(center, 1, 2) + jnp.roll(center, -1, 2)
    return center + diffusion_rate * (beside_all - 6.0 * center)


def one_step(lattice, pair_table, pair_total, planes, owners, across, carry, noise_now):
    positions, speeds, heat_field = carry
    slab_depth = heat_field.shape[0]
    plane_total = slab_depth * owners
    arrived = lax.all_to_all(
        heat_field.reshape(slab_depth, owners), ("gx", "gy"), split_axis=1, concat_axis=0, tiled=True
    )
    column = arrived.reshape(-1)
    column_temp = jnp.take(column, planes).reshape(TZ, TILE)
    local_temp = jnp.broadcast_to(column_temp, (BXT, BYT, TZ, TILE))
    window = padded_2(positions, (("gx", 1), ("gy", 2)), 1)
    density = sweep_pairs(partial(density_term, window, lattice), 1, pair_table, pair_total)
    embed_slope = -embed_scale / (2.0 * jnp.sqrt(density))
    embed_window = padded_2(embed_slope, (("gx", 1), ("gy", 2)), 1)
    force = sweep_pairs(partial(force_term, window, embed_window, lattice), 3, pair_table, pair_total)
    kicker = jnp.sqrt(2.0 * friction * atom_mass * local_temp / time_step)[None] * noise_now
    speeds = speeds + time_step / atom_mass * (force - friction * atom_mass * speeds + kicker)
    positions = positions + time_step * speeds
    power = friction * atom_mass * time_step * jnp.sum(speeds * speeds, axis=0)
    tile_power = jnp.sum(power, axis=(0, 1)).reshape(-1)
    energy = jnp.zeros((plane_total,), jnp.float32).at[planes].add(tile_power)
    arrived = lax.all_to_all(
        energy.reshape(plane_total, 1), ("gx", "gy"), split_axis=0, concat_axis=1, tiled=True
    )
    heat_field = heat_field + arrived.reshape(slab_depth, *across) / heat_capacity

    def relax(sub_index, heat):
        return relax_slab(padded_2(heat, ((("gx", "gy"), 0),), 1))

    heat_field = lax.fori_loop(0, SUB, relax, heat_field)
    return (positions, speeds, heat_field)


def whole_sweep(displacement, velocity, noise, electron_temp, pair_list, pair_count):
    across = (lax.axis_size("gx"), lax.axis_size("gy"))
    owners = across[0] * across[1]
    planes = plane_table(electron_temp.shape[0] * owners).reshape(-1)
    step = partial(
        one_step, lattice_sites(), pair_list[0, 0], pair_count[0, 0], planes, owners, across
    )
    return lax.fori_loop(
        0,
        STEPS,
        lambda n, carry: step(carry, lax.dynamic_index_in_dim(noise, n, 0, keepdims=False)),
        (displacement, velocity, electron_temp),
    )


NEAR_SHELLS = (3, 4, 8)
FAR_SHELLS = (11, 12)
NEAR_LIMIT = 0.2900
FAR_LIMIT = 0.8170
HALF = 0.5 * lattice_edge
FAR_AWAY = 1.0e6
ROWS = 20
BASE = 2
SIZE = TZ * ROWS
EDGES = (2, 3)


def site_offsets(shells):
    span = range(-3, 4)
    found = []
    for x in span:
        for y in span:
            for z in span:
                if x % 2 == y % 2 == z % 2 and x * x + y * y + z * z in shells:
                    found.append((x, y, z))
    return found


def grouped(offsets):
    table = {}
    for x, y, z in offsets:
        table.setdefault((y, z), []).append(x)
    return sorted(table.items())


NEAR = site_offsets(NEAR_SHELLS)
FAR = site_offsets(FAR_SHELLS)
MASK_SLOT = {offset: slot for slot, offset in enumerate(NEAR + FAR)}
MASKS = len(MASK_SLOT)


def by_x(groups):
    table = {}
    for n, ((dy, dz), dxs) in enumerate(groups):
        for dx in dxs:
            table.setdefault(dx, []).append((n, dy, dz))
    return sorted(table.items())


def sign(value):
    return (value > 0) - (value < 0)


def sources(dy, dz):
    s = sign(dz)
    if dy % 2 == 0:
        k = dy // 2
        out = [(None, 0, dz + 8 * k, 0)]
        if s:
            out.append((None, s, dz - 8 * s + 8 * k, 0))
        return out
    low = (dy - 1) // 2
    out = [(0, 0, dz + 8 * low, 0), (1, 0, dz + 8 * (low + 1), 1)]
    for parity, k in ((0, low), (1, low + 1)):
        if any(not 0 <= iz + dz < 8 for iz in range(parity, 8, 2)):
            out.append((parity, s, dz - 8 * s + 8 * k, parity))
    return out


def lanes_of(shape=(8, 128)):
    return lax.broadcasted_iota(jnp.int32, shape, len(shape) - 1)


def rows_of(shape=(8, 128)):
    return lax.broadcasted_iota(jnp.int32, shape, len(shape) - 2)


def turn(value, amount):
    amount = (-amount) % 128
    return value if amount == 0 else pltpu.roll(value, amount, value.ndim - 1)


def pick_lanes(value, index):
    return jnp.take_along_axis(value, index, axis=1, mode="promise_in_bounds")


class Chunk:
    def __init__(self, owners, cells, first=False):
        self.cells = cells
        self.narrow = owners <= 32
        halo = 9 if cells == 2 else 14
        if self.narrow:
            self.tail = 9 if cells == 2 else 13
            self.tail_lane = 96
            self.reach = (self.tail, 64)
            self.rows = self.tail + 1
        else:
            self.tail = halo
            self.tail_lane = 0
            self.reach = (halo + 1, 64)
            self.rows = halo + 2
        if first:
            self.live = [(self.reach[0], 0), (self.rows, 0), (self.rows, 64)]
            self.rows += 1

    def x_home(self, plane, row):
        if plane < 8:
            return self.cells * (plane // 2) + row, plane % 2
        return 4 * self.cells + row // 2, row % 2


def repeat_tail(value, chunk):
    if not chunk.narrow:
        return value
    return pick_lanes(value, 96 + lanes_of(value.shape) % 32)


def from_tiles(read, out):
    lane = lanes_of((TZ, 128))
    own = (lane >= 32) & (lane < 96)
    for c in range(3):
        for ix in range(BXT):
            first, second = [read(c, ix, iy) for iy in range(BYT)]
            for cx in range(CB):
                both = jnp.where(lane < 64, turn(first, 32 * cx - 32), turn(second, 32 * cx - 64))
                start = c * TZ * 8 + CB * ix + cx
                out[pl.ds(start, TZ, stride=8), :] = jnp.where(own, both, 0.0)


def to_tiles(source, out):
    lane = lanes_of((TZ, 128))
    for c in range(3):
        for ix in range(BXT):
            rows = [source[pl.ds(c * TZ * 8 + CB * ix + cx, TZ, stride=8), :] for cx in range(CB)]
            for iy in range(BYT):
                value = None
                for cx in range(CB):
                    piece = turn(rows[cx], 32 + 32 * iy - 32 * cx)
                    value = piece if value is None else jnp.where(lane >= 32 * cx, piece, value)
                out[c, ix, :, iy, :] = value


def stage_halo(own, stage, chunk, tail_row, extras):
    w = chunk.cells
    lane, row = lanes_of(), rows_of()
    kinds = {}
    depth = stage.shape[0] // 4
    low = lane < 64
    third = [pick for pick in range(5)] if w == 3 else []
    for kind, (axis, side) in enumerate((("x", -1), ("x", 1), ("y", -1), ("y", 1))):
        at = kind * depth
        kinds[(axis, side)] = at
        if axis == "x":
            first = 8 - w if side == 1 else 0
            for pair in range(4):
                both = jnp.where(low, turn(own(2 * pair), 32), turn(own(2 * pair + 1), -32))
                stage[at + w * pair : at + w * pair + w, :] = both[first : first + w]
            last = own(8)
            a, b = turn(last, 32), turn(last, -32)
            low1 = lanes_of((1, 128)) < 64
            stage[at + 4 * w : at + 4 * w + 1, :] = jnp.where(
                low1, a[first : first + 1], b[first + 1 : first + 2]
            )
            if w == 3:
                stage[at + 13 : at + 14, :] = a[first + 2 : first + 3]
        else:
            start = 80 if side == 1 else 32
            packed = None
            for plane in range(8):
                piece = turn(own(plane), start - 16 * plane)
                packed = piece if packed is None else jnp.where(lane >= 16 * plane, piece, packed)
            stage[at : at + 8, :] = packed
            flat = pick_lanes(own(8), start + lane % 16)
            flat = jnp.where(lane // 16 == row, flat, 0.0)
            stage[at + 8 : at + 9, :] = jnp.sum(flat, axis=0, keepdims=True)
            start = 72 if side == 1 else 48
            for pair in third:
                flat = pick_lanes(own(2 * pair), start + lane % 8)
                if pair < 4:
                    flat = jnp.where(low, flat, pick_lanes(own(2 * pair + 1), start + lane % 8))
                flat = jnp.where(lane % 64 // 8 == row, flat, 0.0)
                stage[at + 9 + pair : at + 10 + pair, :] = jnp.sum(flat, axis=0, keepdims=True)
        for (where, lane_from, lane_to), value in tail_row + extras.get((axis, side), []):
            lane1 = lanes_of((1, 128))
            old = stage[at + where : at + where + 1, :]
            here = (lane1 >= lane_from) & (lane1 < lane_to)
            stage[at + where : at + where + 1, :] = jnp.where(here, value, old)
    return kinds


def send_chunks(stage, kinds, send_ref, chunk, ids, owners):
    tails = sorted({chunk.tail, chunk.reach[0]})
    at = kinds[("x", 1)]
    rows = {where: stage[at + where : at + where + 1, :] for where in tails}

    def fill(index, carry):
        for where in tails:
            send_ref[index, :, 128 * where : 128 * where + 128] = rows[where]
        return carry

    lax.fori_loop(0, owners, fill, 0, unroll=8)
    for (sx, sy), ident in ids.items():
        if (sx, sy) == (0, 0):
            continue
        at = kinds[("y", sy)] if sy else kinds[("x", sx)]
        for k in range(chunk.rows):
            send_ref[ident, :, 128 * k : 128 * k + 128] = stage[at + k : at + k + 1, :]


def receive_chunks(recv_ref, landed, tails_at, chunk, ids, owners):
    depth = landed.shape[0] // 9
    homes = {}
    for n, ((sx, sy), ident) in enumerate(ids.items()):
        if (sx, sy) == (0, 0):
            continue
        homes[(sx, sy)] = n * depth
        for k in range(chunk.rows):
            landed[n * depth + k : n * depth + k + 1, :] = recv_ref[ident, :, 128 * k : 128 * k + 128]

    tails = sorted({chunk.tail, chunk.reach[0]})

    def take(index, carry):
        for n, where in enumerate(tails):
            tails_at[pl.ds(n * owners + index, 1), :] = recv_ref[index, :, 128 * where : 128 * where + 128]
        return carry

    lax.fori_loop(0, owners, take, 0, unroll=8)
    return homes


def build_window(own, landed, homes, window, chunk):
    w = chunk.cells
    lane, row = lanes_of(), rows_of()
    zero = jnp.zeros((8, 128), jnp.float32)
    for plane in range(9):
        at = plane * ROWS + BASE
        centre = own(plane)
        before, after = zero, zero
        for sy in (-1, 1):
            target = 16 if sy == -1 else 96
            here = (lane >= target) & (lane < target + 16)
            beyond = 8 if sy == -1 else 112
            here_third = (lane >= beyond) & (lane < beyond + 8)
            for sx in (-1, 0, 1):
                base = homes[(sx, sy)]
                if plane < 8:
                    piece = turn(landed[base : base + 8, :], 16 * plane - target)
                else:
                    wide = jnp.broadcast_to(landed[base + 8 : base + 9, :], (8, 128))
                    piece = pick_lanes(wide, 16 * row + lane % 16)
                old = (before, centre, after)[sx + 1]
                new = jnp.where(here, piece, old)
                if w == 3:
                    wide = landed[base + 9 + plane // 2 : base + 10 + plane // 2, :]
                    wide = jnp.broadcast_to(wide, (8, 128))
                    piece = pick_lanes(wide, 64 * (plane % 2) + 8 * row + lane % 8)
                    new = jnp.where(here_third, piece, new)
                if sx == -1:
                    before = new
                elif sx == 0:
                    centre = new
                else:
                    after = new
        window[at + 4 : at + 12, :] = centre
        window[at : at + 4, :] = before[4:]
        window[at + 12 : at + 16, :] = after[:4]
        here1 = (lanes_of((1, 128)) >= 32) & (lanes_of((1, 128)) < 96)
        for sx in (-1, 1):
            base = homes[(sx, 0)]
            for k in range(w):
                home, half = chunk.x_home(plane, k)
                piece = turn(landed[base + home : base + home + 1, :], -32 if half == 0 else 32)
                to = at + (4 - w + k if sx == -1 else 12 + k)
                old = window[to : to + 1, :]
                window[to : to + 1, :] = jnp.where(here1, piece, old)


def shifted_planes(count, source, out, groups, constants):
    half_layer = lanes_of((16, 128)) % 8
    parity = half_layer % 2
    for n, ((dy, dz), _) in enumerate(groups):
        carried = (half_layer + dz >= 8) | (half_layer + dz < 0)
        for c in range(count):
            for t in range(TZ):
                value = None
                for want, carry_z, shift, down in sources(dy, dz):
                    row = (c * TZ + (t + carry_z) % TZ) * ROWS + BASE + down
                    piece = turn(source[row : row + 16, :], shift)
                    if value is None:
                        value = piece
                        continue
                    here = None
                    if want is not None:
                        here = parity == want
                    if carry_z:
                        here = carried if here is None else here & carried
                    value = jnp.where(here, piece, value)
                shift_by = constants(c, dy, dz)
                if shift_by:
                    value = value + shift_by
                at = n * count * SIZE + (c * TZ + t) * ROWS + BASE
                out[at : at + 16, :] = value


def coordinate_shift(c, dy, dz):
    return (0.0, HALF * dy, HALF * dz)[c]


def no_shift(c, dy, dz):
    return 0.0


def row_start(dx):
    return dx // 2 if dx % 2 == 0 else (dx - 1) // 2


def densities(window, moved, masks_ref, slope, gaps, inverses, groups):
    def sweep(rows, keep):
        own = [window[rows(c * SIZE), :] for c in range(3)]
        total = jnp.zeros(own[0].shape, jnp.float32)
        for dx, parts in by_x(groups):
            down = row_start(dx)
            own_x = own[0] - HALF * dx
            for n, dy, dz in parts:
                other = [moved[rows((3 * n + c) * SIZE + down), :] for c in range(3)]
                slot = MASK_SLOT[(dx, dy, dz)]
                ex = own_x - other[0]
                ey = own[1] - other[1]
                ez = own[2] - other[2]
                square = ex * ex + ey * ey + (ez * ez + masks_ref[rows(slot * SIZE), :])
                inverse = lax.rsqrt(square)
                gap = jnp.minimum(square * inverse - density_cut, 0.0)
                total = total + gap * gap
                if keep is not None:
                    gaps[keep + 24 * slot : keep + 24 * slot + 8, :] = gap
                    inverses[keep + 24 * slot : keep + 24 * slot + 8, :] = inverse
        slope[rows(0), :] = -embed_scale * lax.rsqrt(total)

    for t in range(TZ):
        sweep(lambda base: pl.ds(base + t * ROWS + BASE + 4, 8), 8 * t)
    for edge in EDGES:
        sweep(lambda base: pl.ds(base + BASE + edge, 2 * TZ, stride=ROWS // 2), None)


def forces(t, window, moved, slope, slope_moved, gaps, inverses, groups):
    at = t * ROWS + BASE + 4
    own = [window[c * SIZE + at : c * SIZE + at + 8, :] for c in range(3)]
    own_slope = slope[at : at + 8, :]
    first = 2.0 * (coef_zero + coef_one * pair_cut + coef_two * pair_cut * pair_cut)
    second = 3.0 * (coef_one + 2.0 * coef_two * pair_cut)
    third = 4.0 * coef_two
    zero = jnp.zeros((8, 128), jnp.float32)
    total = [zero, zero, zero]
    sum_all = zero
    for dx, parts in by_x(groups):
        down = row_start(dx)
        sum_here = zero
        for n, dy, dz in parts:
            slot = MASK_SLOT[(dx, dy, dz)]
            row = 3 * n * SIZE + at + down
            other_slope = slope_moved[n * SIZE + at + down : n * SIZE + at + down + 8, :]
            gap = gaps[24 * slot + 8 * t : 24 * slot + 8 * t + 8, :]
            inverse = inverses[24 * slot + 8 * t : 24 * slot + 8 * t + 8, :]
            near = jnp.minimum(gap + (density_cut - pair_cut), 0.0)
            scalar = (own_slope + other_slope) * gap + near * (first + near * (second + third * near))
            scalar = scalar * inverse
            sum_here = sum_here + scalar
            for c in range(3):
                total[c] = total[c] + scalar * moved[row + c * SIZE : row + c * SIZE + 8, :]
        sum_all = sum_all + sum_here
        if dx:
            total[0] = total[0] + (HALF * dx) * sum_here
    return [total[c] - own[c] * sum_all for c in range(3)]


def diffuse_grid(grid, across):
    nx, ny = across
    for _ in range(SUB):
        columns = []
        for x in range(nx):
            heat = grid[x]
            beside = grid[(x + 1) % nx] + grid[(x - 1) % nx]
            beside = beside + pltpu.roll(heat, 1, 0) + pltpu.roll(heat, ny - 1, 0)
            beside = beside + pltpu.roll(heat, 1, 1) + pltpu.roll(heat, 127, 1)
            columns.append(heat + diffusion_rate * (beside - 6.0 * heat))
        grid = columns
    return grid


LAYERS = 2 * CB * TZ


def temperatures_by_layer(column, plane_total):
    layer = 2 * CB * rows_of() + lanes_of() % (2 * CB)
    layer = jnp.minimum(layer, LAYERS - 1)
    return pick_lanes(jnp.broadcast_to(column, (8, 128)), layer * plane_total // LAYERS)


def energies_by_plane(power, plane_total):
    row, lane = rows_of(), lanes_of()
    stacked = jnp.zeros((8, 128), jnp.float32)
    for t in range(TZ):
        stacked = jnp.where(row == t, power[t], stacked)
    for shift in (8, 16, 32, 64):
        stacked = stacked + pltpu.roll(stacked, shift, 1)
    plane = lane % plane_total
    start = (plane * LAYERS + plane_total - 1) // plane_total
    total = jnp.zeros((8, 128), jnp.float32)
    for extra in range(max(1, -(-LAYERS // plane_total))):
        layer = start + extra
        inside = layer - 2 * CB * row
        here = (inside >= 0) & (inside < 2 * CB) & (layer < LAYERS)
        here = here & (layer * plane_total // LAYERS == plane)
        taken = pick_lanes(stacked, jnp.clip(inside, 0, 2 * CB - 1))
        total = total + jnp.where(here, taken, 0.0)
    return jnp.sum(total, axis=0, keepdims=True)


def neighbour_ids(across):
    nx, ny = across
    bx, by = lax.axis_index("gx"), lax.axis_index("gy")
    at_x = {-1: jnp.where(bx == 0, nx - 1, bx - 1), 0: bx, 1: jnp.where(bx == nx - 1, 0, bx + 1)}
    at_y = {-1: jnp.where(by == 0, ny - 1, by - 1), 0: by, 1: jnp.where(by == ny - 1, 0, by + 1)}
    return {(sx, sy): at_x[sx] * ny + at_y[sy] for sx in (-1, 0, 1) for sy in (-1, 0, 1)}


def prepare(across, chunk, disp, heat, pairs, count, send, own_u, live, lists, disp_in, heat_in, pairs_in, count_in, stage, sems):
    nx, ny = across
    owners = nx * ny
    copies = [
        pltpu.make_async_copy(source, target, sems.at[n])
        for n, (source, target) in enumerate(
            ((disp, disp_in), (heat, heat_in), (pairs, pairs_in), (count, count_in))
        )
    ]
    for copy in copies:
        copy.start()
    lists[...] = jnp.full(lists.shape, -1, jnp.int32)
    for copy in copies:
        copy.wait()

    from_tiles(lambda c, ix, iy: disp_in[c, ix, :, iy, :], own_u)

    slots = pairs_in.shape[3]
    width = lists.shape[1]
    lists[0:2, 0:slots] = pairs_in[0, 0]
    tile = lists[0:1, :]
    code = lists[1:2, :]
    valid = (lanes_of((1, width)) < count_in[0, 0]) & (tile >= 0)
    column = jnp.where(tile >= 3, 1, 0) + jnp.where(tile >= 6, 1, 0) + jnp.where(tile >= 9, 1, 0)
    depth = jnp.where(valid, tile - 3 * column, -1)
    place = 32 * column + code
    left = jnp.where(rows_of((8, width)) == depth, 1.0, 0.0)
    right = jnp.where(rows_of((128, width)) == place, 1.0, 0.0)
    found = lax.dot_general(
        left, right, (((1,), (1,)), ((), ())), preferred_element_type=jnp.float32
    )
    live[...] = found

    lane_n = lanes_of((nx, 128))
    planes = jnp.zeros((nx, 128), jnp.float32)
    for y in range(ny):
        value = jnp.broadcast_to(heat_in[0, :, y : y + 1], (nx, 128))
        planes = jnp.where(lane_n % ny == y, value, planes)
    planes = jnp.where(lane_n % owners // ny == rows_of((nx, 128)), planes, 0.0)
    field = jnp.sum(planes, axis=0, keepdims=True)

    lane = lanes_of()
    halves = {
        ("x", -1): found,
        ("x", 1): turn(found, 64),
        ("y", -1): jnp.where(lane < 32, found, turn(found, 32)),
        ("y", 1): jnp.where(lane < 32, turn(found, 32), turn(found, 64)),
    }
    extras = {}
    for key, value in halves.items():
        extras[key] = [
            ((where, to, to + 64), value[t : t + 1] if to == 0 else turn(value, -64)[t : t + 1])
            for t, (where, to) in enumerate(chunk.live)
        ]
    kinds = stage_halo(
        lambda plane: own_u[8 * plane : 8 * plane + 8, :],
        stage,
        chunk,
        [((chunk.tail, chunk.tail_lane, 128), field)],
        extras,
    )
    send_chunks(stage, kinds, send, chunk, neighbour_ids(across), owners)


def make_masks(chunk, homes, landed, live, masks_ref, table, spread_ref, cases):
    lane1 = lanes_of((1, 128))
    table[...] = jnp.zeros((128, 128), jnp.float32)
    for x in range(4):
        for y in range(4):
            sx, sy = (-1, 0, 0, 1)[x], (-1, 0, 0, 1)[y]
            ix, iy = (1, 0, 1, 0)[x], (1, 0, 1, 0)[y]
            row = jnp.zeros((1, 128), jnp.float32)
            for t in range(TZ):
                if (sx, sy) == (0, 0):
                    value, start = live[t : t + 1, :], 32 * (2 * ix + iy)
                else:
                    where, start = chunk.live[t]
                    value = landed[homes[(sx, sy)] + where : homes[(sx, sy)] + where + 1, :]
                    start = start + 32 * (ix if sy else iy)
                here = (lane1 >= 32 * t) & (lane1 < 32 * t + 32)
                row = jnp.where(here, turn(value, start - 32 * t), row)
            table[4 * x + y : 4 * x + y + 1, :] = row
    by_code = jnp.transpose(table[...])
    big = (128, 128)
    for x in range(4):
        pick = jnp.where(rows_of(big) == 4 * x + lanes_of(big) // 32, 1.0, 0.0)
        alive = jnp.dot(by_code, pick, preferred_element_type=jnp.float32)
        spread_ref[128 * x : 128 * x + 128, :] = FAR_AWAY * (1.0 - alive)

    lane = lanes_of()
    half_layer = lane % 8
    parity = lane % 2
    cell_y = lane // 8 % 4
    low_rows = rows_of() < 4

    def crossing(position, step):
        return (position + step < 0) | (position + step >= 8)

    groups = grouped(NEAR + FAR)

    def at_t(t, carry):
        for code in range(27):
            for block in range(2):
                first, second = [
                    spread_ref[pl.ds(128 * x + 32 * t + code, 1), :] for x in (2 * block, 2 * block + 1)
                ]
                cases[16 * code + 8 * block : 16 * code + 8 * block + 8, :] = jnp.where(
                    low_rows, jnp.broadcast_to(first, (8, 128)), jnp.broadcast_to(second, (8, 128))
                )

        def case(ex, ey, ez, block):
            code = 9 * (ex + 1) + 3 * (ey + 1) + ez + 1
            return cases[16 * code + 8 * block : 16 * code + 8 * block + 8, :]

        for dz in sorted({key[1] for key, _ in groups}):
            cross_z = crossing(half_layer, dz)
            in_z = {}

            def level_z(ex, ey, block):
                if (ex, ey, block) not in in_z:
                    value = case(ex, ey, 0, block)
                    if dz:
                        value = jnp.where(cross_z, case(ex, ey, sign(dz), block), value)
                    in_z[(ex, ey, block)] = value
                return in_z[(ex, ey, block)]

            for (dy, other_z), dxs in groups:
                if other_z != dz:
                    continue
                cross_y = crossing(2 * cell_y + parity, dy)
                in_y = {}

                def level_y(ex, block):
                    if (ex, block) not in in_y:
                        value = level_z(ex, 0, block)
                        if dy:
                            value = jnp.where(cross_y, level_z(ex, sign(dy), block), value)
                        in_y[(ex, block)] = value
                    return in_y[(ex, block)]

                for dx in dxs:
                    cross_x = crossing(2 * (rows_of() % 4) + parity, dx)
                    for block in range(2):
                        value = level_y(0, block)
                        if dx:
                            value = jnp.where(cross_x, level_y(sign(dx), block), value)
                        at = MASK_SLOT[(dx, dy, dz)] * SIZE + BASE + 8 * block
                        masks_ref[pl.ds(at + t * ROWS, 8), :] = value
        return carry

    lax.fori_loop(0, TZ, at_t, 0)


def step_kernel(step, across, arriving, leaving, groups, limit, *refs):
    nx, ny = across
    owners = nx * ny
    refs = list(refs)
    last = leaving is None

    def take(count):
        taken = refs[:count]
        del refs[:count]
        return taken

    recv, in_u, in_v, noise = take(4)
    if step == 0:
        (live,) = take(1)
    else:
        masks_ref, in_grid, in_bad = take(3)
    send, out_grid, out_bad, out_u, out_v = take(5)
    if step == 0:
        (masks_ref,) = take(1)
    window, moved, slope, slope_moved, gaps, inverses, landed, tails_at, noise_in, noise_own = take(10)
    sems, u_own, v_own, stage = take(4)
    extra = refs
    if not last:
        u_own, v_own = out_u, out_v
    noise_copy = pltpu.make_async_copy(noise.at[step], noise_in, sems.at[0])
    noise_copy.start()
    if step == 0:
        v_in, table, spread_ref, cases = extra
        v_copy = pltpu.make_async_copy(in_v, v_in, sems.at[1])
        v_copy.start()
    ids = neighbour_ids(across)
    lane = lanes_of()

    homes = receive_chunks(recv, landed, tails_at, arriving, ids, owners)
    if step == 0:
        make_masks(arriving, homes, landed, live, masks_ref, table, spread_ref, cases)

    def own_u(plane):
        return in_u[8 * plane : 8 * plane + 8, :]

    build_window(own_u, landed, homes, window, arriving)
    shifted_planes(3, window, moved, groups, coordinate_shift)
    densities(window, moved, masks_ref, slope, gaps, inverses, groups)
    shifted_planes(1, slope, slope_moved, groups, no_shift)

    tail = repeat_tail(tails_at[0:owners, :], arriving)
    if step == 0:
        table[...] = jnp.zeros((128, 128), jnp.float32)
        table[0:owners, :] = tail
        turned = jnp.transpose(table[...])[:owners]
        reach = 128
        while reach > owners:
            reach //= 2
            turned = turned + pltpu.roll(turned, reach, 1)
        grid = [turned[ny * x : ny * x + ny] for x in range(nx)]
        out_bad[...] = jnp.zeros((8, 128), jnp.float32)
    else:
        grid = [
            in_grid[ny * x : ny * x + ny, :] + tail[ny * x : ny * x + ny] * (1.0 / heat_capacity)
            for x in range(nx)
        ]
        grid = diffuse_grid(grid, across)
        where, start = arriving.reach
        from_row = owners * (where != arriving.tail)
        furthest = tails_at[from_row : from_row + owners, :]
        lane_n = lanes_of((owners, 128))
        furthest = jnp.where((lane_n >= start) & (lane_n < start + 32), furthest, 0.0)
        reached = jnp.max(furthest, axis=0, keepdims=True)
        reached = jnp.max(reached, axis=1, keepdims=True)
        over = jnp.broadcast_to(jnp.where(reached > limit, 1.0, 0.0), (8, 128))
        out_bad[...] = jnp.maximum(in_bad[...], over)
    for x in range(nx):
        out_grid[ny * x : ny * x + ny, :] = grid[x]
    local = temperatures_by_layer(out_grid[pl.ds(ids[(0, 0)], 1), :], owners)
    kick = jnp.sqrt(local * (2.0 * friction * atom_mass / time_step))

    noise_copy.wait()
    from_tiles(lambda c, ix, iy: noise_in[c, ix, :, iy, :], noise_own)
    speeds_in = in_v
    if step == 0:
        v_copy.wait()
        from_tiles(lambda c, ix, iy: v_in[c, ix, :, iy, :], v_own)
        speeds_in = v_own

    active = (lane >= 32) & (lane < 96)
    power = []
    furthest = jnp.zeros((8, 128), jnp.float32)
    for t in range(TZ):
        force = forces(t, window, moved, slope, slope_moved, gaps, inverses, groups)
        layer = jnp.zeros((8, 128), jnp.float32)
        for c in range(3):
            at = 8 * (c * TZ + t)
            speed = speeds_in[at : at + 8, :]
            push = force[c] - friction * atom_mass * speed + kick[t : t + 1] * noise_own[at : at + 8, :]
            speed = speed + time_step / atom_mass * push
            speed = jnp.where(active, speed, 0.0)
            place = own_u(c * TZ + t) + time_step * speed
            v_own[at : at + 8, :] = speed
            u_own[at : at + 8, :] = place
            layer = layer + speed * speed
            furthest = jnp.maximum(furthest, jnp.abs(place))
        power.append(jnp.sum(layer, axis=0, keepdims=True))
    energy = energies_by_plane(power, owners) * (friction * atom_mass * time_step)
    if last:
        send[...] = jnp.broadcast_to(energy, (owners, 128))
        to_tiles(u_own, out_u)
        to_tiles(v_own, out_v)
        return
    furthest = jnp.max(furthest, axis=0, keepdims=True)
    furthest = jnp.broadcast_to(jnp.max(furthest, axis=1, keepdims=True), (1, 128))
    where, start = leaving.reach
    tail_row = [
        ((leaving.tail, leaving.tail_lane, 128), energy),
        ((where, start, start + 32), furthest),
    ]
    kinds = stage_halo(
        lambda plane: u_own[8 * plane : 8 * plane + 8, :], stage, leaving, tail_row, {}
    )
    send_chunks(stage, kinds, send, leaving, ids, owners)


def finish(across, recv, in_grid, heat):
    nx, ny = across
    grid = [
        in_grid[ny * x : ny * x + ny, :] + recv[ny * x : ny * x + ny, :] * (1.0 / heat_capacity)
        for x in range(nx)
    ]
    grid = diffuse_grid(grid, across)
    me = lax.axis_index("gx") * ny + lax.axis_index("gy")
    flat = rows_of((ny, 128)) == lanes_of((ny, 128))
    for x in range(nx):
        mine = jnp.where(lanes_of((ny, 128)) == me, grid[x], 0.0)
        mine = jnp.broadcast_to(jnp.sum(mine, axis=1, keepdims=True), (ny, 128))
        row = jnp.sum(jnp.where(flat, mine, 0.0), axis=0, keepdims=True)
        heat[0, x : x + 1, :] = row[:, :ny]


def exchange(value):
    return lax.all_to_all(value, ("gx", "gy"), split_axis=0, concat_axis=0, tiled=True)


VMEM_BYTES = 28 * 1024 * 1024


def call(kernel, outs, scratch, operands, anywhere=(), name=None):
    specs = [
        pl.BlockSpec(memory_space=pl.ANY if n in anywhere else pltpu.VMEM)
        for n in range(len(operands))
    ]
    return pl.pallas_call(
        kernel,
        out_shape=[jax.ShapeDtypeStruct(shape, jnp.float32) for shape in outs],
        in_specs=specs,
        out_specs=[pl.BlockSpec(memory_space=pltpu.VMEM)] * len(outs),
        scratch_shapes=scratch,
        compiler_params=pltpu.CompilerParams(vmem_limit_bytes=VMEM_BYTES),
        name=name,
    )(*operands)


def stencil_steps(displacement, velocity, noise, electron_temp, pair_list, pair_count):
    across = (lax.axis_size("gx"), lax.axis_size("gy"))
    owners = across[0] * across[1]

    def vmem(*shape):
        return pltpu.VMEM(shape, jnp.float32)

    tiles = (3, BXT, TZ, BYT, TILE)
    placed_u = jnp.swapaxes(displacement, 2, 3)
    placed_v = jnp.swapaxes(velocity, 2, 3)
    placed_noise = jnp.swapaxes(noise, 3, 4)
    slots = pair_list.shape[-1]
    first, two, three = Chunk(owners, 2, True), Chunk(owners, 2), Chunk(owners, 3)
    send, own_u, live = call(
        partial(prepare, across, first),
        [(owners, 1, 128 * first.rows), (72, 128), (8, 128)],
        [
            pltpu.VMEM((8, (slots + 127) // 128 * 128), jnp.int32),
            vmem(*tiles),
            vmem(*electron_temp.shape),
            pltpu.VMEM(pair_list.shape, jnp.int32),
            pltpu.SMEM(pair_count.shape, jnp.int32),
            vmem(4 * 16, 128),
            pltpu.SemaphoreType.DMA((4,)),
        ],
        (placed_u, electron_temp, pair_list, pair_count),
        anywhere=(0, 1, 2, 3),
        name="prepare",
    )
    near, far = grouped(NEAR), grouped(NEAR + FAR)
    plan = [
        (first, two, near, 1.0),
        (two, three, near, NEAR_LIMIT),
        (three, three, far, FAR_LIMIT),
        (three, None, far, FAR_LIMIT),
    ]
    own_v = placed_v
    masks = grid = bad = None
    for step, (arriving, leaving, groups, limit) in enumerate(plan):
        recv = exchange(send)
        last = leaving is None
        pairs = sum(len(dxs) for _, dxs in groups)
        outs = [
            (owners, 128) if last else (owners, 1, 128 * leaving.rows),
            (owners, 128),
            (8, 128),
            tiles if last else (72, 128),
            tiles if last else (72, 128),
        ]
        scratch = [
            vmem(3 * SIZE, 128),
            vmem(len(groups) * 3 * SIZE, 128),
            vmem(SIZE, 128),
            vmem(len(groups) * SIZE, 128),
            vmem(24 * pairs, 128),
            vmem(24 * pairs, 128),
            vmem(9 * 16, 128),
            vmem(2 * owners, 128),
            vmem(*tiles),
            vmem(72, 128),
            pltpu.SemaphoreType.DMA((2,)),
            vmem(72, 128),
            vmem(72, 128),
            vmem(4 * 16, 128),
        ]
        if step == 0:
            outs.append((MASKS * SIZE, 128))
            scratch += [vmem(*tiles), vmem(128, 128), vmem(512, 128), vmem(27 * 16, 128)]
            operands = (recv, own_u, own_v, placed_noise, live)
        else:
            operands = (recv, own_u, own_v, placed_noise, masks, grid, bad)
        got = call(
            partial(step_kernel, step, across, arriving, leaving, groups, limit),
            outs,
            scratch,
            operands,
            anywhere=(2, 3) if step == 0 else (3,),
            name=f"step{step}",
        )
        send, grid, bad, own_u, own_v = got[:5]
        if step == 0:
            masks = got[5]
    recv = exchange(send)
    (heat,) = call(partial(finish, across), [electron_temp.shape], [], (recv, grid), name="finish")
    return bad[0, 0], jnp.swapaxes(own_u, 2, 3), jnp.swapaxes(own_v, 2, 3), heat


def per_device(displacement, velocity, noise, electron_temp, pair_list, pair_count):
    given = (displacement, velocity, noise, electron_temp, pair_list, pair_count)
    bad, new_u, new_v, heat = stencil_steps(*given)
    return lax.cond(bad > 0.5, lambda: whole_sweep(*given), lambda: (new_u, new_v, heat))


def solution(mesh):
    placed = (
        P(None, "gx", "gy", None, None),
        P(None, "gx", "gy", None, None),
        P(None, None, "gx", "gy", None, None),
        P(("gx", "gy"), None, None),
        P("gx", "gy", None, None),
        P("gx", "gy"),
    )
    return jax.shard_map(
        per_device,
        mesh=mesh,
        in_specs=placed,
        out_specs=(
            P(None, "gx", "gy", None, None),
            P(None, "gx", "gy", None, None),
            P(("gx", "gy"), None, None),
        ),
        check_vma=False,
    )
```

time: 91.4 us -> 76.4 us (0.84)
  Pallas kernels: 20.4 us -> 13.3 us
  blocking collectives: 55.2 us -> 49.7 us
  local copies, waits for them, and re-layouts: 4.22 us -> 1.83 us
    pallas_call x6, Pallas kernels: 20.4 us -> 13.3 us  [call(): pl.pallas_call(kernel, out_shape=[jax.ShapeDtypeStruct(shape, jnp.float32...]
    all_to_all x4, blocking collectives: 55.2 us -> 49.7 us  [exchange(): lax.all_to_all(value, ('gx', 'gy'), split_axis=0, concat_axis=0, tiled=True)]
    unnamed x16 -> x15, local copies, waits for them, and re-layouts: 3.68 us -> 1.32 us
where the time goes in v2:
time: 76.4 us; the launch traced here: 76 us
  blocking collectives  49.7 us (65%)
  Pallas kernels  13.3 us (17%)
  waiting for transfers between devices  5.93 us (8%)
  starting transfers between devices  3.01 us (4%)
  between operations  2.07 us (3%)
  local copies, waits for them, and re-layouts  1.83 us (2%)
    all_to_all x4, blocking collectives, exchange(): lax.all_to_all(value, ('gx', 'gy'), split_axis=0, concat_axis=0, tiled=True)  49.7 us
    pallas_call x6, Pallas kernels, call(): pl.pallas_call(kernel, out_shape=[jax.ShapeDtypeStruct(shape, jnp.float32...  13.3 us
    all_to_all x1, waiting for transfers between devices, exchange(): lax.all_to_all(value, ('gx', 'gy'), split_axis=0, concat_axis=0, tiled=True)  5.93 us
    all_to_all x1, starting transfers between devices, exchange(): lax.all_to_all(value, ('gx', 'gy'), split_axis=0, concat_axis=0, tiled=True)  3.01 us
  transfers between devices with their start and end apart: 1, of which 1 were waited for; matrix products, arithmetic and copies ran while one was open for 1% of the time, Pallas kernels for 0%

profile of v2, /device:TPU:0, one launch (start us, length us, event | category | flops | bytes accessed | tf_op | source)
XLA Modules:
  0.0 76.0 jit_solution(12161456059872085707)
XLA Ops:
  0.6 0.7 copy.157.heat
  2.0 1.1 %prepare.1 = (f32[32,1,1408]{2,1,0:T(1,128)S(1)}, f32[72,128]{1,0:T(8,128)S(1)}, f32[8,128]{1,0:T(8,128)S(1)}) custom-call(f32[3,2,3,2,128]{4,3,2,1,0:T(2,128)} %bitcast.398, f32[1,4,8]{2,1,0:T(4,128)S(1)} %copy.157.heat, s32[1,1,2,324]{3,2,1,0:T(2,128)} %pairs.1, s32[1,1]{1,0:T(1,128)S(6)} %copy.156.count), custom_call_target="tpu_custom_call" | custom-call | tf_op jit(solution)/shard_map/prepare/pallas_call | solution.py:915
  3.1 0.0 copy-start.1
  3.1 15.8 %all_to_all.102.refs_0_ = f32[32,1,1408]{2,1,0:T(1,128)S(1)} all-to-all(f32[32,1,1408]{2,1,0:T(1,128)S(1)} %get-tuple-element.989), channel_id=1, replica_groups=mesh['gx'=4,'gy'=8] {'gx','gy'}, dimensions={0} | all-to-all | bytes 360448 | tf_op jit(solution)/shard_map/all_to_all | solution.py:904
  18.9 2.6 %step0.1 = (f32[32,1,1280]{2,1,0:T(1,128)S(1)}, f32[32,128]{1,0:T(8,128)S(1)}, f32[8,128]{1,0:T(8,128)S(1)}, f32[72,128]{1,0:T(8,128)S(1)}, f32[72,128]{1,0:T(8,128)S(1)}, /*index=5*/f32[3480,128]{1,0:T(8,128)S(1)}) custom-call(f32[32,1,1408]{2,1,0:T(1,128)S(1)} %all_to_all.102.refs_0_, f32[72,128]{1,0:T(8,128)S(1)} %get-tuple-element.990.refs_1_, ...), custom_call_target="tpu_custom_call" | custom-call | tf_op jit(solution)/shard_map/step0/pallas_call | solution.py:915
  21.5 10.8 %all_to_all.103.refs_0_ = f32[32,1,1280]{2,1,0:T(1,128)S(1)} all-to-all(f32[32,1,1280]{2,1,0:T(1,128)S(1)} %get-tuple-element.992), channel_id=1, replica_groups=mesh['gx'=4,'gy'=8] {'gx','gy'}, dimensions={0} | all-to-all | bytes 327680 | tf_op jit(solution)/shard_map/all_to_all | solution.py:904
  32.3 2.0 %step1.1 = (f32[32,1,1792]{2,1,0:T(1,128)S(1)}, f32[32,128]{1,0:T(8,128)S(1)}, f32[8,128]{1,0:T(8,128)S(1)}, f32[72,128]{1,0:T(8,128)S(1)}, f32[72,128]{1,0:T(8,128)S(1)}) custom-call(f32[32,1,1280]{2,1,0:T(1,128)S(1)} %all_to_all.103.refs_0_, f32[72,128]{1,0:T(8,128)S(1)} %get-tuple-element.993.refs_1_, f32[72,128]{1,0:T(8,128)S(1)} %get-tuple-element.994.refs_2_, ...), custom_call_target="tpu_custom_call" | custom-call | tf_op jit(solution)/shard_map/step1/pallas_call | solution.py:915
  34.3 11.2 %all_to_all.104.refs_0_ = f32[32,1,1792]{2,1,0:T(1,128)S(1)} all-to-all(f32[32,1,1792]{2,1,0:T(1,128)S(1)} %get-tuple-element.998), channel_id=1, replica_groups=mesh['gx'=4,'gy'=8] {'gx','gy'}, dimensions={0} | all-to-all | bytes 458752 | tf_op jit(solution)/shard_map/all_to_all | solution.py:904
  45.5 0.0 copy-done.1
  45.5 3.2 %step2.1 = (f32[32,1,1792]{2,1,0:T(1,128)S(1)}, f32[32,128]{1,0:T(8,128)S(1)}, f32[8,128]{1,0:T(8,128)S(1)}, f32[72,128]{1,0:T(8,128)S(1)}, f32[72,128]{1,0:T(8,128)S(1)}) custom-call(f32[32,1,1792]{2,1,0:T(1,128)S(1)} %all_to_all.104.refs_0_, f32[72,128]{1,0:T(8,128)S(1)} %get-tuple-element.999.refs_1_, f32[72,128]{1,0:T(8,128)S(1)} %get-tuple-element.1000.refs_2_, ...), custom_call_target="tpu_custom_call" | custom-call | tf_op jit(solution)/shard_map/step2/pallas_call | solution.py:915
  48.7 0.0 copy-start.2
  48.7 0.0 copy-start.3
  48.7 0.0 copy-start.4
  48.7 12.0 %all_to_all.105.refs_0_ = f32[32,1,1792]{2,1,0:T(1,128)S(1)} all-to-all(f32[32,1,1792]{2,1,0:T(1,128)S(1)} %get-tuple-element.1003), channel_id=1, replica_groups=mesh['gx'=4,'gy'=8] {'gx','gy'}, dimensions={0} | all-to-all | bytes 458752 | tf_op jit(solution)/shard_map/all_to_all | solution.py:904
  60.7 3.8 %step3.1 = (f32[32,128]{1,0:T(8,128)}, f32[32,128]{1,0:T(8,128)S(1)}, f32[8,128]{1,0:T(8,128)S(1)}, f32[3,2,3,2,128]{4,3,2,1,0:T(2,128)S(1)}, f32[3,2,3,2,128]{4,3,2,1,0:T(2,128)S(1)}) custom-call(f32[32,1,1792]{2,1,0:T(1,128)S(1)} %all_to_all.105.refs_0_, f32[72,128]{1,0:T(8,128)S(1)} %get-tuple-element.1004.refs_1_, ...), custom_call_target="tpu_custom_call" | custom-call | tf_op jit(solution)/shard_map/step3/pallas_call | solution.py:915
  64.5 3.0 %all-to-all-start.6 = ((f32[32,1,128]{2,1,0:T(1,128)}), f32[32,1,128]{2,1,0:T(1,128)S(1)}, u32[]{:S(2)}, u32[]{:S(2)}) async-start(f32[32,1,128]{2,1,0:T(1,128)} %bitcast.39), calls=%async_computation.6 | async-start | bytes 32768 | tf_op jit(solution)/shard_map/all_to_all | solution.py:904
  67.5 0.5 slice.177
  68.6 5.9 %all-to-all-done.6 = f32[32,1,128]{2,1,0:T(1,128)S(1)} async-done(((f32[32,1,128]{2,1,0:T(1,128)}), f32[32,1,128]{2,1,0:T(1,128)S(1)}, u32[]{:S(2)}, u32[]{:S(2)}) %all-to-all-start.6) | async-done | bytes 16416 | tf_op jit(solution)/shard_map/all_to_all | solution.py:904
  74.6 0.5 finish.1
  75.1 0.0 copy-done.2
  75.1 0.0 copy-done.3
  75.1 0.0 copy-done.4
  75.1 0.2 conditional.1
  75.3 0.0 copy-start.5
  75.4 0.0 copy-start.6
  75.4 0.0 copy-start.7
  75.4 0.5 copy-done.5
  75.9 0.0 copy-done.6
  76.0 0.0 copy-done.7
Async XLA Ops:
  3.1 42.4 %copy-start.1 = (f32[4,3,2,2,3,128]{5,3,4,2,1,0:T(2,128)S(1)}, f32[4,3,2,2,3,128]{5,3,4,2,1,0:T(2,128)}, u32[]{:S(2)}) copy-start(f32[4,3,2,2,3,128]{5,3,4,2,1,0:T(2,128)} %param.18) | copy-start | bytes 221188
  48.7 26.4 %copy-start.2 = (s32[1,1,2,324]{3,2,1,0:T(2,128)S(1)}, s32[1,1,2,324]{3,2,1,0:T(2,128)}, u32[]{:S(2)}) copy-start(s32[1,1,2,324]{3,2,1,0:T(2,128)} %pairs.1) | copy-start | bytes 7780
  48.7 26.4 %copy-start.3 = (f32[3,2,2,3,128]{4,2,3,1,0:T(2,128)S(1)}, f32[3,2,2,3,128]{4,2,3,1,0:T(2,128)}, u32[]{:S(2)}) copy-start(f32[3,2,2,3,128]{4,2,3,1,0:T(2,128)} %param.17) | copy-start | bytes 55300
  48.7 26.4 %copy-start.4 = (f32[3,2,2,3,128]{4,2,3,1,0:T(2,128)S(1)}, f32[3,2,2,3,128]{4,2,3,1,0:T(2,128)}, u32[]{:S(2)}) copy-start(f32[3,2,2,3,128]{4,2,3,1,0:T(2,128)} %param.16) | copy-start | bytes 55300
  64.5 10.1 %all-to-all-start.6 = ((f32[32,1,128]{2,1,0:T(1,128)}), f32[32,1,128]{2,1,0:T(1,128)S(1)}, u32[]{:S(2)}, u32[]{:S(2)}) async-start(f32[32,1,128]{2,1,0:T(1,128)} %bitcast.39), calls=%async_computation.6 | async-start | bytes 32768 | tf_op jit(solution)/shard_map/all_to_all | solution.py:904
  75.3 0.6 copy-start.5
  75.4 0.6 copy-start.6
  75.4 0.6 copy-start.7

commit v3 on v2

--- a/solution.py
+++ b/solution.py
@@ -235,22 +235,6 @@
 
 def sign(value):
     return (value > 0) - (value < 0)
-
-
-def sources(dy, dz):
-    s = sign(dz)
-    if dy % 2 == 0:
-        k = dy // 2
-        out = [(None, 0, dz + 8 * k, 0)]
-        if s:
-            out.append((None, s, dz - 8 * s + 8 * k, 0))
-        return out
-    low = (dy - 1) // 2
-    out = [(0, 0, dz + 8 * low, 0), (1, 0, dz + 8 * (low + 1), 1)]
-    for parity, k in ((0, low), (1, low + 1)):
-        if any(not 0 <= iz + dz < 8 for iz in range(parity, 8, 2)):
-            out.append((parity, s, dz - 8 * s + 8 * k, parity))
-    return out
 
 
 def lanes_of(shape=(8, 128)):
@@ -394,14 +378,14 @@
 
 
 def receive_chunks(recv_ref, landed, tails_at, chunk, ids, owners):
-    depth = landed.shape[0] // 9
+    depth = (landed.shape[0] - 2 * PAD) // 9
     homes = {}
     for n, ((sx, sy), ident) in enumerate(ids.items()):
         if (sx, sy) == (0, 0):
             continue
-        homes[(sx, sy)] = n * depth
+        homes[(sx, sy)] = PAD + n * depth
         for k in range(chunk.rows):
-            landed[n * depth + k : n * depth + k + 1, :] = recv_ref[ident, :, 128 * k : 128 * k + 128]
+            landed[PAD + n * depth + k : PAD + n * depth + k + 1, :] = recv_ref[ident, :, 128 * k : 128 * k + 128]
 
     tails = sorted({chunk.tail, chunk.reach[0]})
 
@@ -414,78 +398,126 @@
     return homes
 
 
-def build_window(own, landed, homes, window, chunk):
+PAD = 8
+
+
+def build_window(own, landed, homes, window, chunk, origin):
     w = chunk.cells
     lane, row = lanes_of(), rows_of()
     zero = jnp.zeros((8, 128), jnp.float32)
+    middle = (lane >= 32) & (lane < 96)
+    first_rows = row < 4
+
+    def outer(start, size, sy):
+        values = [landed[homes[(sx, sy)] + start : homes[(sx, sy)] + start + size, :] for sx in (1, -1)]
+        if size == 1:
+            values = [jnp.broadcast_to(value, (8, 128)) for value in values]
+        return jnp.where(first_rows, values[0], values[1])
+
+    def inner(start, size, sy):
+        value = landed[homes[(0, sy)] + start : homes[(0, sy)] + start + size, :]
+        return jnp.broadcast_to(value, (8, 128))
+
+    sides = (-1, 1)
+    packed = {(sy, out): (outer if out else inner)(0, 8, sy) for sy in sides for out in (0, 1)}
     for plane in range(9):
         at = plane * ROWS + BASE
-        centre = own(plane)
-        before, after = zero, zero
-        for sy in (-1, 1):
+        parts = [own(plane), zero]
+        for sy in sides:
             target = 16 if sy == -1 else 96
             here = (lane >= target) & (lane < target + 16)
             beyond = 8 if sy == -1 else 112
             here_third = (lane >= beyond) & (lane < beyond + 8)
-            for sx in (-1, 0, 1):
-                base = homes[(sx, sy)]
+            for out in (0, 1):
                 if plane < 8:
-                    piece = turn(landed[base : base + 8, :], 16 * plane - target)
+                    piece = turn(packed[(sy, out)], 16 * plane - target)
                 else:
-                    wide = jnp.broadcast_to(landed[base + 8 : base + 9, :], (8, 128))
+                    wide = (outer if out else inner)(8, 1, sy)
                     piece = pick_lanes(wide, 16 * row + lane % 16)
-                old = (before, centre, after)[sx + 1]
-                new = jnp.where(here, piece, old)
+                parts[out] = jnp.where(here, piece, parts[out])
                 if w == 3:
-                    wide = landed[base + 9 + plane // 2 : base + 10 + plane // 2, :]
-                    wide = jnp.broadcast_to(wide, (8, 128))
+                    wide = (outer if out else inner)(9 + plane // 2, 1, sy)
                     piece = pick_lanes(wide, 64 * (plane % 2) + 8 * row + lane % 8)
-                    new = jnp.where(here_third, piece, new)
-                if sx == -1:
-                    before = new
-                elif sx == 0:
-                    centre = new
-                else:
-                    after = new
-        window[at + 4 : at + 12, :] = centre
-        window[at : at + 4, :] = before[4:]
-        window[at + 12 : at + 16, :] = after[:4]
-        here1 = (lanes_of((1, 128)) >= 32) & (lanes_of((1, 128)) < 96)
-        for sx in (-1, 1):
-            base = homes[(sx, 0)]
+                    parts[out] = jnp.where(here_third, piece, parts[out])
+        centre, rim = parts
+        if plane < 8:
+            home, half = chunk.x_home(plane, 0)
+            back = -32 if half == 0 else 32
+            behind = landed[pl.ds(origin + homes[(1, 0)] + home, 8), :]
+            ahead = landed[pl.ds(origin + homes[(-1, 0)] + home - (4 - w) - 4, 8), :]
+            piece = turn(jnp.where(first_rows, behind, ahead), back)
+            rim = jnp.where(middle & ((row < w) | (row >= 8 - w)), piece, rim)
+        else:
             for k in range(w):
                 home, half = chunk.x_home(plane, k)
-                piece = turn(landed[base + home : base + home + 1, :], -32 if half == 0 else 32)
-                to = at + (4 - w + k if sx == -1 else 12 + k)
-                old = window[to : to + 1, :]
-                window[to : to + 1, :] = jnp.where(here1, piece, old)
-
-
-def shifted_planes(count, source, out, groups, constants):
+                back = -32 if half == 0 else 32
+                for sx, to in ((1, k), (-1, 8 - w + k)):
+                    base = homes[(sx, 0)] + home
+                    piece = turn(jnp.broadcast_to(landed[base : base + 1, :], (8, 128)), back)
+                    rim = jnp.where(middle & (row == to), piece, rim)
+        window[pl.ds(origin + at, 8), :] = pltpu.roll(rim, 4, 0)
+        window[pl.ds(origin + at + 12, 8), :] = rim
+        window[pl.ds(origin + at + 4, 8), :] = centre
+
+
+def mix_planes(count, source, mixed, origin):
+    even = lanes_of((16, 128)) % 2 == 0
+    for plane in range(count * TZ):
+        at = plane * ROWS + BASE
+        here = source[pl.ds(origin + at, 16), :]
+        after = turn(source[pl.ds(origin + at + 1, 16), :], 8)
+        mixed[pl.ds(origin + at, 16), :] = jnp.where(even, after, here)
+
+
+def sources(dy, dz, use_mixed):
+    s = sign(dz)
+    low = dy // 2
+    if dy % 2 == 0 or use_mixed:
+        out = [(None, 0, dz + 8 * low, 0)]
+        if s:
+            out.append((None, s, dz - 8 * s + 8 * low, 0))
+        return out
+    out = [(0, 0, dz + 8 * low, 0), (1, 0, dz + 8 * (low + 1), 1)]
+    for parity, k in ((0, low), (1, low + 1)):
+        if any(not 0 <= iz + dz < 8 for iz in range(parity, 8, 2)):
+            out.append((parity, s, dz - 8 * s + 8 * k, parity))
+    return out
+
+
+def shift_planes(count, source, mixed, out, groups, constants, origin):
     half_layer = lanes_of((16, 128)) % 8
     parity = half_layer % 2
-    for n, ((dy, dz), _) in enumerate(groups):
-        carried = (half_layer + dz >= 8) | (half_layer + dz < 0)
-        for c in range(count):
-            for t in range(TZ):
-                value = None
-                for want, carry_z, shift, down in sources(dy, dz):
-                    row = (c * TZ + (t + carry_z) % TZ) * ROWS + BASE + down
-                    piece = turn(source[row : row + 16, :], shift)
-                    if value is None:
-                        value = piece
-                        continue
-                    here = None
-                    if want is not None:
-                        here = parity == want
-                    if carry_z:
-                        here = carried if here is None else here & carried
-                    value = jnp.where(here, piece, value)
-                shift_by = constants(c, dy, dz)
-                if shift_by:
-                    value = value + shift_by
-                at = n * count * SIZE + (c * TZ + t) * ROWS + BASE
-                out[at : at + 16, :] = value
+    slots = {key: n for n, (key, _) in enumerate(groups)}
+    for c in range(count):
+        for dz in sorted({key[1] for key in slots}, key=abs):
+            dys = sorted(key[0] for key in slots if key[1] == dz)
+            carried = (half_layer + dz >= 8) | (half_layer + dz < 0)
+            ref = mixed if dz % 2 and mixed is not None else source
+            wanted = {dy: sources(dy, dz, mixed is not None) for dy in dys}
+            turned = {}
+            for shift, down in sorted({part[2:] for parts in wanted.values() for part in parts}):
+                for t in range(TZ):
+                    at = (c * TZ + t) * ROWS + BASE + down
+                    turned[(t, shift, down)] = turn(ref[pl.ds(origin + at, 16), :], shift)
+            for dy in dys:
+                for t in range(TZ):
+                    value = None
+                    for want, carry_z, shift, down in wanted[dy]:
+                        piece = turned[((t + carry_z) % TZ, shift, down)]
+                        if value is None:
+                            value = piece
+                            continue
+                        here = None
+                        if want is not None:
+                            here = parity == want
+                        if carry_z:
+                            here = carried if here is None else here & carried
+                        value = jnp.where(here, piece, value)
+                    shift_by = constants(c, dy, dz)
+                    if shift_by:
+                        value = value + shift_by
+                    at = slots[(dy, dz)] * count * SIZE + (c * TZ + t) * ROWS + BASE
+                    out[pl.ds(origin + at, 16), :] = value
 
 
 def coordinate_shift(c, dy, dz):
@@ -500,38 +532,32 @@
     return dx // 2 if dx % 2 == 0 else (dx - 1) // 2
 
 
-def densities(window, moved, masks_ref, slope, gaps, inverses, groups):
-    def sweep(rows, keep):
-        own = [window[rows(c * SIZE), :] for c in range(3)]
-        total = jnp.zeros(own[0].shape, jnp.float32)
-        for dx, parts in by_x(groups):
-            down = row_start(dx)
-            own_x = own[0] - HALF * dx
-            for n, dy, dz in parts:
-                other = [moved[rows((3 * n + c) * SIZE + down), :] for c in range(3)]
-                slot = MASK_SLOT[(dx, dy, dz)]
-                ex = own_x - other[0]
-                ey = own[1] - other[1]
-                ez = own[2] - other[2]
-                square = ex * ex + ey * ey + (ez * ez + masks_ref[rows(slot * SIZE), :])
-                inverse = lax.rsqrt(square)
-                gap = jnp.minimum(square * inverse - density_cut, 0.0)
-                total = total + gap * gap
-                if keep is not None:
-                    gaps[keep + 24 * slot : keep + 24 * slot + 8, :] = gap
-                    inverses[keep + 24 * slot : keep + 24 * slot + 8, :] = inverse
-        slope[rows(0), :] = -embed_scale * lax.rsqrt(total)
-
-    for t in range(TZ):
-        sweep(lambda base: pl.ds(base + t * ROWS + BASE + 4, 8), 8 * t)
-    for edge in EDGES:
-        sweep(lambda base: pl.ds(base + BASE + edge, 2 * TZ, stride=ROWS // 2), None)
-
-
-def forces(t, window, moved, slope, slope_moved, gaps, inverses, groups):
+def density_sweep(rows, keep, window, moved, masks_ref, slope, gaps, inverses, groups):
+    own = [window[rows(c * SIZE), :] for c in range(3)]
+    total = jnp.zeros(own[0].shape, jnp.float32)
+    for dx, parts in by_x(groups):
+        down = row_start(dx)
+        own_x = own[0] - HALF * dx
+        for n, dy, dz in parts:
+            other = [moved[rows((3 * n + c) * SIZE + down), :] for c in range(3)]
+            slot = MASK_SLOT[(dx, dy, dz)]
+            ex = own_x - other[0]
+            ey = own[1] - other[1]
+            ez = own[2] - other[2]
+            square = ex * ex + ey * ey + (ez * ez + masks_ref[rows(slot * SIZE), :])
+            inverse = lax.rsqrt(square)
+            gap = jnp.minimum(square * inverse - density_cut, 0.0)
+            total = total + gap * gap
+            if keep is not None:
+                gaps[keep + 24 * slot : keep + 24 * slot + 8, :] = gap
+                inverses[keep + 24 * slot : keep + 24 * slot + 8, :] = inverse
+    slope[rows(0), :] = -embed_scale * lax.rsqrt(total)
+
+
+def forces(t, window, moved, slope, slope_moved, gaps, inverses, groups, origin):
     at = t * ROWS + BASE + 4
-    own = [window[c * SIZE + at : c * SIZE + at + 8, :] for c in range(3)]
-    own_slope = slope[at : at + 8, :]
+    own = [window[pl.ds(origin + (c * SIZE + at), 8), :] for c in range(3)]
+    own_slope = slope[pl.ds(origin + at, 8), :]
     first = 2.0 * (coef_zero + coef_one * pair_cut + coef_two * pair_cut * pair_cut)
     second = 3.0 * (coef_one + 2.0 * coef_two * pair_cut)
     third = 4.0 * coef_two
@@ -544,7 +570,7 @@
         for n, dy, dz in parts:
             slot = MASK_SLOT[(dx, dy, dz)]
             row = 3 * n * SIZE + at + down
-            other_slope = slope_moved[n * SIZE + at + down : n * SIZE + at + down + 8, :]
+            other_slope = slope_moved[pl.ds(origin + (n * SIZE + at + down), 8), :]
             gap = gaps[24 * slot + 8 * t : 24 * slot + 8 * t + 8, :]
             inverse = inverses[24 * slot + 8 * t : 24 * slot + 8 * t + 8, :]
             near = jnp.minimum(gap + (density_cut - pair_cut), 0.0)
@@ -552,25 +578,46 @@
             scalar = scalar * inverse
             sum_here = sum_here + scalar
             for c in range(3):
-                total[c] = total[c] + scalar * moved[row + c * SIZE : row + c * SIZE + 8, :]
+                total[c] = total[c] + scalar * moved[pl.ds(origin + (row + c * SIZE), 8), :]
         sum_all = sum_all + sum_here
         if dx:
             total[0] = total[0] + (HALF * dx) * sum_here
     return [total[c] - own[c] * sum_all for c in range(3)]
 
 
+def binomial(n, k):
+    value = 1
+    for j in range(k):
+        value = value * (n - j) // (j + 1)
+    return value
+
+
 def diffuse_grid(grid, across):
     nx, ny = across
-    for _ in range(SUB):
+    d = diffusion_rate
+    pairs = [
+        [heat] + [pltpu.roll(heat, k, 1) + pltpu.roll(heat, 128 - k, 1) for k in range(1, SUB + 1)]
+        for heat in grid
+    ]
+
+    def powers(x, k):
+        total = None
+        for j in range(k // 2 + 1):
+            weight = binomial(k, j) * binomial(SUB, k) * d**k
+            term = weight * pairs[x][k - 2 * j]
+            total = term if total is None else total + term
+        return total
+
+    result = [powers(x, 0) for x in range(nx)]
+    for k in range(1, SUB + 1):
         columns = []
         for x in range(nx):
-            heat = grid[x]
-            beside = grid[(x + 1) % nx] + grid[(x - 1) % nx]
+            heat = result[x]
+            beside = result[(x + 1) % nx] + result[(x - 1) % nx]
             beside = beside + pltpu.roll(heat, 1, 0) + pltpu.roll(heat, ny - 1, 0)
-            beside = beside + pltpu.roll(heat, 1, 1) + pltpu.roll(heat, 127, 1)
-            columns.append(heat + diffusion_rate * (beside - 6.0 * heat))
-        grid = columns
-    return grid
+            columns.append(((1.0 - 6.0 * d) * heat + powers(x, k)) + d * beside)
+        result = columns
+    return result
 
 
 LAYERS = 2 * CB * TZ
@@ -587,8 +634,6 @@
     stacked = jnp.zeros((8, 128), jnp.float32)
     for t in range(TZ):
         stacked = jnp.where(row == t, power[t], stacked)
-    for shift in (8, 16, 32, 64):
-        stacked = stacked + pltpu.roll(stacked, shift, 1)
     plane = lane % plane_total
     start = (plane * LAYERS + plane_total - 1) // plane_total
     total = jnp.zeros((8, 128), jnp.float32)
@@ -597,8 +642,11 @@
         inside = layer - 2 * CB * row
         here = (inside >= 0) & (inside < 2 * CB) & (layer < LAYERS)
         here = here & (layer * plane_total // LAYERS == plane)
-        taken = pick_lanes(stacked, jnp.clip(inside, 0, 2 * CB - 1))
-        total = total + jnp.where(here, taken, 0.0)
+        first = 32 + jnp.clip(inside, 0, 2 * CB - 1)
+        taken = [pick_lanes(stacked, first + 8 * y) for y in range(BYT * CB)]
+        while len(taken) > 1:
+            taken = [a + b for a, b in zip(taken[::2], taken[1::2])]
+        total = total + jnp.where(here, taken[0], 0.0)
     return jnp.sum(total, axis=0, keepdims=True)
 
 
@@ -783,7 +831,7 @@
     if step == 0:
         (masks_ref,) = take(1)
     window, moved, slope, slope_moved, gaps, inverses, landed, tails_at, noise_in, noise_own = take(10)
-    sems, u_own, v_own, stage = take(4)
+    sems, u_own, v_own, stage, mixed = take(5)
     extra = refs
     if not last:
         u_own, v_own = out_u, out_v
@@ -799,14 +847,6 @@
     homes = receive_chunks(recv, landed, tails_at, arriving, ids, owners)
     if step == 0:
         make_masks(arriving, homes, landed, live, masks_ref, table, spread_ref, cases)
-
-    def own_u(plane):
-        return in_u[8 * plane : 8 * plane + 8, :]
-
-    build_window(own_u, landed, homes, window, arriving)
-    shifted_planes(3, window, moved, groups, coordinate_shift)
-    densities(window, moved, masks_ref, slope, gaps, inverses, groups)
-    shifted_planes(1, slope, slope_moved, groups, no_shift)
 
     tail = repeat_tail(tails_at[0:owners, :], arriving)
     if step == 0:
@@ -839,6 +879,24 @@
     local = temperatures_by_layer(out_grid[pl.ds(ids[(0, 0)], 1), :], owners)
     kick = jnp.sqrt(local * (2.0 * friction * atom_mass / time_step))
 
+    def own_u(plane):
+        return in_u[8 * plane : 8 * plane + 8, :]
+
+    origin = jnp.minimum(lax.axis_index("gx"), 0)
+    build_window(own_u, landed, homes, window, arriving, origin)
+    mix_planes(3, window, mixed, origin)
+    known = (window, moved, masks_ref, slope, gaps, inverses, groups)
+    shift_planes(3, window, mixed, moved, groups, coordinate_shift, origin)
+    for t in range(TZ):
+        start = t * ROWS + BASE + 4
+        density_sweep(lambda base: pl.ds(origin + (base + start), 8), 8 * t, *known)
+    for edge in EDGES:
+        start = BASE + edge
+        density_sweep(
+            lambda base: pl.ds(origin + (base + start), 2 * TZ, stride=ROWS // 2), None, *known
+        )
+    shift_planes(1, slope, None, slope_moved, groups, no_shift, origin)
+
     noise_copy.wait()
     from_tiles(lambda c, ix, iy: noise_in[c, ix, :, iy, :], noise_own)
     speeds_in = in_v
@@ -851,7 +909,7 @@
     power = []
     furthest = jnp.zeros((8, 128), jnp.float32)
     for t in range(TZ):
-        force = forces(t, window, moved, slope, slope_moved, gaps, inverses, groups)
+        force = forces(t, window, moved, slope, slope_moved, gaps, inverses, groups, origin)
         layer = jnp.zeros((8, 128), jnp.float32)
         for c in range(3):
             at = 8 * (c * TZ + t)
@@ -907,9 +965,9 @@
 VMEM_BYTES = 28 * 1024 * 1024
 
 
-def call(kernel, outs, scratch, operands, anywhere=(), name=None):
+def call(kernel, outs, scratch, operands, in_hbm=(), name=None):
     specs = [
-        pl.BlockSpec(memory_space=pl.ANY if n in anywhere else pltpu.VMEM)
+        pl.BlockSpec(memory_space=pltpu.HBM if n in in_hbm else pltpu.VMEM)
         for n in range(len(operands))
     ]
     return pl.pallas_call(
@@ -949,7 +1007,7 @@
             pltpu.SemaphoreType.DMA((4,)),
         ],
         (placed_u, electron_temp, pair_list, pair_count),
-        anywhere=(0, 1, 2, 3),
+        in_hbm=(0, 1, 2, 3),
         name="prepare",
     )
     near, far = grouped(NEAR), grouped(NEAR + FAR)
@@ -973,13 +1031,13 @@
             tiles if last else (72, 128),
         ]
         scratch = [
-            vmem(3 * SIZE, 128),
+            vmem(3 * SIZE + PAD, 128),
             vmem(len(groups) * 3 * SIZE, 128),
             vmem(SIZE, 128),
             vmem(len(groups) * SIZE, 128),
             vmem(24 * pairs, 128),
             vmem(24 * pairs, 128),
-            vmem(9 * 16, 128),
+            vmem(9 * 16 + 2 * PAD, 128),
             vmem(2 * owners, 128),
             vmem(*tiles),
             vmem(72, 128),
@@ -987,6 +1045,7 @@
             vmem(72, 128),
             vmem(72, 128),
             vmem(4 * 16, 128),
+            vmem(3 * SIZE, 128),
         ]
         if step == 0:
             outs.append((MASKS * SIZE, 128))
@@ -999,7 +1058,7 @@
             outs,
             scratch,
             operands,
-            anywhere=(2, 3) if step == 0 else (3,),
+            in_hbm=(2, 3) if step == 0 else (3,),
             name=f"step{step}",
         )
         send, grid, bad, own_u, own_v = got[:5]

time: 76.4 us -> 73.3 us (0.959)
  Pallas kernels: 13.3 us -> 10.2 us
    pallas_call x6, Pallas kernels: 13.3 us -> 10.2 us  [call(): pl.pallas_call(kernel, out_shape=[jax.ShapeDtypeStruct(shape, jnp.float32...]
where the time goes in v3:
time: 73.3 us; the launch traced here: 72.9 us
  blocking collectives  49.7 us (68%)
  Pallas kernels  10.2 us (14%)
  waiting for transfers between devices  5.93 us (8%)
  starting transfers between devices  3.01 us (4%)
  between operations  2.07 us (3%)
  local copies, waits for them, and re-layouts  1.83 us (2%)
    all_to_all x4, blocking collectives, exchange(): lax.all_to_all(value, ('gx', 'gy'), split_axis=0, concat_axis=0, tiled=True)  49.7 us
    pallas_call x6, Pallas kernels, call(): pl.pallas_call(kernel, out_shape=[jax.ShapeDtypeStruct(shape, jnp.float32...  10.2 us
    all_to_all x1, waiting for transfers between devices, exchange(): lax.all_to_all(value, ('gx', 'gy'), split_axis=0, concat_axis=0, tiled=True)  5.93 us
    all_to_all x1, starting transfers between devices, exchange(): lax.all_to_all(value, ('gx', 'gy'), split_axis=0, concat_axis=0, tiled=True)  3.01 us
  transfers between devices with their start and end apart: 1, of which 1 were waited for; matrix products, arithmetic and copies ran while one was open for 1% of the time, Pallas kernels for 0%

profile of v3, /device:TPU:0, one launch (start us, length us, event | category | flops | bytes accessed | tf_op | source)
XLA Modules:
  0.0 72.9 jit_solution(10168100178059835678)
XLA Ops:
  0.6 0.7 copy.157.heat
  2.0 1.1 %prepare.1 = (f32[32,1,1408]{2,1,0:T(1,128)S(1)}, f32[72,128]{1,0:T(8,128)S(1)}, f32[8,128]{1,0:T(8,128)S(1)}) custom-call(f32[3,2,3,2,128]{4,3,2,1,0:T(2,128)} %bitcast.398, f32[1,4,8]{2,1,0:T(4,128)S(1)} %copy.157.heat, s32[1,1,2,324]{3,2,1,0:T(2,128)} %pairs.1, s32[1,1]{1,0:T(1,128)S(6)} %copy.156.count), custom_call_target="tpu_custom_call" | custom-call | tf_op jit(solution)/shard_map/prepare/pallas_call | solution.py:973
  3.1 0.0 copy-start.1
  3.1 15.8 %all_to_all.102.refs_0_ = f32[32,1,1408]{2,1,0:T(1,128)S(1)} all-to-all(f32[32,1,1408]{2,1,0:T(1,128)S(1)} %get-tuple-element.989), channel_id=1, replica_groups=mesh['gx'=4,'gy'=8] {'gx','gy'}, dimensions={0} | all-to-all | bytes 360448 | tf_op jit(solution)/shard_map/all_to_all | solution.py:962
  18.9 2.1 %step0.1 = (f32[32,1,1280]{2,1,0:T(1,128)S(1)}, f32[32,128]{1,0:T(8,128)S(1)}, f32[8,128]{1,0:T(8,128)S(1)}, f32[72,128]{1,0:T(8,128)S(1)}, f32[72,128]{1,0:T(8,128)S(1)}, /*index=5*/f32[3480,128]{1,0:T(8,128)S(1)}) custom-call(f32[32,1,1408]{2,1,0:T(1,128)S(1)} %all_to_all.102.refs_0_, f32[72,128]{1,0:T(8,128)S(1)} %get-tuple-element.990.refs_1_, ...), custom_call_target="tpu_custom_call" | custom-call | tf_op jit(solution)/shard_map/step0/pallas_call | solution.py:973
  21.0 10.8 %all_to_all.103.refs_0_ = f32[32,1,1280]{2,1,0:T(1,128)S(1)} all-to-all(f32[32,1,1280]{2,1,0:T(1,128)S(1)} %get-tuple-element.992), channel_id=1, replica_groups=mesh['gx'=4,'gy'=8] {'gx','gy'}, dimensions={0} | all-to-all | bytes 327680 | tf_op jit(solution)/shard_map/all_to_all | solution.py:962
  31.8 1.5 %step1.1 = (f32[32,1,1792]{2,1,0:T(1,128)S(1)}, f32[32,128]{1,0:T(8,128)S(1)}, f32[8,128]{1,0:T(8,128)S(1)}, f32[72,128]{1,0:T(8,128)S(1)}, f32[72,128]{1,0:T(8,128)S(1)}) custom-call(f32[32,1,1280]{2,1,0:T(1,128)S(1)} %all_to_all.103.refs_0_, f32[72,128]{1,0:T(8,128)S(1)} %get-tuple-element.993.refs_1_, f32[72,128]{1,0:T(8,128)S(1)} %get-tuple-element.994.refs_2_, ...), custom_call_target="tpu_custom_call" | custom-call | tf_op jit(solution)/shard_map/step1/pallas_call | solution.py:973
  33.3 11.1 %all_to_all.104.refs_0_ = f32[32,1,1792]{2,1,0:T(1,128)S(1)} all-to-all(f32[32,1,1792]{2,1,0:T(1,128)S(1)} %get-tuple-element.998), channel_id=1, replica_groups=mesh['gx'=4,'gy'=8] {'gx','gy'}, dimensions={0} | all-to-all | bytes 458752 | tf_op jit(solution)/shard_map/all_to_all | solution.py:962
  44.5 0.0 copy-done.1
  44.5 2.4 %step2.1 = (f32[32,1,1792]{2,1,0:T(1,128)S(1)}, f32[32,128]{1,0:T(8,128)S(1)}, f32[8,128]{1,0:T(8,128)S(1)}, f32[72,128]{1,0:T(8,128)S(1)}, f32[72,128]{1,0:T(8,128)S(1)}) custom-call(f32[32,1,1792]{2,1,0:T(1,128)S(1)} %all_to_all.104.refs_0_, f32[72,128]{1,0:T(8,128)S(1)} %get-tuple-element.999.refs_1_, f32[72,128]{1,0:T(8,128)S(1)} %get-tuple-element.1000.refs_2_, ...), custom_call_target="tpu_custom_call" | custom-call | tf_op jit(solution)/shard_map/step2/pallas_call | solution.py:973
  46.8 0.0 copy-start.2
  46.9 0.0 copy-start.3
  46.9 0.0 copy-start.4
  46.9 12.0 %all_to_all.105.refs_0_ = f32[32,1,1792]{2,1,0:T(1,128)S(1)} all-to-all(f32[32,1,1792]{2,1,0:T(1,128)S(1)} %get-tuple-element.1003), channel_id=1, replica_groups=mesh['gx'=4,'gy'=8] {'gx','gy'}, dimensions={0} | all-to-all | bytes 458752 | tf_op jit(solution)/shard_map/all_to_all | solution.py:962
  58.8 2.9 %step3.1 = (f32[32,128]{1,0:T(8,128)}, f32[32,128]{1,0:T(8,128)S(1)}, f32[8,128]{1,0:T(8,128)S(1)}, f32[3,2,3,2,128]{4,3,2,1,0:T(2,128)S(1)}, f32[3,2,3,2,128]{4,3,2,1,0:T(2,128)S(1)}) custom-call(f32[32,1,1792]{2,1,0:T(1,128)S(1)} %all_to_all.105.refs_0_, f32[72,128]{1,0:T(8,128)S(1)} %get-tuple-element.1004.refs_1_, ...), custom_call_target="tpu_custom_call" | custom-call | tf_op jit(solution)/shard_map/step3/pallas_call | solution.py:973
  61.7 3.0 %all-to-all-start.6 = ((f32[32,1,128]{2,1,0:T(1,128)}), f32[32,1,128]{2,1,0:T(1,128)S(1)}, u32[]{:S(2)}, u32[]{:S(2)}) async-start(f32[32,1,128]{2,1,0:T(1,128)} %bitcast.39), calls=%async_computation.6 | async-start | bytes 32768 | tf_op jit(solution)/shard_map/all_to_all | solution.py:962
  64.8 0.5 slice.177
  65.9 5.9 %all-to-all-done.6 = f32[32,1,128]{2,1,0:T(1,128)S(1)} async-done(((f32[32,1,128]{2,1,0:T(1,128)}), f32[32,1,128]{2,1,0:T(1,128)S(1)}, u32[]{:S(2)}, u32[]{:S(2)}) %all-to-all-start.6) | async-done | bytes 16416 | tf_op jit(solution)/shard_map/all_to_all | solution.py:962
  71.9 0.2 finish.1
  72.1 0.0 copy-done.2
  72.1 0.0 copy-done.3
  72.1 0.0 copy-done.4
  72.1 0.2 conditional.1
  72.3 0.0 copy-start.5
  72.3 0.0 copy-start.6
  72.3 0.0 copy-start.7
  72.3 0.5 copy-done.5
  72.9 0.0 copy-done.6
  72.9 0.0 copy-done.7
Async XLA Ops:
  3.1 41.4 %copy-start.1 = (f32[4,3,2,2,3,128]{5,3,4,2,1,0:T(2,128)S(1)}, f32[4,3,2,2,3,128]{5,3,4,2,1,0:T(2,128)}, u32[]{:S(2)}) copy-start(f32[4,3,2,2,3,128]{5,3,4,2,1,0:T(2,128)} %param.18) | copy-start | bytes 221188
  46.8 25.2 %copy-start.2 = (s32[1,1,2,324]{3,2,1,0:T(2,128)S(1)}, s32[1,1,2,324]{3,2,1,0:T(2,128)}, u32[]{:S(2)}) copy-start(s32[1,1,2,324]{3,2,1,0:T(2,128)} %pairs.1) | copy-start | bytes 7780
  46.9 25.2 %copy-start.3 = (f32[3,2,2,3,128]{4,2,3,1,0:T(2,128)S(1)}, f32[3,2,2,3,128]{4,2,3,1,0:T(2,128)}, u32[]{:S(2)}) copy-start(f32[3,2,2,3,128]{4,2,3,1,0:T(2,128)} %param.17) | copy-start | bytes 55300
  46.9 25.2 %copy-start.4 = (f32[3,2,2,3,128]{4,2,3,1,0:T(2,128)S(1)}, f32[3,2,2,3,128]{4,2,3,1,0:T(2,128)}, u32[]{:S(2)}) copy-start(f32[3,2,2,3,128]{4,2,3,1,0:T(2,128)} %param.16) | copy-start | bytes 55300
  61.7 10.1 %all-to-all-start.6 = ((f32[32,1,128]{2,1,0:T(1,128)}), f32[32,1,128]{2,1,0:T(1,128)S(1)}, u32[]{:S(2)}, u32[]{:S(2)}) async-start(f32[32,1,128]{2,1,0:T(1,128)} %bitcast.39), calls=%async_computation.6 | async-start | bytes 32768 | tf_op jit(solution)/shard_map/all_to_all | solution.py:962
  72.3 0.6 copy-start.5
  72.3 0.6 copy-start.6
  72.3 0.6 copy-start.7

commit v4 on v3

--- a/solution.py
+++ b/solution.py
@@ -308,6 +308,14 @@
                     piece = turn(rows[cx], 32 + 32 * iy - 32 * cx)
                     value = piece if value is None else jnp.where(lane >= 32 * cx, piece, value)
                 out[c, ix, :, iy, :] = value
+
+
+def each(count, body):
+    if count <= 32:
+        for index in range(count):
+            body(index, 0)
+    else:
+        lax.fori_loop(0, count, body, 0, unroll=8)
 
 
 def stage_halo(own, stage, chunk, tail_row, extras):
@@ -363,17 +371,25 @@
     at = kinds[("x", 1)]
     rows = {where: stage[at + where : at + where + 1, :] for where in tails}
 
-    def fill(index, carry):
-        for where in tails:
-            send_ref[index, :, 128 * where : 128 * where + 128] = rows[where]
-        return carry
-
-    lax.fori_loop(0, owners, fill, 0, unroll=8)
     for (sx, sy), ident in ids.items():
         if (sx, sy) == (0, 0):
             continue
         at = kinds[("y", sy)] if sy else kinds[("x", sx)]
         for k in range(chunk.rows):
+            if k not in tails:
+                send_ref[ident, :, 128 * k : 128 * k + 128] = stage[at + k : at + k + 1, :]
+
+    def fill(index, carry):
+        for where in tails:
+            send_ref[index, :, 128 * where : 128 * where + 128] = rows[where]
+        return carry
+
+    each(owners, fill)
+    for (sx, sy), ident in ids.items():
+        if (sx, sy) == (0, 0):
+            continue
+        at = kinds[("y", sy)] if sy else kinds[("x", sx)]
+        for k in tails:
             send_ref[ident, :, 128 * k : 128 * k + 128] = stage[at + k : at + k + 1, :]
 
 
@@ -394,7 +410,7 @@
             tails_at[pl.ds(n * owners + index, 1), :] = recv_ref[index, :, 128 * where : 128 * where + 128]
         return carry
 
-    lax.fori_loop(0, owners, take, 0, unroll=8)
+    each(owners, take)
     return homes
 
 
@@ -489,7 +505,7 @@
     parity = half_layer % 2
     slots = {key: n for n, (key, _) in enumerate(groups)}
     for c in range(count):
-        for dz in sorted({key[1] for key in slots}, key=abs):
+        for dz in sorted({key[1] for key in slots}, key=lambda z: (z % 2, abs(z))):
             dys = sorted(key[0] for key in slots if key[1] == dz)
             carried = (half_layer + dz >= 8) | (half_layer + dz < 0)
             ref = mixed if dz % 2 and mixed is not None else source
@@ -658,7 +674,7 @@
     return {(sx, sy): at_x[sx] * ny + at_y[sy] for sx in (-1, 0, 1) for sy in (-1, 0, 1)}
 
 
-def prepare(across, chunk, disp, heat, pairs, count, send, own_u, live, lists, disp_in, heat_in, pairs_in, count_in, stage, sems):
+def prepare(across, chunk, disp, heat, pairs, count, vel, noise, send, own_u, live, kept_heat, kept_count, near_vel, near_noise, lists, disp_in, heat_in, pairs_in, count_in, stage, sems):
     nx, ny = across
     owners = nx * ny
     copies = [
@@ -667,13 +683,19 @@
             ((disp, disp_in), (heat, heat_in), (pairs, pairs_in), (count, count_in))
         )
     ]
-    for copy in copies:
+    later = [
+        pltpu.make_async_copy(vel, near_vel, sems.at[4]),
+        pltpu.make_async_copy(noise, near_noise, sems.at[5]),
+    ]
+    for copy in copies + later:
         copy.start()
     lists[...] = jnp.full(lists.shape, -1, jnp.int32)
     for copy in copies:
         copy.wait()
 
     from_tiles(lambda c, ix, iy: disp_in[c, ix, :, iy, :], own_u)
+    kept_heat[...] = heat_in[...]
+    kept_count[...] = jnp.full((8, 128), count_in[0, 0], jnp.int32)
 
     slots = pairs_in.shape[3]
     width = lists.shape[1]
@@ -720,6 +742,8 @@
         extras,
     )
     send_chunks(stage, kinds, send, chunk, neighbour_ids(across), owners)
+    for copy in later:
+        copy.wait()
 
 
 def make_masks(chunk, homes, landed, live, masks_ref, table, spread_ref, cases):
@@ -830,17 +854,16 @@
     send, out_grid, out_bad, out_u, out_v = take(5)
     if step == 0:
         (masks_ref,) = take(1)
-    window, moved, slope, slope_moved, gaps, inverses, landed, tails_at, noise_in, noise_own = take(10)
-    sems, u_own, v_own, stage, mixed = take(5)
+    window, moved, slope, slope_moved, gaps, inverses, landed, tails_at, noise_own = take(9)
+    v_own, stage, mixed = take(3)
     extra = refs
-    if not last:
-        u_own, v_own = out_u, out_v
-    noise_copy = pltpu.make_async_copy(noise.at[step], noise_in, sems.at[0])
-    noise_copy.start()
+    u_own = out_u
+    if step:
+        v_own = out_v
+    else:
+        v_own, v_start = out_v, v_own
     if step == 0:
-        v_in, table, spread_ref, cases = extra
-        v_copy = pltpu.make_async_copy(in_v, v_in, sems.at[1])
-        v_copy.start()
+        table, spread_ref, cases = extra
     ids = neighbour_ids(across)
     lane = lanes_of()
 
@@ -897,13 +920,11 @@
         )
     shift_planes(1, slope, None, slope_moved, groups, no_shift, origin)
 
-    noise_copy.wait()
-    from_tiles(lambda c, ix, iy: noise_in[c, ix, :, iy, :], noise_own)
+    from_tiles(lambda c, ix, iy: noise[step, c, ix, :, iy, :], noise_own)
     speeds_in = in_v
     if step == 0:
-        v_copy.wait()
-        from_tiles(lambda c, ix, iy: v_in[c, ix, :, iy, :], v_own)
-        speeds_in = v_own
+        from_tiles(lambda c, ix, iy: in_v[c, ix, :, iy, :], v_start)
+        speeds_in = v_start
 
     active = (lane >= 32) & (lane < 96)
     power = []
@@ -926,8 +947,6 @@
     energy = energies_by_plane(power, owners) * (friction * atom_mass * time_step)
     if last:
         send[...] = jnp.broadcast_to(energy, (owners, 128))
-        to_tiles(u_own, out_u)
-        to_tiles(v_own, out_v)
         return
     furthest = jnp.max(furthest, axis=0, keepdims=True)
     furthest = jnp.broadcast_to(jnp.max(furthest, axis=1, keepdims=True), (1, 128))
@@ -958,6 +977,11 @@
         heat[0, x : x + 1, :] = row[:, :ny]
 
 
+def leave(in_u, in_v, new_u, new_v):
+    to_tiles(in_u, new_u)
+    to_tiles(in_v, new_v)
+
+
 def exchange(value):
     return lax.all_to_all(value, ("gx", "gy"), split_axis=0, concat_axis=0, tiled=True)
 
@@ -972,7 +996,10 @@
     ]
     return pl.pallas_call(
         kernel,
-        out_shape=[jax.ShapeDtypeStruct(shape, jnp.float32) for shape in outs],
+        out_shape=[
+            jax.ShapeDtypeStruct(*(out if isinstance(out[1], type) else (out, jnp.float32)))
+            for out in outs
+        ],
         in_specs=specs,
         out_specs=[pl.BlockSpec(memory_space=pltpu.VMEM)] * len(outs),
         scratch_shapes=scratch,
@@ -994,9 +1021,17 @@
     placed_noise = jnp.swapaxes(noise, 3, 4)
     slots = pair_list.shape[-1]
     first, two, three = Chunk(owners, 2, True), Chunk(owners, 2), Chunk(owners, 3)
-    send, own_u, live = call(
+    send, own_u, live, kept_heat, kept_count, own_v, near_noise = call(
         partial(prepare, across, first),
-        [(owners, 1, 128 * first.rows), (72, 128), (8, 128)],
+        [
+            (owners, 1, 128 * first.rows),
+            (72, 128),
+            (8, 128),
+            electron_temp.shape,
+            ((8, 128), jnp.int32),
+            placed_v.shape,
+            placed_noise.shape,
+        ],
         [
             pltpu.VMEM((8, (slots + 127) // 128 * 128), jnp.int32),
             vmem(*tiles),
@@ -1004,10 +1039,17 @@
             pltpu.VMEM(pair_list.shape, jnp.int32),
             pltpu.SMEM(pair_count.shape, jnp.int32),
             vmem(4 * 16, 128),
-            pltpu.SemaphoreType.DMA((4,)),
+            pltpu.SemaphoreType.DMA((6,)),
         ],
-        (placed_u, electron_temp, pair_list, pair_count),
-        in_hbm=(0, 1, 2, 3),
+        (
+            placed_u,
+            pltpu.with_memory_space_constraint(electron_temp, pltpu.HBM),
+            pair_list,
+            pair_count,
+            placed_v,
+            placed_noise,
+        ),
+        in_hbm=(0, 1, 2, 3, 4, 5),
         name="prepare",
     )
     near, far = grouped(NEAR), grouped(NEAR + FAR)
@@ -1017,7 +1059,6 @@
         (three, three, far, FAR_LIMIT),
         (three, None, far, FAR_LIMIT),
     ]
-    own_v = placed_v
     masks = grid = bad = None
     for step, (arriving, leaving, groups, limit) in enumerate(plan):
         recv = exchange(send)
@@ -1027,8 +1068,8 @@
             (owners, 128) if last else (owners, 1, 128 * leaving.rows),
             (owners, 128),
             (8, 128),
-            tiles if last else (72, 128),
-            tiles if last else (72, 128),
+            (72, 128),
+            (72, 128),
         ]
         scratch = [
             vmem(3 * SIZE + PAD, 128),
@@ -1039,9 +1080,6 @@
             vmem(24 * pairs, 128),
             vmem(9 * 16 + 2 * PAD, 128),
             vmem(2 * owners, 128),
-            vmem(*tiles),
-            vmem(72, 128),
-            pltpu.SemaphoreType.DMA((2,)),
             vmem(72, 128),
             vmem(72, 128),
             vmem(4 * 16, 128),
@@ -1049,29 +1087,31 @@
         ]
         if step == 0:
             outs.append((MASKS * SIZE, 128))
-            scratch += [vmem(*tiles), vmem(128, 128), vmem(512, 128), vmem(27 * 16, 128)]
-            operands = (recv, own_u, own_v, placed_noise, live)
+            scratch += [vmem(128, 128), vmem(512, 128), vmem(27 * 16, 128)]
+            operands = (recv, own_u, own_v, near_noise, live)
         else:
-            operands = (recv, own_u, own_v, placed_noise, masks, grid, bad)
+            operands = (recv, own_u, own_v, near_noise, masks, grid, bad)
         got = call(
             partial(step_kernel, step, across, arriving, leaving, groups, limit),
             outs,
             scratch,
             operands,
-            in_hbm=(2, 3) if step == 0 else (3,),
             name=f"step{step}",
         )
         send, grid, bad, own_u, own_v = got[:5]
         if step == 0:
             masks = got[5]
     recv = exchange(send)
+    new_u, new_v = call(leave, [tiles, tiles], [], (own_u, own_v), name="leave")
     (heat,) = call(partial(finish, across), [electron_temp.shape], [], (recv, grid), name="finish")
-    return bad[0, 0], jnp.swapaxes(own_u, 2, 3), jnp.swapaxes(own_v, 2, 3), heat
+    kept = (kept_heat, kept_count[:1, :1])
+    return bad[0, 0], kept, jnp.swapaxes(new_u, 2, 3), jnp.swapaxes(new_v, 2, 3), heat
 
 
 def per_device(displacement, velocity, noise, electron_temp, pair_list, pair_count):
     given = (displacement, velocity, noise, electron_temp, pair_list, pair_count)
-    bad, new_u, new_v, heat = stencil_steps(*given)
+    bad, (kept_heat, kept_count), new_u, new_v, heat = stencil_steps(*given)
+    given = (displacement, velocity, noise, kept_heat, pair_list, kept_count)
     return lax.cond(bad > 0.5, lambda: whole_sweep(*given), lambda: (new_u, new_v, heat))
 
 

time: 73.3 us -> 71.7 us (0.978)
    pallas_call x6 -> x7, Pallas kernels: 10.2 us -> 9.54 us  [call(): pl.pallas_call(kernel, out_shape=[jax.ShapeDtypeStruct(*(out if isinstanc...]
where the time goes in v4:
time: 71.7 us; the launch traced here: 71.4 us
  blocking collectives  49.7 us (69%)
  Pallas kernels  9.54 us (13%)
  waiting for transfers between devices  5.78 us (8%)
  starting transfers between devices  3.01 us (4%)
  between operations  2.06 us (3%)
  local copies, waits for them, and re-layouts  1.14 us (2%)
    all_to_all x4, blocking collectives, exchange(): lax.all_to_all(value, ('gx', 'gy'), split_axis=0, concat_axis=0, tiled=True)  49.7 us
    pallas_call x7, Pallas kernels, call(): pl.pallas_call(kernel, out_shape=[jax.ShapeDtypeStruct(*(out if isinstanc...  9.54 us
    all_to_all x1, waiting for transfers between devices, exchange(): lax.all_to_all(value, ('gx', 'gy'), split_axis=0, concat_axis=0, tiled=True)  5.78 us
    all_to_all x1, starting transfers between devices, exchange(): lax.all_to_all(value, ('gx', 'gy'), split_axis=0, concat_axis=0, tiled=True)  3.01 us
  transfers between devices with their start and end apart: 1, of which 1 were waited for; matrix products, arithmetic and copies ran while one was open for 1% of the time, Pallas kernels for 0%

profile of v4, /device:TPU:0, one launch (start us, length us, event | category | flops | bytes accessed | tf_op | source)
XLA Modules:
  0.0 71.4 jit_solution(15743628458998602227)
XLA Ops:
  1.3 1.1 %prepare.1 = (f32[32,1,1408]{2,1,0:T(1,128)S(1)}, f32[72,128]{1,0:T(8,128)S(1)}, f32[8,128]{1,0:T(8,128)S(1)}, f32[1,4,8]{2,1,0:T(4,128)S(1)}, s32[8,128]{1,0:T(...) custom-call(f32[3,2,3,2,128]{4,3,2,1,0:T(2,128)} %bitcast.394, f32[1,4,8]{2,1,0:T(4,128)} %heat.1, ...), custom_call_target="tpu_custom_call" | custom-call | tf_op jit(solution)/shard_map/prepare/pallas_call | solution.py:997
  2.4 15.8 %all_to_all.102.refs_0_ = f32[32,1,1408]{2,1,0:T(1,128)S(1)} all-to-all(f32[32,1,1408]{2,1,0:T(1,128)S(1)} %get-tuple-element.995), channel_id=1, replica_groups=mesh['gx'=4,'gy'=8] {'gx','gy'}, dimensions={0} | all-to-all | bytes 360448 | tf_op jit(solution)/shard_map/all_to_all | solution.py:986
  18.2 1.9 %step0.1 = (f32[32,1,1280]{2,1,0:T(1,128)S(1)}, f32[32,128]{1,0:T(8,128)S(1)}, f32[8,128]{1,0:T(8,128)S(1)}, f32[72,128]{1,0:T(8,128)S(1)}, f32[72,128]{1,0:T(8,128)S(1)}, /*index=5*/f32[3480,128]{1,0:T(8,128)S(1)}) custom-call(f32[32,1,1408]{2,1,0:T(1,128)S(1)} %all_to_all.102.refs_0_, f32[72,128]{1,0:T(8,128)S(1)} %get-tuple-element.996.refs_1_, ...), custom_call_target="tpu_custom_call" | custom-call | tf_op jit(solution)/shard_map/step0/pallas_call | solution.py:997
  20.1 10.8 %all_to_all.103.refs_0_ = f32[32,1,1280]{2,1,0:T(1,128)S(1)} all-to-all(f32[32,1,1280]{2,1,0:T(1,128)S(1)} %get-tuple-element.1000), channel_id=1, replica_groups=mesh['gx'=4,'gy'=8] {'gx','gy'}, dimensions={0} | all-to-all | bytes 327680 | tf_op jit(solution)/shard_map/all_to_all | solution.py:986
  30.9 1.4 %step1.1 = (f32[32,1,1792]{2,1,0:T(1,128)S(1)}, f32[32,128]{1,0:T(8,128)S(1)}, f32[8,128]{1,0:T(8,128)S(1)}, f32[72,128]{1,0:T(8,128)S(1)}, f32[72,128]{1,0:T(8,128)S(1)}) custom-call(f32[32,1,1280]{2,1,0:T(1,128)S(1)} %all_to_all.103.refs_0_, f32[72,128]{1,0:T(8,128)S(1)} %get-tuple-element.1001.refs_1_, f32[72,128]{1,0:T(8,128)S(1)} %get-tuple-element.1002.refs_2_, ...), custom_call_target="tpu_custom_call" | custom-call | tf_op jit(solution)/shard_map/step1/pallas_call | solution.py:997
  32.3 11.1 %all_to_all.104.refs_0_ = f32[32,1,1792]{2,1,0:T(1,128)S(1)} all-to-all(f32[32,1,1792]{2,1,0:T(1,128)S(1)} %get-tuple-element.1006), channel_id=1, replica_groups=mesh['gx'=4,'gy'=8] {'gx','gy'}, dimensions={0} | all-to-all | bytes 458752 | tf_op jit(solution)/shard_map/all_to_all | solution.py:986
  43.4 2.2 %step2.1 = (f32[32,1,1792]{2,1,0:T(1,128)S(1)}, f32[32,128]{1,0:T(8,128)S(1)}, f32[8,128]{1,0:T(8,128)S(1)}, f32[72,128]{1,0:T(8,128)S(1)}, f32[72,128]{1,0:T(8,128)S(1)}) custom-call(f32[32,1,1792]{2,1,0:T(1,128)S(1)} %all_to_all.104.refs_0_, f32[72,128]{1,0:T(8,128)S(1)} %get-tuple-element.1007.refs_1_, f32[72,128]{1,0:T(8,128)S(1)} %get-tuple-element.1008.refs_2_, ...), custom_call_target="tpu_custom_call" | custom-call | tf_op jit(solution)/shard_map/step2/pallas_call | solution.py:997
  45.6 0.0 copy-start.1
  45.6 0.0 copy-start.2
  45.6 0.0 copy-start.3
  45.6 12.0 %all_to_all.105.refs_0_ = f32[32,1,1792]{2,1,0:T(1,128)S(1)} all-to-all(f32[32,1,1792]{2,1,0:T(1,128)S(1)} %get-tuple-element.1011), channel_id=1, replica_groups=mesh['gx'=4,'gy'=8] {'gx','gy'}, dimensions={0} | all-to-all | bytes 458752 | tf_op jit(solution)/shard_map/all_to_all | solution.py:986
  57.6 2.6 %step3.1 = (f32[32,128]{1,0:T(8,128)}, f32[32,128]{1,0:T(8,128)S(1)}, f32[8,128]{1,0:T(8,128)S(1)}, f32[72,128]{1,0:T(8,128)S(1)}, f32[72,128]{1,0:T(8,128)S(1)}) custom-call(f32[32,1,1792]{2,1,0:T(1,128)S(1)} %all_to_all.105.refs_0_, f32[72,128]{1,0:T(8,128)S(1)} %get-tuple-element.1012.refs_1_, f32[72,128]{1,0:T(8,128)S(1)} %get-tuple-element.1013.refs_2_, ...), custom_call_target="tpu_custom_call" | custom-call | tf_op jit(solution)/shard_map/step3/pallas_call | solution.py:997
  60.2 3.0 %all-to-all-start.6 = ((f32[32,1,128]{2,1,0:T(1,128)}), f32[32,1,128]{2,1,0:T(1,128)S(1)}, u32[]{:S(2)}, u32[]{:S(2)}) async-start(f32[32,1,128]{2,1,0:T(1,128)} %bitcast.39), calls=%async_computation.6 | async-start | bytes 32768 | tf_op jit(solution)/shard_map/all_to_all | solution.py:986
  63.2 0.5 slice.180
  64.4 0.1 leave.1
  64.5 5.8 %all-to-all-done.6 = f32[32,1,128]{2,1,0:T(1,128)S(1)} async-done(((f32[32,1,128]{2,1,0:T(1,128)}), f32[32,1,128]{2,1,0:T(1,128)S(1)}, u32[]{:S(2)}, u32[]{:S(2)}) %all-to-all-start.6) | async-done | bytes 16416 | tf_op jit(solution)/shard_map/all_to_all | solution.py:986
  70.3 0.2 finish.1
  70.5 0.0 copy-done.1
  70.5 0.0 copy-done.2
  70.5 0.0 copy-done.3
  70.6 0.2 conditional.1
  70.8 0.0 copy-start.4
  70.8 0.0 copy-start.5
  70.8 0.0 copy-start.6
  70.8 0.5 copy-done.4
  71.3 0.0 copy-done.5
  71.4 0.0 copy-done.6
Async XLA Ops:
  45.6 25.0 %copy-start.1 = (s32[1,1,2,324]{3,2,1,0:T(2,128)S(1)}, s32[1,1,2,324]{3,2,1,0:T(2,128)}, u32[]{:S(2)}) copy-start(s32[1,1,2,324]{3,2,1,0:T(2,128)} %pairs.1) | copy-start | bytes 7780
  45.6 25.0 %copy-start.2 = (f32[3,2,2,3,128]{4,2,3,1,0:T(2,128)S(1)}, f32[3,2,2,3,128]{4,2,3,1,0:T(2,128)}, u32[]{:S(2)}) copy-start(f32[3,2,2,3,128]{4,2,3,1,0:T(2,128)} %param.16) | copy-start | bytes 55300
  45.6 25.0 %copy-start.3 = (f32[3,2,2,3,128]{4,2,3,1,0:T(2,128)S(1)}, f32[3,2,2,3,128]{4,2,3,1,0:T(2,128)}, u32[]{:S(2)}) copy-start(f32[3,2,2,3,128]{4,2,3,1,0:T(2,128)} %param.17) | copy-start | bytes 55300
  60.2 10.1 %all-to-all-start.6 = ((f32[32,1,128]{2,1,0:T(1,128)}), f32[32,1,128]{2,1,0:T(1,128)S(1)}, u32[]{:S(2)}, u32[]{:S(2)}) async-start(f32[32,1,128]{2,1,0:T(1,128)} %bitcast.39), calls=%async_computation.6 | async-start | bytes 32768 | tf_op jit(solution)/shard_map/all_to_all | solution.py:986
  70.8 0.6 copy-start.4
  70.8 0.6 copy-start.5
  70.8 0.6 copy-start.6
